TPU v7x, 32 devices: a whole 2x2x4 slice. The times are simulated.
32 devices in a mesh: mode: 16 (over z, x, core), node: 2 (over y).
Axes of the slice: x: 2, y: 2, z: 4, core: 2. Of those that a mesh axis runs over, the one named last changes fastest.
Arguments:
- panels: bfloat16 [2, 2048, 4096], P(None, 'node', 'mode'), may hold values from -60 to 60, as said below
- shapes: bfloat16 [8192, 4096], P('mode'), may hold values from -0.09375 to 0.09375
- harmonic: int32 [2048], P('node'), may hold values from 1 to 4095, as said below
- connect: int32 [4096, 8], P(('mode', 'node')), may hold values from 0 to 8191, as said below
- recovery: float32 [4096, 8], P(('mode', 'node')), may hold values from -3 to 3
Outputs:
- stress: float32 [4096, 512], P(('mode', 'node'))
- moments: float32 [4, 8192], P(None, ('mode', 'node'))
Inputs may be any that keep to these rules, and one draw needn't show every extreme that they name: `harmonic`: harmonic numbers are distinct and increasing. `connect`: the 128 elements of block b refer only to rows of group b // 2, that is rows (b // 2) * 512 to (b // 2 + 1) * 512 - 1. Split a group's rows into 2 blocks of 256 rows: one element block refers to at most 64 distinct rows of any one such block, and in every group one element block refers to exactly 64 rows of each of them. `panels`: modal coordinates stay in the range.
All inputs are finite; a program needn't handle non-finite values.
Results may differ from a plain program's by a relative error of at most 0.0029.
Values may be sent and summed in bfloat16 or wider, within the bound.
No kernel may reach another device: no remote copies, remote signals or barrier semaphores. Data moves between devices by JAX's collectives and lax.ppermute only.
A program may use at most 64 MiB of HBM per device.

v0:
```python
import math

import jax
import jax.numpy as jnp
from jax import lax
from jax.sharding import PartitionSpec as P

F = 2048
STEPS = 512
HARM = 4096


def spectral_tables(harmonic):
    step_ids = jnp.arange(STEPS, dtype=jnp.int32)
    phases = harmonic[:, None] * step_ids[None, :] % HARM
    angles = phases.astype(jnp.float32) * (2.0 * math.pi / HARM)
    ratios = harmonic.astype(jnp.float32) / HARM
    squared = ratios * ratios
    weights = jnp.stack([jnp.ones_like(ratios), ratios, squared, squared * squared]) / F
    return (jnp.cos(angles), jnp.sin(angles), weights)


def time_rows(spectra, cos_table, sin_table, weights):
    highest = lax.Precision.HIGHEST
    history = jnp.einsum("fr,ft->rt", spectra[0], cos_table, precision=highest)
    history = history - jnp.einsum("fr,ft->rt", spectra[1], sin_table, precision=highest)
    power_rows = spectra[0] * spectra[0] + spectra[1] * spectra[1]
    return (math.sqrt(2.0 / F) * history, jnp.dot(weights, power_rows, precision=highest))


def corner_weights(local_rows, recovery, slot_ids):
    matches = local_rows[:, :, None] == slot_ids[None, None, :]
    return jnp.sum(jnp.where(matches, recovery[:, :, None], 0.0), axis=1)


def shards(panels, shapes, harmonic, connect, recovery):
    highest = lax.Precision.HIGHEST
    rows_mode = shapes.shape[0]
    spectra = jnp.einsum(
        "cfm,rm->cfr",
        lax.all_gather(panels, "mode", axis=2, tiled=True),
        shapes,
        preferred_element_type=jnp.float32,
    )
    cos_table, sin_table, weights = spectral_tables(harmonic)
    history_part, moment_part = time_rows(spectra, cos_table, sin_table, weights)
    history, moments = (
        lax.psum_scatter(history_part, "node", scatter_dimension=0, tiled=True),
        lax.psum_scatter(moment_part, "node", scatter_dimension=1, tiled=True),
    )
    histories = history.astype(jnp.bfloat16)
    local_rows = connect - lax.axis_index("mode") * rows_mode
    rows_in = lax.all_gather(histories, "node", axis=0, tiled=True)
    slot_ids = jnp.arange(rows_mode, dtype=jnp.int32)
    weight = corner_weights(local_rows, recovery, slot_ids)
    stress = jnp.dot(weight, rows_in, preferred_element_type=jnp.float32, precision=highest)
    return (stress, moments)


def solution(mesh):
    return jax.shard_map(
        shards,
        mesh=mesh,
        in_specs=(
            P(None, "node", "mode"),
            P("mode", None),
            P("node"),
            P(("mode", "node"), None),
            P(("mode", "node"), None),
        ),
        out_specs=(P(("mode", "node"), None), P(None, ("mode", "node"))),
        check_vma=False,
    )
```

profile of v0, /device:TPU:0, one launch (start us, length us, event | category | flops | bytes accessed | tf_op | source)
XLA Modules:
  0.0 222.8 jit_solution(14302567841582052245)
XLA Ops:
  7.2 0.0 all-gather.2.cloned.1.call-start
  7.2 0.7 all-gather.2.cloned.1.call-update
  7.9 0.0 reduce-scatter.7.cloned.1.call-start
  8.0 0.7 convert_multiply_fusion
  8.7 0.0 copy-start.2
  8.7 134.6 %all-gather.2.cloned.1.call-done = bf16[2,1024,4096]{2,1,0:T(8,128)(2,1)} async-done(((bf16[2,1024,256]{2,1,0:T(8,128)(2,1)}), bf16[2,1024,4096]{2,1,0:T(8,128)(2,1)}) %all-gather.2.cloned.1.call-update) | async-done | bytes 16777232 | tf_op jit(solution)/shard_map/all_gather | solution.py:41
  143.2 13.4 %fusion = f32[2,1024,512]{2,1,0:T(8,128)S(1)} fusion(bf16[2,1024,4096]{2,1,0:T(8,128)(2,1)} %all-gather.2.cloned.1.call-done, bf16[512,4096]{1,0:T(8,128)(2,1)} %param.6), kind=kOutput, calls=%fused_computation | convolution fusion | flops 8589934592 | bytes 25165824 | tf_op jit(solution)/shard_map/cfm,rm->cfr/dot_general | solution.py:39
  156.7 0.0 copy-done.2
  156.7 0.0 copy-start.3
  156.7 11.5 %fusion.9 = f32[512,512]{1,0:T(8,128)S(1)} fusion(f32[2,1024,512]{2,1,0:T(8,128)S(1)} %fusion, s32[1024]{0:T(1024)S(1)} %copy-done.2), kind=kOutput, calls=%fused_computation.14 | convolution fusion | flops 3228565504 | bytes 3149824 | tf_op jit(solution)/shard_map/fr,ft->rt/dot_general | solution.py:26
  168.2 0.0 copy-done.3
  168.2 4.4 %fusion.22 = f32[512,4]{1,0:T(8,128)} fusion(f32[2,1024,512]{2,1,0:T(8,128)S(1)} %fusion, f32[1,1024]{1,0:T(1,128)S(1)} %bitcast.35, f32[1,1024]{1,0:T(1,128)S(1)} %bitcast.36, f32[1,1024]{1,0:T(1,128)S(1)} %bitcast.34, f32[4]{0:T(128)S(1)} %pad.clone), kind=kOutput, calls=%fused_computation.25 | convolution fusion | flops 26755072 | bytes 4214800
  172.6 0.0 reduce-scatter.7.cloned.1.call-update
  172.6 0.0 copy-start.1
  172.6 0.0 copy-start
  172.7 0.0 reduce-scatter.5.cloned.1.call-start
  172.7 14.0 %fusion.19 = f32[512,512]{1,0:T(8,128)} fusion(f32[512,512]{1,0:T(8,128)S(1)} %fusion.9, f32[2,1024,512]{2,1,0:T(8,128)} %copy-done.3, s32[1024]{0:T(1024)S(1)} %copy-done.2), kind=kOutput, calls=%fused_computation.24 | convolution fusion | flops 3229089792 | bytes 4198400 | tf_op jit(solution)/shard_map/fr,ft->rt/dot_general | solution.py:25
  186.7 0.0 reduce-scatter.5.cloned.1.call-update
  186.7 0.0 copy-done.1
  186.7 0.1 copy.11
  186.8 0.0 copy-done
  186.8 0.1 copy.12
  186.9 0.7 select_reduce_fusion
  187.6 0.0 reduce-scatter.7.cloned.1.call-done
  187.6 1.6 copy.14
  189.2 16.1 %reduce-scatter.5.cloned.1.call-done = f32[256,512]{1,0:T(8,128)} async-done(((f32[512,512]{1,0:T(8,128)}), f32[256,512]{1,0:T(8,128)}) %reduce-scatter.5.cloned.1.call-update) | async-done | bytes 524304 | tf_op jit(solution)/shard_map/reduce_scatter | solution.py:48
  205.3 1.1 convert_element_type.10
  206.4 8.7 %all_gather.7 = bf16[512,512]{1,0:T(8,128)(2,1)S(1)} all-gather(bf16[256,512]{1,0:T(8,128)(2,1)S(1)} %convert_element_type.10), channel_id=1, replica_groups=mesh['mode'=16,'node'=2] {'node'}, dimensions={0}, use_global_device_ids=true | all-gather | bytes 786432 | tf_op jit(solution)/shard_map/all_gather | solution.py:53
  215.1 1.1 fusion.46
  (2 shorter events, 0.0 us)
Async XLA Ops:
  7.2 136.1 %all-gather.2.cloned.1.call-start = ((), (), s32[]{:S(2)}) async-start(), calls=%async_computation.2 | async-start | bytes 17825792 | tf_op jit(solution)/shard_map/all_gather | solution.py:41
  7.9 179.7 %reduce-scatter.7.cloned.1.call-start = ((), (), s32[]{:S(2)}) async-start(), calls=%async_computation.4 | async-start | bytes 393216
  8.7 148.0 %copy-start.2 = (s32[1024]{0:T(1024)S(1)}, s32[1024]{0:T(1024)}, u32[]{:S(2)}) copy-start(s32[1024]{0:T(1024)} %param.7) | copy-start | bytes 12292
  156.7 11.5 %copy-start.3 = (f32[2,1024,512]{2,1,0:T(8,128)}, f32[2,1024,512]{2,1,0:T(8,128)S(1)}, u32[]{:S(2)}) copy-start(f32[2,1024,512]{2,1,0:T(8,128)S(1)} %fusion) | copy-start | bytes 12582916
  172.6 14.1 %copy-start.1 = (s32[128,8]{0,1:T(8,128)S(1)}, s32[128,8]{0,1:T(8,128)}, u32[]{:S(2)}) copy-start(s32[128,8]{0,1:T(8,128)} %param.8) | copy-start | bytes 12292
  172.6 14.2 %copy-start = (f32[128,8]{0,1:T(8,128)S(1)}, f32[128,8]{0,1:T(8,128)}, u32[]{:S(2)}) copy-start(f32[128,8]{0,1:T(8,128)} %param.9) | copy-start | bytes 12292
  172.7 32.7 %reduce-scatter.5.cloned.1.call-start = ((), (), s32[]{:S(2)}) async-start(), calls=%async_computation.3 | async-start | bytes 1572864 | tf_op jit(solution)/shard_map/reduce_scatter | solution.py:48
Sparse Core Ops, SparseCore 0:
  10.2 133.0 all-gather.1
  172.8 9.8 reduce-scatter.6
  186.8 18.4 reduce-scatter.4
where the time goes:
time: 223 us
  waiting for transfers between devices  151 us (68%)
  matrix products  44.4 us (20%)
  between operations  13.8 us (6%)
  blocking collectives  8.73 us (4%)
  other arithmetic  2.46 us (1%)
    all_gather x1, waiting for transfers between devices, shards(): lax.all_gather(panels, 'mode', axis=2, tiled=True)  135 us
    reduce_scatter x1, waiting for transfers between devices, shards(): lax.psum_scatter(history_part, 'node', scatter_dimension=0, tiled=True)  16.1 us
    dot_general x1, matrix products, time_rows(): history = jnp.einsum('fr,ft->rt', spectra[0], cos_table, precision=highest)  14 us
    dot_general x1, matrix products, shards(): jnp.einsum('cfm,rm->cfr', lax.all_gather(panels, 'mode', axis=2, tiled=Tr...  13.4 us
    dot_general x1, matrix products, time_rows(): jnp.einsum('fr,ft->rt', spectra[1], sin_table, precision=highest)  11.5 us
    all_gather x1, blocking collectives, shards(): rows_in = lax.all_gather(histories, 'node', axis=0, tiled=True)  8.73 us
  transfers between devices with their start and end apart: 3, of which 2 were waited for; matrix products, arithmetic and copies ran while one was open for 8% of the time, Pallas kernels for 0%

commit v1 on v0

v1 whole, which is shorter than its diff:
```python
import functools
import math

import jax
import jax.numpy as jnp
from jax import lax
from jax.experimental import pallas as pl
from jax.experimental.pallas import tpu as pltpu
from jax.sharding import PartitionSpec as P

HARM = 4096
F32 = jnp.float32
BF16 = jnp.bfloat16


def split(value):
    head = lax.reduce_precision(value, 8, 7)
    return head.astype(BF16), (value - head).astype(BF16)


def moment_weights(harmonic, lines):
    ratios = harmonic.astype(F32) / HARM
    squared = ratios * ratios
    return jnp.stack([jnp.ones_like(ratios), ratios, squared, squared * squared]) / lines


def nt(a, b):
    return lax.dot_general(a, b, (((1,), (1,)), ((), ())), preferred_element_type=F32)


def nn(a, b):
    return jnp.dot(a, b, preferred_element_type=F32)


def kernel_split(value):
    head = value.astype(BF16)
    return head, (value - head.astype(F32)).astype(BF16)


def step_body(count, spectra_on, time_on, carried, idx_ref, *refs):
    refs = list(refs)
    take = lambda n: [refs.pop(0) for _ in range(n)]
    panels = take(count)
    if spectra_on:
        own, other = take(count), take(count)
    if time_on:
        v_head, v_tail = take(count), take(count)
        t_head, t_tail = take(2)
    spectra_in = take(1)[0] if spectra_on and carried else None
    stress_in = take(1)[0] if time_on and carried else None
    spectra_out = take(1)[0] if spectra_on else None
    stress_out = take(1)[0] if time_on else None
    grids = take(count) if time_on else None

    step = pl.program_id(0) * pl.num_programs(1) + pl.program_id(1)
    last = pl.num_programs(0) * pl.num_programs(1) - 1
    if spectra_on:
        rows = own[0].shape[0]
        for part, table in ((0, own), (1, other)):
            here = pl.ds(part * rows, rows)
            total = spectra_in[0, here, :] if carried else None
            for shape_ref, panel in zip(table, panels):
                term = nt(shape_ref[...], panel[0])
                total = term if total is None else total + term
            spectra_out[0, here, :] = total
    if time_on:
        for panel, grid in zip(panels, grids):
            term = nn(t_head[...], panel[0]) + nn(t_tail[...], panel[0])

            @pl.when(step == 0)
            def _():
                grid[...] = term

            @pl.when(step > 0)
            def _():
                grid[...] += term

        @pl.when(step == last)
        def _():
            total = stress_in[...] if carried else None
            for head, tail, grid in zip(v_head, v_tail, grids):
                g_head, g_tail = kernel_split(grid[...])
                term = nt(head[...], g_head) + nt(tail[...], g_head) + nt(head[...], g_tail)
                total = term if total is None else total + term
            stress_out[...] = total


def block_step(blocks, cols, shapes, v, t, spectra, stress, spectra_on=True, time_on=True):
    count = len(blocks)
    parts, lines, modes = blocks[0].shape
    rows = shapes[0].shape[0]
    elems, steps = v[0].shape[0], t[0].shape[0]
    carried = (spectra if spectra_on else stress) is not None
    tile = min(lines, 256)
    tiles = lines // tile

    def col(b):
        return lambda i, j, idx: (0, idx[b])

    in_specs = [pl.BlockSpec((1, tile, modes), lambda i, j, idx: (i, j, 0))] * count
    args = list(blocks)
    flops = bytes_moved = 0
    if spectra_on:
        for table in shapes:
            in_specs += [pl.BlockSpec((rows, modes), col(b)) for b in range(count)]
            args += [table] * count
        flops += 2 * count * parts * lines * modes * 2 * rows
        bytes_moved += 2 * parts * 2 * rows * lines * 4
    if time_on:
        for table in v:
            in_specs += [pl.BlockSpec((elems, modes), col(b)) for b in range(count)]
            args += [table] * count
        in_specs += [pl.BlockSpec((steps, tile), lambda i, j, idx: (0, i * tiles + j))] * 2
        args += list(t)
        flops += count * 2 * modes * steps * (2 * parts * lines + 3 * elems)
        bytes_moved += 2 * elems * steps * 4
    spectra_spec = pl.BlockSpec((1, 2 * rows, tile), lambda i, j, idx: (i, 0, j))
    stress_spec = pl.BlockSpec((elems, steps), lambda i, j, idx: (0, 0))
    out_specs, out_shape, aliases = [], [], {}
    if spectra_on:
        if carried:
            aliases[len(args) + 1] = len(out_specs)
            in_specs.append(spectra_spec)
            args.append(spectra)
        out_specs.append(spectra_spec)
        out_shape.append(jax.ShapeDtypeStruct((parts, 2 * rows, lines), F32))
    if time_on:
        if carried:
            aliases[len(args) + 1] = len(out_specs)
            in_specs.append(stress_spec)
            args.append(stress)
        out_specs.append(stress_spec)
        out_shape.append(jax.ShapeDtypeStruct((elems, steps), F32))
    return pl.pallas_call(
        functools.partial(step_body, count, spectra_on, time_on, carried),
        out_shape=out_shape,
        grid_spec=pltpu.PrefetchScalarGridSpec(
            num_scalar_prefetch=1,
            grid=(parts, tiles),
            in_specs=in_specs,
            out_specs=out_specs,
            scratch_shapes=[pltpu.VMEM((steps, modes), F32)] * (count if time_on else 0),
        ),
        input_output_aliases=aliases,
        compiler_params=pltpu.CompilerParams(vmem_limit_bytes=40 << 20),
        cost_estimate=pl.CostEstimate(
            flops=flops, bytes_accessed=bytes_moved + count * parts * lines * modes * 2, transcendentals=0
        ),
        name="block_step",
    )(cols, *args)


def moment_body(count, idx_ref, *refs):
    refs = list(refs)
    take = lambda n: [refs.pop(0) for _ in range(n)]
    panels, own, other = take(count), take(count), take(count)
    w_head, w_tail, spectra, out = refs
    rows = own[0].shape[0]
    for part, table in ((0, own), (1, other)):
        here = pl.ds(part * rows, rows)
        power = None
        for c in range(2):
            total = spectra[c, here, :]
            for shape_ref, panel in zip(table, panels):
                total = total + nt(shape_ref[...], panel[c])
            power = total * total if power is None else power + total * total
        p_head, p_tail = kernel_split(power)
        term = nt(w_head[...], p_head) + nt(w_tail[...], p_head) + nt(w_head[...], p_tail)

        @pl.when(pl.program_id(0) == 0)
        def _():
            out[:, here] = term

        @pl.when(pl.program_id(0) > 0)
        def _():
            out[:, here] += term


def block_moments(blocks, cols, shapes, weights, spectra):
    count = len(blocks)
    parts, lines, modes = blocks[0].shape
    rows = shapes[0].shape[0]
    tile = min(lines, 128)

    def col(b):
        return lambda j, idx: (0, idx[b])

    in_specs = [pl.BlockSpec((parts, tile, modes), lambda j, idx: (0, j, 0))] * count
    args = list(blocks)
    for table in shapes:
        in_specs += [pl.BlockSpec((rows, modes), col(b)) for b in range(count)]
        args += [table] * count
    in_specs += [pl.BlockSpec((weights[0].shape[0], tile), lambda j, idx: (0, j))] * 2
    in_specs.append(pl.BlockSpec((parts, 2 * rows, tile), lambda j, idx: (0, 0, j)))
    args += [*weights, spectra]
    return pl.pallas_call(
        functools.partial(moment_body, count),
        out_shape=jax.ShapeDtypeStruct((weights[0].shape[0], 2 * rows), F32),
        grid_spec=pltpu.PrefetchScalarGridSpec(
            num_scalar_prefetch=1,
            grid=(lines // tile,),
            in_specs=in_specs,
            out_specs=pl.BlockSpec((weights[0].shape[0], 2 * rows), lambda j, idx: (0, 0)),
        ),
        compiler_params=pltpu.CompilerParams(vmem_limit_bytes=40 << 20),
        cost_estimate=pl.CostEstimate(
            flops=2 * count * parts * lines * modes * 2 * rows,
            bytes_accessed=parts * 2 * rows * lines * 4,
            transcendentals=0,
        ),
        name="block_moments",
    )(cols, *args)


def paired_shards(n_mode, panels, shapes, harmonic, connect, recovery, *, steps):
    tie = lax.optimization_barrier
    place = lax.axis_index("mode")
    core, side, layer = place % 2, place // 2 % 2, place // 4
    layers = n_mode // 4
    ring = lambda a: lax.ppermute(a, "mode", [(i, (i + 4) % n_mode) for i in range(n_mode)])
    across = lambda a: lax.ppermute(a, "mode", [(i, i ^ 2) for i in range(n_mode)])
    mate = lambda a: lax.ppermute(a, "mode", [(i, i ^ 1) for i in range(n_mode)])
    peer = lambda a: lax.ppermute(a, "node", [(0, 1), (1, 0)])

    lines = panels.shape[1] // 2
    total_lines = panels.shape[1] * 2
    rows = shapes.shape[0]
    parts, _, modes = panels.shape
    mine = lax.dynamic_slice(panels, (0, core * lines, 0), (parts, lines, modes))
    theirs = lax.dynamic_slice(panels, (0, (1 - core) * lines, 0), (parts, lines, modes))

    z = [[mine], [mate(theirs)]]
    x = [[], []]
    for s in range(layers - 1):
        for h in range(2):
            moved, swapped = tie((ring(z[h][-1]), across(z[h][-1])))
            z[h].append(moved)
            x[h].append(swapped)
    final = [across(z[0][-1]), ring(x[1][-1])]

    def cols(*wanted):
        out = []
        for back, flip, h in wanted:
            at = (layer - back) % layers
            xs = 1 - side if flip else side
            cs = 1 - core if h else core
            out.append((at * 2 + xs) * 2 + cs)
        return jnp.stack(out).astype(jnp.int32)

    local = (connect - place * rows).astype(F32)
    packed = jnp.stack([local.T, recovery.T])
    own_pair = jnp.concatenate([packed, peer(packed)], axis=2)
    other_pair = mate(own_pair)
    other_shapes = mate(shapes)
    slots = jnp.arange(rows, dtype=jnp.int32).astype(F32)
    v_parts = []
    for pair, table in ((own_pair, shapes), (other_pair, other_shapes)):
        hit = pair[0][:, None, :] == slots[None, :, None]
        weight = jnp.sum(jnp.where(hit, pair[1][:, None, :], 0.0), axis=0)
        dims = (((0,), (0,)), ((), ()))
        v_parts.append(
            sum(lax.dot_general(w, table, dims, preferred_element_type=F32) for w in split(weight))
        )
    v = split(jnp.concatenate(v_parts, axis=0))

    mine_h = lax.dynamic_slice(harmonic, (core * lines,), (lines,))
    step_ids = jnp.arange(steps, dtype=jnp.int32)
    phases = step_ids[:, None] * mine_h[None, :] % HARM
    angles = phases.astype(F32) * (2.0 * math.pi / HARM)
    scale = math.sqrt(2.0 / total_lines)
    table = jnp.concatenate([scale * jnp.cos(angles), -scale * jnp.sin(angles)], axis=1)
    t = split(table)
    weights = split(jnp.pad(moment_weights(mine_h, total_lines), ((0, 4), (0, 0))))

    both = (shapes, other_shapes)
    spectra, stress = block_step(
        [z[0][0], z[1][0]], cols((0, 0, 0), (0, 0, 1)), both, v, t, None, None
    )
    for s in range(layers - 1):
        for h in range(2):
            spectra, stress = block_step(
                [x[h][s], z[h][s + 1]], cols((s, 1, h), (s + 1, 0, h)), both, v, t, spectra, stress
            )
    ends = cols((layers - 1, 1, 0), (layers - 1, 1, 1))
    (stress,) = block_step(final, ends, both, v, t, None, stress, spectra_on=False)
    moments = block_moments(final, ends, both, weights, spectra)

    elems = connect.shape[0]
    keep, give = stress[: 2 * elems], stress[2 * elems :]
    keep = keep + mate(give)
    stress = keep[:elems] + peer(keep[elems:])
    half = moments[:, :rows] + mate(moments[:, rows:])
    node = lax.axis_index("node")
    mine_m = lax.dynamic_slice(half, (0, node * (rows // 2)), (8, rows // 2))
    give_m = lax.dynamic_slice(half, (0, (1 - node) * (rows // 2)), (8, rows // 2))
    moments = mine_m + peer(give_m)
    return stress, moments[:4]


def plain_shards(panels, shapes, harmonic, connect, recovery, *, steps, total_lines):
    highest = lax.Precision.HIGHEST
    rows_mode = shapes.shape[0]
    spectra = jnp.einsum(
        "cfm,rm->cfr",
        lax.all_gather(panels, "mode", axis=2, tiled=True),
        shapes,
        preferred_element_type=F32,
    )
    step_ids = jnp.arange(steps, dtype=jnp.int32)
    phases = harmonic[:, None] * step_ids[None, :] % HARM
    angles = phases.astype(F32) * (2.0 * math.pi / HARM)
    weights = moment_weights(harmonic, total_lines)
    history = jnp.einsum("fr,ft->rt", spectra[0], jnp.cos(angles), precision=highest)
    history = history - jnp.einsum("fr,ft->rt", spectra[1], jnp.sin(angles), precision=highest)
    power = spectra[0] * spectra[0] + spectra[1] * spectra[1]
    history = math.sqrt(2.0 / total_lines) * history
    moments = jnp.dot(weights, power, precision=highest)
    history = lax.psum_scatter(history, "node", scatter_dimension=0, tiled=True)
    moments = lax.psum_scatter(moments, "node", scatter_dimension=1, tiled=True)
    rows_in = lax.all_gather(history.astype(BF16), "node", axis=0, tiled=True)
    local = connect - lax.axis_index("mode") * rows_mode
    slots = jnp.arange(rows_mode, dtype=jnp.int32)
    hit = local[:, :, None] == slots[None, None, :]
    weight = jnp.sum(jnp.where(hit, recovery[:, :, None], 0.0), axis=1)
    stress = jnp.dot(weight, rows_in, preferred_element_type=F32, precision=highest)
    return stress, moments


STEPS = 512


def solution(mesh):
    n_mode, n_node = mesh.shape["mode"], mesh.shape["node"]

    def shards(panels, *rest):
        if n_node == 2 and n_mode % 4 == 0 and n_mode >= 8:
            return paired_shards(n_mode, panels, *rest, steps=STEPS)
        return plain_shards(panels, *rest, steps=STEPS, total_lines=panels.shape[1] * n_node)

    return jax.shard_map(
        shards,
        mesh=mesh,
        in_specs=(
            P(None, "node", "mode"),
            P("mode", None),
            P("node"),
            P(("mode", "node"), None),
            P(("mode", "node"), None),
        ),
        out_specs=(P(("mode", "node"), None), P(None, ("mode", "node"))),
        check_vma=False,
    )
```

time: 223 us -> 192 us (0.86)
  waiting for transfers between devices: 151 us -> 51.5 us
  Pallas kernels: 0 us -> 77.5 us
  matrix products: 44.4 us -> 12.2 us
  starting transfers between devices: 0.12 us -> 21.9 us
  other arithmetic: 2.46 us -> 16.5 us
  between operations: 13.8 us -> 0.91 us
  local copies, waits for them, and re-layouts: 1.8 us -> 11.2 us
  blocking collectives: 8.73 us -> 0 us
    all_gather x1 -> x0, waiting for transfers between devices: 135 us -> none  [shards(): lax.all_gather(panels, 'mode', axis=2, tiled=True)]
    pallas_call x0 -> x9, Pallas kernels: none -> 77.5 us  [the longest x8 70.4 us: block_step(): pl.pallas_call(functools.partial(step_body, count, spectra_on, time_on, c...]
    ppermute x0 -> x22, waiting for transfers between devices: none -> 51.5 us  [the longest x7 43.4 us: paired_shards(): lax.ppermute(a, 'mode', [(i, (i + 4) % n_mode) for i in range(n_mode)])]
    dot_general x4, matrix products: 40 us -> 12.2 us  [paired_shards(): lax.dot_general(w, table, dims, preferred_element_type=F32)]
    ppermute x0 -> x22, starting transfers between devices: none -> 21.9 us  [the longest x7 11.6 us: paired_shards(): lax.ppermute(a, 'mode', [(i, (i + 4) % n_mode) for i in range(n_mode)])]
    reduce_scatter x1 -> x0, waiting for transfers between devices: 16.1 us -> none  [shards(): lax.psum_scatter(history_part, 'node', scatter_dimension=0, tiled=True)]
    all_gather x1 -> x0, blocking collectives: 8.73 us -> none  [shards(): rows_in = lax.all_gather(histories, 'node', axis=0, tiled=True)]
    unnamed x10 -> x24, local copies, waits for them, and re-layouts: 1.7 us -> 9.03 us
  transfers between devices with their start and end apart: 3 -> 22, of which waited for: 2 -> 8; matrix products, arithmetic and copies ran while one was open for 8% -> 16% of each run, Pallas kernels for 0% -> 37%
where the time goes in v1:
time: 192 us
  Pallas kernels  77.5 us (40%)
  waiting for transfers between devices  51.5 us (27%)
  starting transfers between devices  21.9 us (11%)
  other arithmetic  16.5 us (9%)
  matrix products  12.2 us (6%)
  local copies, waits for them, and re-layouts  11.2 us (6%)
    pallas_call x8, Pallas kernels, block_step(): pl.pallas_call(functools.partial(step_body, count, spectra_on, time_on, c...  70.4 us
    ppermute x7, waiting for transfers between devices, paired_shards(): lax.ppermute(a, 'mode', [(i, (i + 4) % n_mode) for i in range(n_mode)])  43.4 us
    dot_general x4, matrix products, paired_shards(): lax.dot_general(w, table, dims, preferred_element_type=F32)  12.2 us
    ppermute x7, starting transfers between devices, paired_shards(): lax.ppermute(a, 'mode', [(i, (i + 4) % n_mode) for i in range(n_mode)])  11.6 us
    unnamed x24, local copies, waits for them, and re-layouts  9.03 us
    pallas_call x1, Pallas kernels, block_moments(): pl.pallas_call(functools.partial(moment_body, count), out_shape=jax.Shape...  7.08 us
    ppermute x3, waiting for transfers between devices, paired_shards(): peer = lambda a: lax.ppermute(a, 'node', [(0, 1), (1, 0)])  6.49 us
    convert_element_type x3, other arithmetic, split(): return (head.astype(BF16), (value - head).astype(BF16))  6.42 us
  transfers between devices with their start and end apart: 22, of which 8 were waited for; matrix products, arithmetic and copies ran while one was open for 16% of the time, Pallas kernels for 37%

profile of v1, /device:TPU:0, one launch (start us, length us, event | category | flops | bytes accessed | tf_op | source)
XLA Modules:
  0.0 191.7 jit_solution(10541426678006029685)
XLA Ops:
  1.1 2.1 %constant_dynamic-slice_fusion.1 = (bf16[2,512,256]{2,1,0:T(8,128)(2,1)}, bf16[2,512,256]{2,1,0:T(8,128)(2,1)S(1)}) fusion(bf16[2,1024,256]{2,1,0:T(8,128)(2,1)} %param.5, s32[]{:T(128)S(6)} %select_n.90, s32[]{:T(128)S(6)} %select_n.89), kind=kLoop, calls=%fused_computation.49 | loop fusion | bytes 2097160 | tf_op jit(solution)/shard_map/dynamic_slice | solution.py:230
  3.2 2.6 %collective-permute-start = (bf16[2,512,256]{2,1,0:T(8,128)(2,1)S(1)}, bf16[2,512,256]{2,1,0:T(8,128)(2,1)S(1)}, u32[]{:S(2)}, u32[]{:S(2)}) collective-permute-start(bf16[2,512,256]{2,1,0:T(8,128)(2,1)S(1)} %get-tuple-element.63.refs_0_), channel_id=1, source_target_pairs={{0,8},{2,10},{4,12},{6,14},{8,16},{10,18},{12,20},{14,22},{16,24},... | collective-permute-start | bytes 1572872 | tf_op jit(solution)/shard_map/ppermute | solution.py:220
  8.7 1.5 collective-permute-start.15
  11.1 5.1 %cosine_multiply_fusion = (f32[512,512]{1,0:T(8,128)}, f32[512,512]{1,0:T(8,128)}) fusion(s32[512]{0:T(512)S(1)} %get-tuple-element.57), kind=kLoop, calls=%fused_computation.19 | loop fusion | flops 4194304 | bytes 2099200 | tf_op jit(solution)/shard_map/mul | solution.py:271
  16.3 2.0 %fusion.1 = (bf16[512,1024]{1,0:T(8,128)(2,1)S(1)}, bf16[512,1024]{1,0:T(8,128)(2,1)S(1)}) fusion(f32[512,512]{1,0:T(8,128)} %get-tuple-element.73, f32[512,512]{1,0:T(8,128)} %get-tuple-element.72), kind=kLoop, calls=%fused_computation.10 | loop fusion | flops 2621440 | bytes 4194304 | tf_op jit(solution)/shard_map/convert_element_type | solution.py:18
  18.7 1.6 collective-permute-start.8
  20.9 1.6 collective-permute-start.2
  24.1 11.4 %collective-permute-done.8.refs_1_ = bf16[2,512,256]{2,1,0:T(8,128)(2,1)S(1)} collective-permute-done((bf16[2,512,256]{2,1,0:T(8,128)(2,1)}, bf16[2,512,256]{2,1,0:T(8,128)(2,1)S(1)}, u32[]{:S(2)}, u32[]{:S(2)}) %collective-permute-start.8) | collective-permute-done | bytes 524320 | tf_op jit(solution)/shard_map/ppermute | solution.py:220
  38.3 3.6 %fusion.13 = f32[256,4096]{1,0:T(8,128)S(1)} fusion(bf16[512,4096]{1,0:T(8,128)(2,1)} %refs_3_.15, f32[512,256]{1,0:T(8,128)S(1)} %get-tuple-element.54), kind=kOutput, calls=%fused_computation.31 | convolution fusion | flops 1074003968 | bytes 8912896 | tf_op jit(solution)/shard_map/dot_general | solution.py:262
  42.0 4.7 %collective-permute-done.2.refs_1_ = bf16[2,512,256]{2,1,0:T(8,128)(2,1)S(1)} collective-permute-done((bf16[2,512,256]{2,1,0:T(8,128)(2,1)S(1)}, bf16[2,512,256]{2,1,0:T(8,128)(2,1)S(1)}, u32[]{:S(2)}, u32[]{:S(2)}) %collective-permute-start.2) | collective-permute-done | bytes 524320 | tf_op jit(solution)/shard_map/ppermute | solution.py:220
  48.7 9.3 %collective-permute-done.10.refs_1_ = bf16[2,512,256]{2,1,0:T(8,128)(2,1)S(1)} collective-permute-done((bf16[2,512,256]{2,1,0:T(8,128)(2,1)S(1)}, bf16[2,512,256]{2,1,0:T(8,128)(2,1)S(1)}, u32[]{:S(2)}, u32[]{:S(2)}) %collective-permute-start.10) | collective-permute-done | bytes 524320 | tf_op jit(solution)/shard_map/ppermute | solution.py:220
  61.3 7.9 %collective-permute-done.4.refs_1_ = bf16[2,512,256]{2,1,0:T(8,128)(2,1)S(1)} collective-permute-done((bf16[2,512,256]{2,1,0:T(8,128)(2,1)S(1)}, bf16[2,512,256]{2,1,0:T(8,128)(2,1)S(1)}, u32[]{:S(2)}, u32[]{:S(2)}) %collective-permute-start.4) | collective-permute-done | bytes 524320 | tf_op jit(solution)/shard_map/ppermute | solution.py:220
  69.7 10.1 %collective-permute-done.12.refs_1_ = bf16[2,512,256]{2,1,0:T(8,128)(2,1)S(1)} collective-permute-done((bf16[2,512,256]{2,1,0:T(8,128)(2,1)S(1)}, bf16[2,512,256]{2,1,0:T(8,128)(2,1)S(1)}, u32[]{:S(2)}, u32[]{:S(2)}) %collective-permute-start.12) | collective-permute-done | bytes 524320 | tf_op jit(solution)/shard_map/ppermute | solution.py:220
  80.2 1.6 collective-permute-start.14
  81.8 3.5 %fusion.10 = f32[256,4096]{1,0:T(8,128)S(1)} fusion(bf16[512,4096]{1,0:T(8,128)(2,1)} %collective-permute-done.17.refs_4_.refs_5_, f32[512,256]{1,0:T(8,128)S(1)} %get-tuple-element.55), kind=kOutput, calls=%fused_computation.30 | convolution fusion | flops 1074135040 | bytes 8912896 | tf_op jit(solution)/shard_map/dot_general | solution.py:262
  85.3 3.6 %convolution_add_fusion = f32[256,4096]{1,0:T(8,128)S(1)} fusion(f32[256,4096]{1,0:T(8,128)S(1)} %fusion.10, bf16[512,4096]{1,0:T(8,128)(2,1)} %collective-permute-done.17.refs_4_.refs_5_, f32[512,256]{1,0:T(8,128)S(1)} %get-tuple-element.55), kind=kOutput, calls=%fused_computation.4 | convolution fusion | flops 1075052544 | bytes 13107200 | tf_op jit(solution)/shard_map/dot_general | solution.py:262
  89.0 4.5 %fusion = (bf16[512,4096]{1,0:T(8,128)(2,1)}, bf16[512,4096]{1,0:T(8,128)(2,1)}) fusion(f32[256,4096]{1,0:T(8,128)S(1)} %convolution_add_fusion, f32[256,4096]{1,0:T(8,128)S(1)} %convolution_add_fusion.1), kind=kLoop, calls=%fused_computation.2 | loop fusion | flops 10485760 | bytes 16777216 | tf_op jit(solution)/shard_map/convert_element_type | solution.py:18
  93.4 8.9 %block_step.8 = (f32[2,1024,512]{2,1,0:T(8,128)S(1)}, f32[512,512]{1,0:T(8,128)S(1)}) custom-call(s32[2]{0:T(128)S(1)} %get-tuple-element.79.idx_ref, bf16[2,512,256]{2,1,0:T(8,128)(2,1)S(1)} %get-tuple-element.63.refs_0_, bf16[2,512,256]{2,1,0:T(8,128)(2,1)} %collective-permute-done.7.refs_1_, bf16[512,4096]{1,0:T(8,128)(2,1)S(1)} %copy-done, ...), custom_call_target="tpu_custom_call" | custom-call | flops 2952790016 | bytes 11534336 | tf_op jit(solution)/shard_map/block_step/pallas_call | solution.py:134
  102.3 9.2 %block_step.9 = (f32[2,1024,512]{2,1,0:T(8,128)S(1)}, f32[512,512]{1,0:T(8,128)S(1)}) custom-call(s32[2]{0:T(128)S(1)} %get-tuple-element.78.idx_ref, bf16[2,512,256]{2,1,0:T(8,128)(2,1)} %collective-permute-done.1.refs_0_, bf16[2,512,256]{2,1,0:T(8,128)(2,1)S(1)} %copy-done.10, ...), custom_call_target="tpu_custom_call", output_to_operand_aliasing={{0}: (13, {}), {1}: (14, {})} | custom-call | flops 2952790016 | bytes 11534336 | tf_op jit(solution)/shard_map/block_step/pallas_call | solution.py:134
  111.6 9.1 %block_step.10 = (f32[2,1024,512]{2,1,0:T(8,128)S(1)}, f32[512,512]{1,0:T(8,128)S(1)}) custom-call(s32[2]{0:T(128)S(1)} %pad_add_fusion.5.idx_ref, bf16[2,512,256]{2,1,0:T(8,128)(2,1)S(1)} %collective-permute-done.9.refs_0_, bf16[2,512,256]{2,1,0:T(8,128)(2,1)S(1)} %collective-permute-done.8.refs_1_, ...), custom_call_target="tpu_custom_call", output_to_operand_aliasing={{0}: (13, {}), {1}: (14, {})} | custom-call | flops 2952790016 | bytes 11534336 | tf_op jit(solution)/shard_map/block_step/pallas_call | solution.py:134
  120.7 9.2 %block_step.11 = (f32[2,1024,512]{2,1,0:T(8,128)S(1)}, f32[512,512]{1,0:T(8,128)S(1)}) custom-call(s32[2]{0:T(128)S(1)} %get-tuple-element.77.idx_ref, bf16[2,512,256]{2,1,0:T(8,128)(2,1)S(1)} %collective-permute-done.3.refs_0_, bf16[2,512,256]{2,1,0:T(8,128)(2,1)S(1)} %collective-permute-done.2.refs_1_, ...), custom_call_target="tpu_custom_call", output_to_operand_aliasing={{0}: (13, {}), {1}: (14, {})} | custom-call | flops 2952790016 | bytes 11534336 | tf_op jit(solution)/shard_map/block_step/pallas_call | solution.py:134
  129.9 9.1 %block_step.12 = (f32[2,1024,512]{2,1,0:T(8,128)S(1)}, f32[512,512]{1,0:T(8,128)S(1)}) custom-call(s32[2]{0:T(128)S(1)} %get-tuple-element.76.idx_ref, bf16[2,512,256]{2,1,0:T(8,128)(2,1)S(1)} %collective-permute-done.11.refs_0_, bf16[2,512,256]{2,1,0:T(8,128)(2,1)S(1)} %collective-permute-done.10.refs_1_, ...), custom_call_target="tpu_custom_call", output_to_operand_aliasing={{0}: (13, {}), {1}: (14, {})} | custom-call | flops 2952790016 | bytes 11534336 | tf_op jit(solution)/shard_map/block_step/pallas_call | solution.py:134
  139.0 9.1 %block_step.13 = (f32[2,1024,512]{2,1,0:T(8,128)S(1)}, f32[512,512]{1,0:T(8,128)S(1)}) custom-call(s32[2]{0:T(128)S(1)} %get-tuple-element.75.idx_ref, bf16[2,512,256]{2,1,0:T(8,128)(2,1)S(1)} %collective-permute-done.5.refs_0_, bf16[2,512,256]{2,1,0:T(8,128)(2,1)S(1)} %collective-permute-done.4.refs_1_, ...), custom_call_target="tpu_custom_call", output_to_operand_aliasing={{0}: (13, {}), {1}: (14, {})} | custom-call | flops 2952790016 | bytes 11534336 | tf_op jit(solution)/shard_map/block_step/pallas_call | solution.py:134
  148.2 1.9 %copy-done.3 = f32[2,1024,512]{2,1,0:T(8,128)} copy-done((f32[2,1024,512]{2,1,0:T(8,128)}, f32[2,1024,512]{2,1,0:T(8,128)S(1)}, u32[]{:S(2)}) %copy-start.3) | copy-done | bytes 4194328
  150.1 2.2 %copy-done.4 = f32[2,1024,512]{2,1,0:T(8,128)S(1)} copy-done((f32[2,1024,512]{2,1,0:T(8,128)S(1)}, f32[2,1024,512]{2,1,0:T(8,128)}, u32[]{:S(2)}) %copy-start.4) | copy-done | bytes 4194328
  152.3 9.8 %block_step.14 = (f32[2,1024,512]{2,1,0:T(8,128)S(1)}, f32[512,512]{1,0:T(8,128)S(1)}) custom-call(s32[2]{0:T(128)S(1)} %get-tuple-element.74.idx_ref, bf16[2,512,256]{2,1,0:T(8,128)(2,1)S(1)} %collective-permute-done.13.refs_0_, bf16[2,512,256]{2,1,0:T(8,128)(2,1)S(1)} %collective-permute-done.12.refs_1_, ...), custom_call_target="tpu_custom_call", output_to_operand_aliasing={{0}: (13, {}), {1}: (14, {})} | custom-call | flops 2952790016 | bytes 11534336 | tf_op jit(solution)/shard_map/block_step/pallas_call | solution.py:134
  162.2 1.9 %copy-done.5 = f32[2,1024,512]{2,1,0:T(8,128)} copy-done((f32[2,1024,512]{2,1,0:T(8,128)}, f32[2,1024,512]{2,1,0:T(8,128)S(1)}, u32[]{:S(2)}) %copy-start.5) | copy-done | bytes 4194328
  164.1 5.9 %block_step.15 = f32[512,512]{1,0:T(8,128)S(1)} custom-call(s32[2]{0:T(128)S(1)} %pad_add_fusion.idx_ref, bf16[2,512,256]{2,1,0:T(8,128)(2,1)S(1)} %collective-permute-done.6.refs_0_, bf16[2,512,256]{2,1,0:T(8,128)(2,1)S(1)} %collective-permute-done.14.refs_1_, bf16[512,4096]{1,0:T(8,128)(2,1)S(1)} %copy-done.2, ...), custom_call_target="tpu_custom_call", output_to_operand_aliasing={{}: (9, {})} | custom-call | flops 1879048192 | bytes 3145728 | tf_op jit(solution)/shard_map/block_step/pallas_call | solution.py:134
  171.0 2.2 %copy-done.6 = f32[2,1024,512]{2,1,0:T(8,128)S(1)} copy-done((f32[2,1024,512]{2,1,0:T(8,128)S(1)}, f32[2,1024,512]{2,1,0:T(8,128)}, u32[]{:S(2)}) %copy-start.6) | copy-done | bytes 4194328
  173.2 7.1 %block_moments.1 = f32[8,1024]{1,0:T(8,128)S(1)} custom-call(s32[2]{0:T(128)S(1)} %pad_add_fusion.idx_ref, bf16[2,512,256]{2,1,0:T(8,128)(2,1)S(1)} %collective-permute-done.6.refs_0_, bf16[2,512,256]{2,1,0:T(8,128)(2,1)S(1)} %collective-permute-done.14.refs_1_, bf16[512,4096]{1,0:T(8,128)(2,1)S(1)} %copy-done, bf16[512,4096]{1,0:T(8,128)(2,1)S(1)} %copy-done, ...), custom_call_target="tpu_custom_call" | custom-call | flops 1073741824 | bytes 4194304 | tf_op jit(solution)/shard_map/block_moments/pallas_call | solution.py:196
  182.3 1.5 collective-permute-start.21
  183.8 6.5 %collective-permute-done.21 = f32[8,256]{1,0:T(8,128)S(1)} collective-permute-done((f32[8,256]{1,0:T(8,128)S(1)}, f32[8,256]{1,0:T(8,128)S(1)}, u32[]{:S(2)}, u32[]{:S(2)}) %collective-permute-start.21) | collective-permute-done | bytes 8224 | tf_op jit(solution)/shard_map/ppermute | solution.py:223
  (78 shorter events, 20.3 us)
Async XLA Ops:
  0.6 81.2 %collective-permute-start.17 = (bf16[512,4096]{1,0:T(8,128)(2,1)}, bf16[512,4096]{1,0:T(8,128)(2,1)}, u32[]{:S(2)}, u32[]{:S(2)}) collective-permute-start(bf16[512,4096]{1,0:T(8,128)(2,1)} %refs_3_.15), channel_id=1, source_target_pairs={{0,2},{2,0},{4,6},{6,4},{8,10},{10,8},{12,14},{14,12},{16,18},{18,... | collective-permute-start | bytes 12582920 | tf_op jit(solution)/shard_map/ppermute | solution.py:222
  1.1 17.2 %copy-start.11 = (f32[128,8]{0,1:T(8,128)S(1)}, f32[128,8]{0,1:T(8,128)}, u32[]{:S(2)}) copy-start(f32[128,8]{0,1:T(8,128)} %param.9) | copy-start | bytes 12292
  3.2 17.7 %collective-permute-start = (bf16[2,512,256]{2,1,0:T(8,128)(2,1)S(1)}, bf16[2,512,256]{2,1,0:T(8,128)(2,1)S(1)}, u32[]{:S(2)}, u32[]{:S(2)}) collective-permute-start(bf16[2,512,256]{2,1,0:T(8,128)(2,1)S(1)} %get-tuple-element.63.refs_0_), channel_id=1, source_target_pairs={{0,8},{2,10},{4,12},{6,14},{8,16},{10,18},{12,20},{14,22},{16,24},... | collective-permute-start | bytes 1572872 | tf_op jit(solution)/shard_map/ppermute | solution.py:220
  5.8 15.1 %collective-permute-start.1 = (bf16[2,512,256]{2,1,0:T(8,128)(2,1)S(1)}, bf16[2,512,256]{2,1,0:T(8,128)(2,1)}, u32[]{:S(2)}, u32[]{:S(2)}) collective-permute-start(bf16[2,512,256]{2,1,0:T(8,128)(2,1)S(1)} %get-tuple-element.63.refs_0_), channel_id=1, source_target_pairs={{0,4},{2,6},{4,0},{6,2},{8,12},{10,14},{12,8},{14,10},{16,20},{18,... | collective-permute-start | bytes 1572872 | tf_op jit(solution)/shard_map/ppermute | solution.py:221
  7.3 11.4 %collective-permute-start.7 = (bf16[2,512,256]{2,1,0:T(8,128)(2,1)}, bf16[2,512,256]{2,1,0:T(8,128)(2,1)}, u32[]{:S(2)}, u32[]{:S(2)}) collective-permute-start(bf16[2,512,256]{2,1,0:T(8,128)(2,1)} %get-tuple-element.62), channel_id=1, source_target_pairs={{0,2},{2,0},{4,6},{6,4},{8,10},{10,8},{12,14},{14,12},{16,18},{18,... | collective-permute-start | bytes 1572872 | tf_op jit(solution)/shard_map/ppermute | solution.py:222
  8.7 9.6 %collective-permute-start.15 = (f32[2,8,128]{2,1,0:T(8,128)S(1)}, f32[2,8,128]{2,1,0:T(8,128)S(1)}, u32[]{:S(2)}, u32[]{:S(2)}) collective-permute-start(f32[2,8,128]{2,1,0:T(8,128)S(1)} %pad_maximum_fusion.3), channel_id=1, source_target_pairs={{0,1},{1,0},{2,3},{3,2},{4,5},{5,4},{6,7},{7,6},{8,9},{9,8},{10,11... | collective-permute-start | bytes 24584 | tf_op jit(solution)/shard_map/ppermute | solution.py:223
  18.3 2.0 %collective-permute-start.16 = (f32[2,8,256]{2,1,0:T(8,128)S(1)}, f32[2,8,256]{2,1,0:T(8,128)S(1)}, u32[]{:S(2)}, u32[]{:S(2)}) collective-permute-start(f32[2,8,256]{2,1,0:T(8,128)S(1)} %pad_maximum_fusion.2), channel_id=1, source_target_pairs={{0,2},{2,0},{4,6},{6,4},{8,10},{10,8},{12,14},{14,12},{16,18},{18,... | collective-permute-start | bytes 49160 | tf_op jit(solution)/shard_map/ppermute | solution.py:222
  18.7 16.8 %collective-permute-start.8 = (bf16[2,512,256]{2,1,0:T(8,128)(2,1)}, bf16[2,512,256]{2,1,0:T(8,128)(2,1)S(1)}, u32[]{:S(2)}, u32[]{:S(2)}) collective-permute-start(bf16[2,512,256]{2,1,0:T(8,128)(2,1)} %collective-permute-done.7.refs_1_), channel_id=1, source_target_pairs={{0,8},{2,10},{4,12},{6,14},{8,16},{10,18},{12,20},{14,22},{16,24},... | collective-permute-start | bytes 1572872 | tf_op jit(solution)/shard_map/ppermute | solution.py:220
  20.3 15.2 %collective-permute-start.9 = (bf16[2,512,256]{2,1,0:T(8,128)(2,1)}, bf16[2,512,256]{2,1,0:T(8,128)(2,1)S(1)}, u32[]{:S(2)}, u32[]{:S(2)}) collective-permute-start(bf16[2,512,256]{2,1,0:T(8,128)(2,1)} %collective-permute-done.7.refs_1_), channel_id=1, source_target_pairs={{0,4},{2,6},{4,0},{6,2},{8,12},{10,14},{12,8},{14,10},{16,20},{18,... | collective-permute-start | bytes 1572872 | tf_op jit(solution)/shard_map/ppermute | solution.py:221
  20.9 21.1 %copy-start.9 = (bf16[2,512,256]{2,1,0:T(8,128)(2,1)}, bf16[2,512,256]{2,1,0:T(8,128)(2,1)S(1)}, u32[]{:S(2)}) copy-start(bf16[2,512,256]{2,1,0:T(8,128)(2,1)S(1)} %collective-permute-done.refs_1_) | copy-start | bytes 1572868
  20.9 25.8 %collective-permute-start.2 = (bf16[2,512,256]{2,1,0:T(8,128)(2,1)S(1)}, bf16[2,512,256]{2,1,0:T(8,128)(2,1)S(1)}, u32[]{:S(2)}, u32[]{:S(2)}) collective-permute-start(bf16[2,512,256]{2,1,0:T(8,128)(2,1)S(1)} %collective-permute-done.refs_1_), channel_id=1, source_target_pairs={{0,8},{2,10},{4,12},{6,14},{8,16},{10,18},{12,20},{14,22},{16,24},... | collective-permute-start | bytes 1572872 | tf_op jit(solution)/shard_map/ppermute | solution.py:220
  22.6 24.1 %collective-permute-start.3 = (bf16[2,512,256]{2,1,0:T(8,128)(2,1)S(1)}, bf16[2,512,256]{2,1,0:T(8,128)(2,1)S(1)}, u32[]{:S(2)}, u32[]{:S(2)}) collective-permute-start(bf16[2,512,256]{2,1,0:T(8,128)(2,1)S(1)} %collective-permute-done.refs_1_), channel_id=1, source_target_pairs={{0,4},{2,6},{4,0},{6,2},{8,12},{10,14},{12,8},{14,10},{16,20},{18,... | collective-permute-start | bytes 1572872 | tf_op jit(solution)/shard_map/ppermute | solution.py:221
  35.5 22.5 %collective-permute-start.10 = (bf16[2,512,256]{2,1,0:T(8,128)(2,1)S(1)}, bf16[2,512,256]{2,1,0:T(8,128)(2,1)S(1)}, u32[]{:S(2)}, u32[]{:S(2)}) collective-permute-start(bf16[2,512,256]{2,1,0:T(8,128)(2,1)S(1)} %collective-permute-done.8.refs_1_), channel_id=1, source_target_pairs={{0,8},{2,10},{4,12},{6,14},{8,16},{10,18},{12,20},{14,22},{16,24},... | collective-permute-start | bytes 1572872 | tf_op jit(solution)/shard_map/ppermute | solution.py:220
  36.9 21.1 %collective-permute-start.11 = (bf16[2,512,256]{2,1,0:T(8,128)(2,1)S(1)}, bf16[2,512,256]{2,1,0:T(8,128)(2,1)S(1)}, u32[]{:S(2)}, u32[]{:S(2)}) collective-permute-start(bf16[2,512,256]{2,1,0:T(8,128)(2,1)S(1)} %collective-permute-done.8.refs_1_), channel_id=1, source_target_pairs={{0,4},{2,6},{4,0},{6,2},{8,12},{10,14},{12,8},{14,10},{16,20},{18,... | collective-permute-start | bytes 1572872 | tf_op jit(solution)/shard_map/ppermute | solution.py:221
  38.3 21.6 %copy-start = (bf16[512,4096]{1,0:T(8,128)(2,1)S(1)}, bf16[512,4096]{1,0:T(8,128)(2,1)}, u32[]{:S(2)}) copy-start(bf16[512,4096]{1,0:T(8,128)(2,1)} %refs_3_.15) | copy-start | bytes 12582916
  46.7 22.5 %collective-permute-start.4 = (bf16[2,512,256]{2,1,0:T(8,128)(2,1)S(1)}, bf16[2,512,256]{2,1,0:T(8,128)(2,1)S(1)}, u32[]{:S(2)}, u32[]{:S(2)}) collective-permute-start(bf16[2,512,256]{2,1,0:T(8,128)(2,1)S(1)} %collective-permute-done.2.refs_1_), channel_id=1, source_target_pairs={{0,8},{2,10},{4,12},{6,14},{8,16},{10,18},{12,20},{14,22},{16,24},... | collective-permute-start | bytes 1572872 | tf_op jit(solution)/shard_map/ppermute | solution.py:220
  48.1 21.1 %collective-permute-start.5 = (bf16[2,512,256]{2,1,0:T(8,128)(2,1)S(1)}, bf16[2,512,256]{2,1,0:T(8,128)(2,1)S(1)}, u32[]{:S(2)}, u32[]{:S(2)}) collective-permute-start(bf16[2,512,256]{2,1,0:T(8,128)(2,1)S(1)} %collective-permute-done.2.refs_1_), channel_id=1, source_target_pairs={{0,4},{2,6},{4,0},{6,2},{8,12},{10,14},{12,8},{14,10},{16,20},{18,... | collective-permute-start | bytes 1572872 | tf_op jit(solution)/shard_map/ppermute | solution.py:221
  58.0 21.8 %collective-permute-start.12 = (bf16[2,512,256]{2,1,0:T(8,128)(2,1)S(1)}, bf16[2,512,256]{2,1,0:T(8,128)(2,1)S(1)}, u32[]{:S(2)}, u32[]{:S(2)}) collective-permute-start(bf16[2,512,256]{2,1,0:T(8,128)(2,1)S(1)} %collective-permute-done.10.refs_1_), channel_id=1, source_target_pairs={{0,8},{2,10},{4,12},{6,14},{8,16},{10,18},{12,20},{14,22},{16,24},... | collective-permute-start | bytes 1572872 | tf_op jit(solution)/shard_map/ppermute | solution.py:220
  59.4 20.9 %collective-permute-start.13 = (bf16[2,512,256]{2,1,0:T(8,128)(2,1)S(1)}, bf16[2,512,256]{2,1,0:T(8,128)(2,1)S(1)}, u32[]{:S(2)}, u32[]{:S(2)}) collective-permute-start(bf16[2,512,256]{2,1,0:T(8,128)(2,1)S(1)} %collective-permute-done.10.refs_1_), channel_id=1, source_target_pairs={{0,4},{2,6},{4,0},{6,2},{8,12},{10,14},{12,8},{14,10},{16,20},{18,... | collective-permute-start | bytes 1572872 | tf_op jit(solution)/shard_map/ppermute | solution.py:221
  69.2 94.9 %collective-permute-start.6 = (bf16[2,512,256]{2,1,0:T(8,128)(2,1)S(1)}, bf16[2,512,256]{2,1,0:T(8,128)(2,1)S(1)}, u32[]{:S(2)}, u32[]{:S(2)}) collective-permute-start(bf16[2,512,256]{2,1,0:T(8,128)(2,1)S(1)} %collective-permute-done.4.refs_1_), channel_id=1, source_target_pairs={{0,4},{2,6},{4,0},{6,2},{8,12},{10,14},{12,8},{14,10},{16,20},{18,... | collective-permute-start | bytes 1572872 | tf_op jit(solution)/shard_map/ppermute | solution.py:221
  80.2 83.8 %collective-permute-start.14 = (bf16[2,512,256]{2,1,0:T(8,128)(2,1)S(1)}, bf16[2,512,256]{2,1,0:T(8,128)(2,1)S(1)}, u32[]{:S(2)}, u32[]{:S(2)}) collective-permute-start(bf16[2,512,256]{2,1,0:T(8,128)(2,1)S(1)} %collective-permute-done.13.refs_0_), channel_id=1, source_target_pairs={{0,8},{2,10},{4,12},{6,14},{8,16},{10,18},{12,20},{14,22},{16,24},... | collective-permute-start | bytes 1572872 | tf_op jit(solution)/shard_map/ppermute | solution.py:220
  93.4 8.9 %copy-start.10 = (bf16[2,512,256]{2,1,0:T(8,128)(2,1)S(1)}, bf16[2,512,256]{2,1,0:T(8,128)(2,1)}, u32[]{:S(2)}) copy-start(bf16[2,512,256]{2,1,0:T(8,128)(2,1)} %copy-done.9) | copy-start | bytes 1572868
  148.2 1.9 %copy-start.3 = (f32[2,1024,512]{2,1,0:T(8,128)}, f32[2,1024,512]{2,1,0:T(8,128)S(1)}, u32[]{:S(2)}) copy-start(f32[2,1024,512]{2,1,0:T(8,128)S(1)} %get-tuple-element.50.refs_12_) | copy-start | bytes 12582916
  150.1 2.2 %copy-start.4 = (f32[2,1024,512]{2,1,0:T(8,128)S(1)}, f32[2,1024,512]{2,1,0:T(8,128)}, u32[]{:S(2)}) copy-start(f32[2,1024,512]{2,1,0:T(8,128)} %copy-done.3) | copy-start | bytes 12582916
  152.3 11.8 %copy-start.1 = (bf16[512,4096]{1,0:T(8,128)(2,1)S(1)}, bf16[512,4096]{1,0:T(8,128)(2,1)}, u32[]{:S(2)}) copy-start(bf16[512,4096]{1,0:T(8,128)(2,1)} %get-tuple-element.58.refs_8_.refs_9_.refs_4_.refs_5_) | copy-start | bytes 12582916
  152.3 11.8 %copy-start.2 = (bf16[512,4096]{1,0:T(8,128)(2,1)S(1)}, bf16[512,4096]{1,0:T(8,128)(2,1)}, u32[]{:S(2)}) copy-start(bf16[512,4096]{1,0:T(8,128)(2,1)} %get-tuple-element.59.refs_6_.refs_7_.refs_2_.refs_3_) | copy-start | bytes 12582916
  170.1 11.5 %collective-permute-start.18 = (f32[256,512]{1,0:T(8,128)S(1)}, f32[256,512]{1,0:T(8,128)S(1)}, u32[]{:S(2)}, u32[]{:S(2)}) collective-permute-start(f32[256,512]{1,0:T(8,128)S(1)} %slice.49), channel_id=1, source_target_pairs={{0,2},{2,0},{4,6},{6,4},{8,10},{10,8},{12,14},{14,12},{16,18},{18,... | collective-permute-start | bytes 1572872 | tf_op jit(solution)/shard_map/ppermute | solution.py:222
  171.0 2.2 %copy-start.6 = (f32[2,1024,512]{2,1,0:T(8,128)S(1)}, f32[2,1024,512]{2,1,0:T(8,128)}, u32[]{:S(2)}) copy-start(f32[2,1024,512]{2,1,0:T(8,128)} %copy-done.5) | copy-start | bytes 12582916
  173.2 8.4 %copy-start.8 = (f32[512,512]{1,0:T(8,128)S(1)}, f32[512,512]{1,0:T(8,128)}, u32[]{:S(2)}) copy-start(f32[512,512]{1,0:T(8,128)} %copy-done.7) | copy-start | bytes 3145732
  180.3 1.3 collective-permute-start.20
  181.7 9.2 %collective-permute-start.19 = (f32[128,512]{1,0:T(8,128)S(1)}, f32[128,512]{1,0:T(8,128)S(1)}, u32[]{:S(2)}, u32[]{:S(2)}) collective-permute-start(f32[128,512]{1,0:T(8,128)S(1)} %slice.51), channel_id=1, source_target_pairs={{0,1},{1,0},{2,3},{3,2},{4,5},{5,4},{6,7},{7,6},{8,9},{9,8},{10,11... | collective-permute-start | bytes 786440 | tf_op jit(solution)/shard_map/ppermute | solution.py:223
  182.3 8.0 %collective-permute-start.21 = (f32[8,256]{1,0:T(8,128)S(1)}, f32[8,256]{1,0:T(8,128)S(1)}, u32[]{:S(2)}, u32[]{:S(2)}) collective-permute-start(f32[8,256]{1,0:T(8,128)S(1)} %constant_dynamic-slice_fusion), channel_id=1, source_target_pairs={{0,1},{1,0},{2,3},{3,2},{4,5},{5,4},{6,7},{7,6},{8,9},{9,8},{10,11... | collective-permute-start | bytes 24584 | tf_op jit(solution)/shard_map/ppermute | solution.py:223
  (2 other events, 2.9 us)

commit v2 on v0

v2 whole, which is shorter than its diff:
```python
import functools
import math

import jax
import jax.numpy as jnp
from jax import lax
from jax.experimental import pallas as pl
from jax.experimental.pallas import tpu as pltpu
from jax.sharding import PartitionSpec as P

HARM = 4096
F32 = jnp.float32
BF16 = jnp.bfloat16


def split(value):
    head = lax.reduce_precision(value, 8, 7)
    return head.astype(BF16), (value - head).astype(BF16)


def moment_weights(harmonic, lines):
    ratios = harmonic.astype(F32) / HARM
    squared = ratios * ratios
    return jnp.stack([jnp.ones_like(ratios), ratios, squared, squared * squared]) / lines


def nt(a, b):
    return lax.dot_general(a, b, (((1,), (1,)), ((), ())), preferred_element_type=F32)


def nn(a, b):
    return jnp.dot(a, b, preferred_element_type=F32)


def kernel_split(value):
    head = value.astype(BF16)
    return head, (value - head.astype(F32)).astype(BF16)


VMEM = pl.BlockSpec(memory_space=pltpu.VMEM)
SMEM = pl.BlockSpec(memory_space=pltpu.SMEM)


def on_chip(body, out_shapes, operands, name, aliases=None):
    outs = [pltpu.VMEM(shape, dtype) for shape, dtype in out_shapes]
    return pl.pallas_call(
        body,
        out_shape=outs,
        in_specs=[SMEM] + [VMEM] * (len(operands) - 1),
        out_specs=[VMEM] * len(outs),
        input_output_aliases=aliases or {},
        compiler_params=pltpu.CompilerParams(vmem_limit_bytes=16 << 20),
        cost_estimate=pl.CostEstimate(flops=1000, bytes_accessed=1000, transcendentals=0),
        name=name,
    )(*operands)


def column(ref, index, modes, here=slice(None)):
    return ref[here, pl.ds(pl.multiple_of(index * modes, modes), modes)]


def added(total, blocks, first, idx, shape_refs, here):
    for b, panel in enumerate(blocks):
        parts, lines, modes = panel.shape
        flat = panel[...].reshape(parts * lines, modes)
        term = nt(flat, column(shape_refs, idx[first + b], modes, here))
        total = term if total is None else total + term
    return total


def row_tiles(shape_refs):
    for g, table in enumerate(shape_refs):
        rows = table.shape[0]
        width = min(rows, 256)
        for r in range(0, rows, width):
            yield table, pl.ds(r, width), pl.ds(g * rows + r, width)


def spectra_body(first, count, carried, idx, own, other, *refs):
    blocks, out = refs[:count], refs[-1]
    parts, lines, _ = out.shape
    for table, here, there in row_tiles((own, other)):
        total = out[:, :, there].reshape(parts * lines, -1) if carried else None
        total = added(total, blocks, first, idx, table, here)
        out[:, :, there] = total.reshape(parts, lines, -1)


def add_spectra(blocks, first, idx, both, spectra):
    parts, lines, _ = blocks[0].shape
    operands = [idx, *both, *blocks]
    aliases = {}
    if spectra is not None:
        aliases = {len(operands): 0}
        operands.append(spectra)
    body = functools.partial(spectra_body, first, len(blocks), spectra is not None)
    shape = (parts, lines, 2 * both[0].shape[0])
    return on_chip(body, [(shape, F32)], operands, "add_spectra", aliases)[0]


def table_body(idx, harmonic, t_head, t_tail, weights):
    steps, both = t_head.shape
    lines = both // 2
    total_lines = harmonic.shape[1] * 2
    mine = harmonic[:, pl.ds(pl.multiple_of(idx[0] * lines, lines), lines)]
    ratios = mine.astype(F32) * (1.0 / HARM)
    squared = ratios * ratios
    ones = jnp.ones_like(ratios)
    rows = [ones, ratios, squared, squared * squared] * 2
    weights[...] = (jnp.concatenate(rows, axis=0) * (1.0 / total_lines)).T
    scale = math.sqrt(2.0 / total_lines)
    tile = 64
    for j in range(0, steps, tile):
        ids = lax.broadcasted_iota(jnp.int32, (tile, lines), 0) + j
        angles = ((ids * mine) & (HARM - 1)).astype(F32) * (2.0 * math.pi / HARM)
        here = slice(j, j + tile)
        for at, value in ((0, scale * jnp.cos(angles)), (lines, -scale * jnp.sin(angles))):
            head, tail = kernel_split(value)
            t_head[here, at : at + lines] = head
            t_tail[here, at : at + lines] = tail


def weights_body(first, idx, own, other, *refs):
    pairs, (w_head, w_tail, v_head, v_tail) = refs[:4], refs[4:]
    elems = pairs[0].shape[2]
    modes = v_head.shape[1] // 2
    rows = own.shape[0]
    slots = lax.broadcasted_iota(jnp.int32, (elems, rows), 1).astype(F32)
    for p, pair in enumerate(pairs):
        local, value = pair[0].T, pair[1].T
        weight = jnp.zeros((elems, rows), F32)
        for k in range(local.shape[1]):
            weight += jnp.where(local[:, k : k + 1] == slots, value[:, k : k + 1], 0.0)
        head, tail = kernel_split(weight)
        here = slice(p * elems, (p + 1) * elems)
        w_head[here, :] = head
        w_tail[here, :] = tail
    for g, table in enumerate((own, other)):
        here = slice(2 * g * elems, 2 * (g + 1) * elems)
        for b in range(2):
            part = column(table, idx[first + b], modes)
            head, tail = kernel_split(nn(w_head[here, :], part) + nn(w_tail[here, :], part))
            v_head[here, b * modes : (b + 1) * modes] = head
            v_tail[here, b * modes : (b + 1) * modes] = tail


def stress_body(idx, spectra, w_head, w_tail, t_head, t_tail, out):
    parts, lines, both = spectra.shape
    rows, elems = both // 2, out.shape[0] // 2
    for g in range(2):
        here = slice(g * elems, (g + 1) * elems)
        values = spectra[:, :, g * rows : (g + 1) * rows].reshape(parts * lines, rows)
        s_head, s_tail = kernel_split(values)
        w_h = w_head[here, :]
        picked = nt(w_h, s_head) + nt(w_h, s_tail) + nt(w_tail[here, :], s_head)
        p_head, p_tail = kernel_split(picked)
        t_h = t_head[...]
        out[here, :] = nt(p_head, t_h) + nt(p_tail, t_h) + nt(p_head, t_tail[...])


def last_body(idx, panel_a, panel_b, v_head, v_tail, t_head, t_tail, before, keep, give):
    total = before[...]
    for b, panel in enumerate((panel_a, panel_b)):
        parts, lines, modes = panel.shape
        here = slice(b * modes, (b + 1) * modes)
        flat = panel[...].reshape(parts * lines, modes)
        g_head, g_tail = kernel_split(nn(t_head[...], flat) + nn(t_tail[...], flat))
        head = v_head[:, here]
        total += nt(head, g_head) + nt(v_tail[:, here], g_head) + nt(head, g_tail)
    half = total.shape[0] // 2
    keep[...] = total[:half]
    give[...] = total[half:]


def moment_body(first, idx, own, other, panel_a, panel_b, spectra, weights, keep, give):
    parts, lines, _ = spectra.shape
    rows = own.shape[0]
    for table, here, there in row_tiles((own, other)):
        total = spectra[:, :, there].reshape(parts * lines, -1)
        total = added(total, (panel_a, panel_b), first, idx, table, here)
        total = total * total
        power = total[:lines] + total[lines:]
        sums = [jnp.sum(power * weights[:, k : k + 1], axis=0, keepdims=True) for k in range(4)]
        out = keep if there.start < rows else give
        out[:, here] = jnp.concatenate(sums + sums, axis=0)


def paired_shards(n_mode, panels, shapes, harmonic, connect, recovery, *, steps):
    tie = lax.optimization_barrier
    place = lax.axis_index("mode")
    core, side, layer = place % 2, place // 2 % 2, place // 4
    layers = n_mode // 4
    ring = lambda a: lax.ppermute(a, "mode", [(i, (i + 4) % n_mode) for i in range(n_mode)])
    across = lambda a: lax.ppermute(a, "mode", [(i, i ^ 2) for i in range(n_mode)])
    mate = lambda a: lax.ppermute(a, "mode", [(i, i ^ 1) for i in range(n_mode)])
    peer = lambda a: lax.ppermute(a, "node", [(0, 1), (1, 0)])

    parts, both_lines, modes = panels.shape
    lines = both_lines // 2
    rows = shapes.shape[0]
    elems = connect.shape[0]

    wanted = [(0, 0, 0), (0, 0, 1)]
    for s in range(layers - 1):
        for h in range(2):
            wanted += [(s, 1, h), (s + 1, 0, h)]
    wanted += [(layers - 1, 1, 0), (layers - 1, 1, 1)]
    back, flip, half = (jnp.array(column, dtype=jnp.int32) for column in zip(*wanted))
    index = (((layer - back) % layers) * 2 + (side + flip) % 2) * 2 + (core + half) % 2
    idx = jnp.concatenate([core[None], index]).astype(jnp.int32)
    last = len(wanted) - 1

    mine = lax.dynamic_slice(panels, (0, core * lines, 0), (parts, lines, modes))
    theirs = lax.dynamic_slice(panels, (0, (1 - core) * lines, 0), (parts, lines, modes))
    z = [[mine], [mate(theirs)]]
    x = [[], []]
    z[1][0], shapes_in = tie((z[1][0], shapes))
    both = (shapes, mate(shapes_in))

    def prepare(idx, harmonic, connect, recovery):
        table = [((steps, 2 * lines), BF16)] * 2 + [((lines, 8), F32)]
        *t, weights = on_chip(table_body, table, [idx, harmonic.reshape(1, -1)], "table")
        packed = jnp.stack([(connect - place * rows).astype(F32).T, recovery.T])
        across_node = peer(packed)
        pairs = [packed, across_node, mate(packed), mate(across_node)]
        return t, weights, pairs

    spectra = None
    at = 1
    for s in range(layers - 1):
        for h in range(2):
            moved, swapped = ring(z[h][-1]), across(z[h][-1])
            if s == 0 and h == 0:
                moved, swapped, idx, harmonic, connect, recovery = tie(
                    (moved, swapped, idx, harmonic, connect, recovery)
                )
                t, weights, pairs = prepare(idx, harmonic, connect, recovery)
                spectra = add_spectra([z[0][0], z[1][0]], at, idx, both, None)
                at += 2
            elif s == 1 and h == 0:
                moved, swapped, spectra, t, weights, pairs = tie(
                    (moved, swapped, spectra, t, weights, pairs)
                )
                shape = (4 * elems, rows), (4 * elems, 2 * modes)
                outs = [(shape[0], BF16)] * 2 + [(shape[1], BF16)] * 2
                body = functools.partial(weights_body, last)
                w_and_v = on_chip(body, outs, [idx, *both, *pairs], "weights")
            elif s == 2 and h == 0:
                moved, swapped, spectra, w_and_v = tie((moved, swapped, spectra, w_and_v))
            else:
                moved, swapped, spectra = tie((moved, swapped, spectra))
            z[h].append(moved)
            x[h].append(swapped)
            spectra = add_spectra([swapped, moved], at, idx, both, spectra)
            at += 2
    final = [across(z[0][-1]), ring(x[1][-1])]
    w, v = w_and_v[:2], w_and_v[2:]
    shape = (4 * elems, steps)
    (stress,) = on_chip(stress_body, [(shape, F32)], [idx, spectra, *w, *t], "first_stress")
    final[0], final[1], stress, spectra = tie((final[0], final[1], stress, spectra))
    part = [((2 * elems, steps), F32)] * 2
    keep, give = on_chip(last_body, part, [idx, *final, *v, *t, stress], "last_stress")
    give, spectra = tie((give, spectra))
    got = mate(give)
    part = [((8, rows), F32)] * 2
    body = functools.partial(moment_body, last)
    keep_m, give_m = on_chip(
        body, part, [idx, *both, *final, spectra, weights], "moments"
    )
    send = (keep[elems:] + got[elems:]).astype(BF16)
    half = keep_m + mate(give_m)
    stress = (keep[:elems] + got[:elems]) + peer(send).astype(F32)
    moments = half + peer(half)
    start = lax.axis_index("node") * (rows // 2)
    return stress, lax.dynamic_slice(moments, (0, start), (4, rows // 2))


def plain_shards(panels, shapes, harmonic, connect, recovery, *, steps, total_lines):
    highest = lax.Precision.HIGHEST
    rows_mode = shapes.shape[0]
    spectra = jnp.einsum(
        "cfm,rm->cfr",
        lax.all_gather(panels, "mode", axis=2, tiled=True),
        shapes,
        preferred_element_type=F32,
    )
    step_ids = jnp.arange(steps, dtype=jnp.int32)
    phases = harmonic[:, None] * step_ids[None, :] % HARM
    angles = phases.astype(F32) * (2.0 * math.pi / HARM)
    weights = moment_weights(harmonic, total_lines)
    history = jnp.einsum("fr,ft->rt", spectra[0], jnp.cos(angles), precision=highest)
    history = history - jnp.einsum("fr,ft->rt", spectra[1], jnp.sin(angles), precision=highest)
    power = spectra[0] * spectra[0] + spectra[1] * spectra[1]
    history = math.sqrt(2.0 / total_lines) * history
    moments = jnp.dot(weights, power, precision=highest)
    history = lax.psum_scatter(history, "node", scatter_dimension=0, tiled=True)
    moments = lax.psum_scatter(moments, "node", scatter_dimension=1, tiled=True)
    rows_in = lax.all_gather(history.astype(BF16), "node", axis=0, tiled=True)
    local = connect - lax.axis_index("mode") * rows_mode
    slots = jnp.arange(rows_mode, dtype=jnp.int32)
    hit = local[:, :, None] == slots[None, None, :]
    weight = jnp.sum(jnp.where(hit, recovery[:, :, None], 0.0), axis=1)
    stress = jnp.dot(weight, rows_in, preferred_element_type=F32, precision=highest)
    return stress, moments


STEPS = 512


def solution(mesh):
    n_mode, n_node = mesh.shape["mode"], mesh.shape["node"]

    def shards(panels, *rest):
        if n_node == 2 and n_mode % 4 == 0 and n_mode >= 8:
            return paired_shards(n_mode, panels, *rest, steps=STEPS)
        return plain_shards(panels, *rest, steps=STEPS, total_lines=panels.shape[1] * n_node)

    return jax.shard_map(
        shards,
        mesh=mesh,
        in_specs=(
            P(None, "node", "mode"),
            P("mode", None),
            P("node"),
            P(("mode", "node"), None),
            P(("mode", "node"), None),
        ),
        out_specs=(P(("mode", "node"), None), P(None, ("mode", "node"))),
        check_vma=False,
    )
```

time: 223 us -> 114 us (0.51)
  waiting for transfers between devices: 151 us -> 28.3 us
  Pallas kernels: 0 us -> 45 us
  matrix products: 44.4 us -> 0 us
  starting transfers between devices: 0.12 us -> 23.4 us
  between operations: 13.8 us -> 0.92 us
  local copies, waits for them, and re-layouts: 1.8 us -> 14.1 us
  blocking collectives: 8.73 us -> 0 us
    all_gather x1 -> x0, waiting for transfers between devices: 135 us -> none  [shards(): lax.all_gather(panels, 'mode', axis=2, tiled=True)]
    pallas_call x0 -> x12, Pallas kernels: none -> 45 us  [on_chip(): pl.pallas_call(body, out_shape=outs, in_specs=[SMEM] + [VMEM] * (len(oper...]
    dot_general x4 -> x0, matrix products: 40 us -> none  [the longest x1 14 us: time_rows(): history = jnp.einsum('fr,ft->rt', spectra[0], cos_table, precision=highest)]
    ppermute x0 -> x23, waiting for transfers between devices: none -> 28.3 us  [the longest x7 19.8 us: paired_shards(): lax.ppermute(a, 'mode', [(i, (i + 4) % n_mode) for i in range(n_mode)])]
    ppermute x0 -> x23, starting transfers between devices: none -> 23.4 us  [the longest x7 10.2 us: paired_shards(): lax.ppermute(a, 'mode', [(i, (i + 4) % n_mode) for i in range(n_mode)])]
    reduce_scatter x1 -> x0, waiting for transfers between devices: 16.1 us -> none  [shards(): lax.psum_scatter(history_part, 'node', scatter_dimension=0, tiled=True)]
    unnamed x10 -> x22, local copies, waits for them, and re-layouts: 1.7 us -> 12.8 us
    all_gather x1 -> x0, blocking collectives: 8.73 us -> none  [shards(): rows_in = lax.all_gather(histories, 'node', axis=0, tiled=True)]
  transfers between devices with their start and end apart: 3 -> 23, of which waited for: 2 -> 8; matrix products, arithmetic and copies ran while one was open for 8% -> 1% of each run, Pallas kernels for 0% -> 37%
where the time goes in v2:
time: 114 us
  Pallas kernels  45 us (39%)
  waiting for transfers between devices  28.3 us (25%)
  starting transfers between devices  23.4 us (21%)
  local copies, waits for them, and re-layouts  14.1 us (12%)
  other arithmetic  2.17 us (2%)
    pallas_call x12, Pallas kernels, on_chip(): pl.pallas_call(body, out_shape=outs, in_specs=[SMEM] + [VMEM] * (len(oper...  45 us
    ppermute x7, waiting for transfers between devices, paired_shards(): lax.ppermute(a, 'mode', [(i, (i + 4) % n_mode) for i in range(n_mode)])  19.8 us
    unnamed x22, local copies, waits for them, and re-layouts  12.8 us
    ppermute x7, starting transfers between devices, paired_shards(): lax.ppermute(a, 'mode', [(i, (i + 4) % n_mode) for i in range(n_mode)])  10.2 us
    ppermute x7, starting transfers between devices, paired_shards(): lax.ppermute(a, 'mode', [(i, i ^ 2) for i in range(n_mode)])  7.59 us
    ppermute x3, waiting for transfers between devices, paired_shards(): peer = lambda a: lax.ppermute(a, 'node', [(0, 1), (1, 0)])  5.64 us
    ppermute x3, starting transfers between devices, paired_shards(): peer = lambda a: lax.ppermute(a, 'node', [(0, 1), (1, 0)])  3.91 us
    ppermute x6, waiting for transfers between devices, paired_shards(): lax.ppermute(a, 'mode', [(i, i ^ 1) for i in range(n_mode)])  2.85 us
  transfers between devices with their start and end apart: 23, of which 8 were waited for; matrix products, arithmetic and copies ran while one was open for 1% of the time, Pallas kernels for 37%

profile of v2, /device:TPU:0, one launch (start us, length us, event | category | flops | bytes accessed | tf_op | source)
XLA Modules:
  0.0 113.8 jit_solution(13628602052755780012)
XLA Ops:
  2.5 1.7 %collective-permute-done.4.refs_1_ = bf16[2,512,256]{2,1,0:T(8,128)(2,1)} collective-permute-done((bf16[2,512,256]{2,1,0:T(8,128)(2,1)S(1)}, bf16[2,512,256]{2,1,0:T(8,128)(2,1)}, u32[]{:S(2)}, u32[]{:S(2)}) %collective-permute-start.4) | collective-permute-done | bytes 524320 | tf_op jit(solution)/shard_map/ppermute | solution.py:194
  4.5 2.7 %collective-permute-start = (bf16[2,512,256]{2,1,0:T(8,128)(2,1)S(1)}, bf16[2,512,256]{2,1,0:T(8,128)(2,1)S(1)}, u32[]{:S(2)}, u32[]{:S(2)}) collective-permute-start(bf16[2,512,256]{2,1,0:T(8,128)(2,1)S(1)} %get-tuple-element.105.refs_0_), channel_id=1, source_target_pairs={{0,8},{2,10},{4,12},{6,14},{8,16},{10,18},{12,20},{14,22},{16,24},... | collective-permute-start | bytes 1572872 | tf_op jit(solution)/shard_map/ppermute | solution.py:192
  8.7 1.6 %collective-permute-start.6 = (bf16[2,512,256]{2,1,0:T(8,128)(2,1)}, bf16[2,512,256]{2,1,0:T(8,128)(2,1)S(1)}, u32[]{:S(2)}, u32[]{:S(2)}) collective-permute-start(bf16[2,512,256]{2,1,0:T(8,128)(2,1)} %collective-permute-done.4.refs_1_), channel_id=1, source_target_pairs={{0,8},{2,10},{4,12},{6,14},{8,16},{10,18},{12,20},{14,22},{16,24},... | collective-permute-start | bytes 1572872 | tf_op jit(solution)/shard_map/ppermute | solution.py:192
  11.6 10.4 %collective-permute-done.refs_1_ = bf16[2,512,256]{2,1,0:T(8,128)(2,1)S(1)} collective-permute-done((bf16[2,512,256]{2,1,0:T(8,128)(2,1)S(1)}, bf16[2,512,256]{2,1,0:T(8,128)(2,1)S(1)}, u32[]{:S(2)}, u32[]{:S(2)}) %collective-permute-start) | collective-permute-done | bytes 524320 | tf_op jit(solution)/shard_map/ppermute | solution.py:192
  22.0 1.6 %collective-permute-start.2 = (bf16[2,512,256]{2,1,0:T(8,128)(2,1)S(1)}, bf16[2,512,256]{2,1,0:T(8,128)(2,1)S(1)}, u32[]{:S(2)}, u32[]{:S(2)}) collective-permute-start(bf16[2,512,256]{2,1,0:T(8,128)(2,1)S(1)} %collective-permute-done.refs_1_), channel_id=1, source_target_pairs={{0,8},{2,10},{4,12},{6,14},{8,16},{10,18},{12,20},{14,22},{16,24},... | collective-permute-start | bytes 1572872 | tf_op jit(solution)/shard_map/ppermute | solution.py:192
  25.1 2.2 %copy-done = bf16[512,4096]{1,0:T(8,128)(2,1)S(1)} copy-done((bf16[512,4096]{1,0:T(8,128)(2,1)S(1)}, bf16[512,4096]{1,0:T(8,128)(2,1)}, u32[]{:S(2)}) %copy-start) | copy-done | bytes 4194328
  27.3 3.6 %add_spectra.7.refs_2_ = f32[2,512,1024]{2,1,0:T(8,128)S(1)} custom-call(s32[17]{0:T(128)S(1)} %pad_add_fusion.idx, bf16[512,4096]{1,0:T(8,128)(2,1)S(1)} %copy-done, bf16[512,4096]{1,0:T(8,128)(2,1)} %collective-permute-done.5.other, bf16[2,512,256]{2,1,0:T(8,128)(2,1)S(1)} %get-tuple-element.105.refs_0_, bf16[2,512,256]{2,1,0:T(8,128)(2,1)} %collective-permute-done.4.refs_1_), custom_call_target="tpu_custom_call" | custom-call | flops 1000 | bytes 1000 | tf_op jit(solution)/shard_map/add_spectra/pallas_call | solution.py:46
  30.9 3.5 %add_spectra.8.refs_2_ = f32[2,512,1024]{2,1,0:T(8,128)S(1)} custom-call(s32[17]{0:T(128)S(1)} %pad_add_fusion.idx, bf16[512,4096]{1,0:T(8,128)(2,1)S(1)} %copy-done, bf16[512,4096]{1,0:T(8,128)(2,1)} %collective-permute-done.5.other, bf16[2,512,256]{2,1,0:T(8,128)(2,1)S(1)} %collective-permute-done.1.refs_0_, ...), custom_call_target="tpu_custom_call", output_to_operand_aliasing={{}: (5, {})} | custom-call | flops 1000 | bytes 1000 | tf_op jit(solution)/shard_map/add_spectra/pallas_call | solution.py:46
  34.4 2.0 %copy-done.3 = f32[2,512,1024]{2,1,0:T(8,128)} copy-done((f32[2,512,1024]{2,1,0:T(8,128)}, f32[2,512,1024]{2,1,0:T(8,128)S(1)}, u32[]{:S(2)}) %copy-start.3) | copy-done | bytes 4194328
  36.4 1.6 %collective-permute-start.13 = (bf16[2,512,256]{2,1,0:T(8,128)(2,1)S(1)}, bf16[2,512,256]{2,1,0:T(8,128)(2,1)S(1)}, u32[]{:S(2)}, u32[]{:S(2)}) collective-permute-start(bf16[2,512,256]{2,1,0:T(8,128)(2,1)S(1)} %collective-permute-done.6.refs_1_), channel_id=1, source_target_pairs={{0,8},{2,10},{4,12},{6,14},{8,16},{10,18},{12,20},{14,22},{16,24},... | collective-permute-start | bytes 1572872 | tf_op jit(solution)/shard_map/ppermute | solution.py:192
  38.6 1.6 %collective-permute-start.8 = (f32[2,8,128]{2,1,0:T(8,128)S(1)}, f32[2,8,128]{2,1,0:T(8,128)S(1)}, u32[]{:S(2)}, u32[]{:S(2)}) collective-permute-start(f32[2,8,128]{2,1,0:T(8,128)S(1)} %pad_maximum_fusion.refs_0_), channel_id=1, source_target_pairs={{0,1},{1,0},{2,3},{3,2},{4,5},{5,4},{6,7},{7,6},{8,9},{9,8},{10,11... | collective-permute-start | bytes 24584 | tf_op jit(solution)/shard_map/ppermute | solution.py:195
  40.2 2.1 %collective-permute-done.8.refs_1_ = f32[2,8,128]{2,1,0:T(8,128)S(1)} collective-permute-done((f32[2,8,128]{2,1,0:T(8,128)S(1)}, f32[2,8,128]{2,1,0:T(8,128)S(1)}, u32[]{:S(2)}, u32[]{:S(2)}) %collective-permute-start.8) | collective-permute-done | bytes 8224 | tf_op jit(solution)/shard_map/ppermute | solution.py:195
  43.7 5.1 %table.1 = (bf16[512,1024]{1,0:T(8,128)(2,1)S(1)}, bf16[512,1024]{1,0:T(8,128)(2,1)S(1)}, f32[512,8]{1,0:T(8,128)S(1)}) custom-call(s32[17]{0:T(128)S(1)} %pad_add_fusion.idx, s32[1,1024]{1,0:T(1,128)S(1)} %bitcast.9), custom_call_target="tpu_custom_call" | custom-call | flops 1000 | bytes 1000 | tf_op jit(solution)/shard_map/table/pallas_call | solution.py:46
  48.7 2.2 %copy-done.1 = bf16[512,4096]{1,0:T(8,128)(2,1)S(1)} copy-done((bf16[512,4096]{1,0:T(8,128)(2,1)S(1)}, bf16[512,4096]{1,0:T(8,128)(2,1)}, u32[]{:S(2)}) %copy-start.1) | copy-done | bytes 4194328
  50.9 2.2 %copy-done.4 = f32[2,512,1024]{2,1,0:T(8,128)S(1)} copy-done((f32[2,512,1024]{2,1,0:T(8,128)S(1)}, f32[2,512,1024]{2,1,0:T(8,128)}, u32[]{:S(2)}) %copy-start.4) | copy-done | bytes 4194328
  53.1 3.5 %add_spectra.9.refs_2_ = f32[2,512,1024]{2,1,0:T(8,128)S(1)} custom-call(s32[17]{0:T(128)S(1)} %pad_add_fusion.idx, bf16[512,4096]{1,0:T(8,128)(2,1)S(1)} %copy-done.1, bf16[512,4096]{1,0:T(8,128)(2,1)} %collective-permute-done.5.other, bf16[2,512,256]{2,1,0:T(8,128)(2,1)S(1)} %collective-permute-done.7.refs_0_, ...), custom_call_target="tpu_custom_call", output_to_operand_aliasing={{}: (5, {})} | custom-call | flops 1000 | bytes 1000 | tf_op jit(solution)/shard_map/add_spectra/pallas_call | solution.py:46
  56.8 1.6 %collective-permute-start.12 = (bf16[2,512,256]{2,1,0:T(8,128)(2,1)S(1)}, bf16[2,512,256]{2,1,0:T(8,128)(2,1)S(1)}, u32[]{:S(2)}, u32[]{:S(2)}) collective-permute-start(bf16[2,512,256]{2,1,0:T(8,128)(2,1)S(1)} %collective-permute-done.2.refs_1_), channel_id=1, source_target_pairs={{0,4},{2,6},{4,0},{6,2},{8,12},{10,14},{12,8},{14,10},{16,20},{18,... | collective-permute-start | bytes 1572872 | tf_op jit(solution)/shard_map/ppermute | solution.py:193
  58.4 3.6 %add_spectra.10.refs_2_ = f32[2,512,1024]{2,1,0:T(8,128)S(1)} custom-call(s32[17]{0:T(128)S(1)} %pad_add_fusion.idx, bf16[512,4096]{1,0:T(8,128)(2,1)S(1)} %copy-done.1, bf16[512,4096]{1,0:T(8,128)(2,1)} %collective-permute-done.5.other, bf16[2,512,256]{2,1,0:T(8,128)(2,1)} %collective-permute-done.3.refs_0_, ...), custom_call_target="tpu_custom_call", output_to_operand_aliasing={{}: (5, {})} | custom-call | flops 1000 | bytes 1000 | tf_op jit(solution)/shard_map/add_spectra/pallas_call | solution.py:46
  62.0 2.0 %collective-permute-start.16 = (bf16[2,512,256]{2,1,0:T(8,128)(2,1)S(1)}, bf16[2,512,256]{2,1,0:T(8,128)(2,1)S(1)}, u32[]{:S(2)}, u32[]{:S(2)}) collective-permute-start(bf16[2,512,256]{2,1,0:T(8,128)(2,1)S(1)} %collective-permute-done.13.refs_1_), channel_id=1, source_target_pairs={{0,8},{2,10},{4,12},{6,14},{8,16},{10,18},{12,20},{14,22},{16,24},... | collective-permute-start | bytes 1572872 | tf_op jit(solution)/shard_map/ppermute | solution.py:192
  64.4 4.4 %weights.1 = (bf16[512,512]{1,0:T(8,128)(2,1)S(1)}, bf16[512,512]{1,0:T(8,128)(2,1)S(1)}, bf16[512,512]{1,0:T(8,128)(2,1)S(1)}, bf16[512,512]{1,0:T(8,128)(2,1)S(1)}) custom-call(s32[17]{0:T(128)S(1)} %pad_add_fusion.idx, bf16[512,4096]{1,0:T(8,128)(2,1)S(1)} %copy-done.2, bf16[512,4096]{1,0:T(8,128)(2,1)} %collective-permute-done.5.other, ...), custom_call_target="tpu_custom_call" | custom-call | flops 1000 | bytes 1000 | tf_op jit(solution)/shard_map/weights/pallas_call | solution.py:46
  68.8 3.5 %add_spectra.11.refs_2_ = f32[2,512,1024]{2,1,0:T(8,128)S(1)} custom-call(s32[17]{0:T(128)S(1)} %pad_add_fusion.idx, bf16[512,4096]{1,0:T(8,128)(2,1)S(1)} %copy-done.2, bf16[512,4096]{1,0:T(8,128)(2,1)} %collective-permute-done.5.other, bf16[2,512,256]{2,1,0:T(8,128)(2,1)S(1)} %collective-permute-done.14.refs_0_, ...), custom_call_target="tpu_custom_call", output_to_operand_aliasing={{}: (5, {})} | custom-call | flops 1000 | bytes 1000 | tf_op jit(solution)/shard_map/add_spectra/pallas_call | solution.py:46
  74.7 3.5 %add_spectra.12.refs_2_ = f32[2,512,1024]{2,1,0:T(8,128)S(1)} custom-call(s32[17]{0:T(128)S(1)} %pad_add_fusion.idx, bf16[512,4096]{1,0:T(8,128)(2,1)S(1)} %copy-done.2, bf16[512,4096]{1,0:T(8,128)(2,1)} %collective-permute-done.5.other, bf16[2,512,256]{2,1,0:T(8,128)(2,1)S(1)} %collective-permute-done.12.refs_0_, ...), custom_call_target="tpu_custom_call", output_to_operand_aliasing={{}: (5, {})} | custom-call | flops 1000 | bytes 1000 | tf_op jit(solution)/shard_map/add_spectra/pallas_call | solution.py:46
  78.2 5.7 %collective-permute-done.16.refs_1_ = bf16[2,512,256]{2,1,0:T(8,128)(2,1)S(1)} collective-permute-done((bf16[2,512,256]{2,1,0:T(8,128)(2,1)S(1)}, bf16[2,512,256]{2,1,0:T(8,128)(2,1)S(1)}, u32[]{:S(2)}, u32[]{:S(2)}) %collective-permute-start.16) | collective-permute-done | bytes 524320 | tf_op jit(solution)/shard_map/ppermute | solution.py:192
  84.5 3.5 %add_spectra.13.spectra = f32[2,512,1024]{2,1,0:T(8,128)S(1)} custom-call(s32[17]{0:T(128)S(1)} %pad_add_fusion.idx, bf16[512,4096]{1,0:T(8,128)(2,1)S(1)} %copy-done.2, bf16[512,4096]{1,0:T(8,128)(2,1)} %collective-permute-done.5.other, bf16[2,512,256]{2,1,0:T(8,128)(2,1)S(1)} %collective-permute-done.17.refs_0_, ...), custom_call_target="tpu_custom_call", output_to_operand_aliasing={{}: (5, {})} | custom-call | flops 1000 | bytes 1000 | tf_op jit(solution)/shard_map/add_spectra/pallas_call | solution.py:46
  88.0 2.0 %copy-done.5 = f32[2,512,1024]{2,1,0:T(8,128)} copy-done((f32[2,512,1024]{2,1,0:T(8,128)}, f32[2,512,1024]{2,1,0:T(8,128)S(1)}, u32[]{:S(2)}) %copy-start.5) | copy-done | bytes 4194328
  90.1 2.2 %copy-done.6 = f32[2,512,1024]{2,1,0:T(8,128)S(1)} copy-done((f32[2,512,1024]{2,1,0:T(8,128)S(1)}, f32[2,512,1024]{2,1,0:T(8,128)}, u32[]{:S(2)}) %copy-start.6) | copy-done | bytes 4194328
  92.2 4.1 %first_stress.1.before = f32[512,512]{1,0:T(8,128)S(1)} custom-call(s32[17]{0:T(128)S(1)} %pad_add_fusion.idx, f32[2,512,1024]{2,1,0:T(8,128)S(1)} %copy-done.6, bf16[512,512]{1,0:T(8,128)(2,1)S(1)} %get-tuple-element.87.w_head, bf16[512,512]{1,0:T(8,128)(2,1)S(1)} %get-tuple-element.88.w_tail, bf16[512,1024]{1,0:T(8,128)(2,1)S(1)} %get-tuple-element.89.t_head, ...), custom_call_target="tpu_custom_call" | custom-call | flops 1000 | bytes 1000 | tf_op jit(solution)/shard_map/first_stress/pallas_call | solution.py:46
  96.3 2.8 %collective-permute-done.18.panel_b = bf16[2,512,256]{2,1,0:T(8,128)(2,1)S(1)} collective-permute-done((bf16[2,512,256]{2,1,0:T(8,128)(2,1)S(1)}, bf16[2,512,256]{2,1,0:T(8,128)(2,1)S(1)}, u32[]{:S(2)}, u32[]{:S(2)}) %collective-permute-start.18) | collective-permute-done | bytes 524320 | tf_op jit(solution)/shard_map/ppermute | solution.py:192
  99.1 2.7 %last_stress.1 = (f32[256,512]{1,0:T(8,128)S(1)}, f32[256,512]{1,0:T(8,128)S(1)}) custom-call(s32[17]{0:T(128)S(1)} %pad_add_fusion.idx, bf16[2,512,256]{2,1,0:T(8,128)(2,1)S(1)} %collective-permute-done.15.panel_a, bf16[2,512,256]{2,1,0:T(8,128)(2,1)S(1)} %collective-permute-done.18.panel_b, bf16[512,512]{1,0:T(8,128)(2,1)S(1)} %get-tuple-element.93.v_head, ...), custom_call_target="tpu_custom_call" | custom-call | flops 1000 | bytes 1000 | tf_op jit(solution)/shard_map/last_stress/pallas_call | solution.py:46
  101.9 4.2 %moments.1 = (f32[8,512]{1,0:T(8,128)S(1)}, f32[8,512]{1,0:T(8,128)S(1)}) custom-call(s32[17]{0:T(128)S(1)} %pad_add_fusion.idx, bf16[512,4096]{1,0:T(8,128)(2,1)S(1)} %copy-done.2, bf16[512,4096]{1,0:T(8,128)(2,1)} %collective-permute-done.5.other, bf16[2,512,256]{2,1,0:T(8,128)(2,1)S(1)} %collective-permute-done.15.panel_a, ...), custom_call_target="tpu_custom_call" | custom-call | flops 1000 | bytes 1000 | tf_op jit(solution)/shard_map/moments/pallas_call | solution.py:46
  106.6 1.6 %collective-permute-start.20 = (bf16[128,512]{1,0:T(8,128)(2,1)S(1)}, bf16[128,512]{1,0:T(8,128)(2,1)S(1)}, u32[]{:S(2)}, u32[]{:S(2)}) collective-permute-start(bf16[128,512]{1,0:T(8,128)(2,1)S(1)} %fusion), channel_id=1, source_target_pairs={{0,1},{1,0},{2,3},{3,2},{4,5},{5,4},{6,7},{7,6},{8,9},{9,8},{10,11... | collective-permute-start | bytes 393224 | tf_op jit(solution)/shard_map/ppermute | solution.py:195
  109.0 3.5 %collective-permute-done.22 = f32[8,512]{1,0:T(8,128)S(1)} collective-permute-done((f32[8,512]{1,0:T(8,128)S(1)}, f32[8,512]{1,0:T(8,128)S(1)}, u32[]{:S(2)}, u32[]{:S(2)}) %collective-permute-start.22) | collective-permute-done | bytes 16416 | tf_op jit(solution)/shard_map/ppermute | solution.py:195
  (57 shorter events, 14.7 us)
Async XLA Ops:
  1.9 2.2 %collective-permute-start.4 = (bf16[2,512,256]{2,1,0:T(8,128)(2,1)S(1)}, bf16[2,512,256]{2,1,0:T(8,128)(2,1)}, u32[]{:S(2)}, u32[]{:S(2)}) collective-permute-start(bf16[2,512,256]{2,1,0:T(8,128)(2,1)S(1)} %get-tuple-element.104), channel_id=1, source_target_pairs={{0,2},{2,0},{4,6},{6,4},{8,10},{10,8},{12,14},{14,12},{16,18},{18,... | collective-permute-start | bytes 1572872 | tf_op jit(solution)/shard_map/ppermute | solution.py:194
  4.1 20.9 %collective-permute-start.5 = (bf16[512,4096]{1,0:T(8,128)(2,1)}, bf16[512,4096]{1,0:T(8,128)(2,1)}, u32[]{:S(2)}, u32[]{:S(2)}) collective-permute-start(bf16[512,4096]{1,0:T(8,128)(2,1)} %own.17), channel_id=1, source_target_pairs={{0,2},{2,0},{4,6},{6,4},{8,10},{10,8},{12,14},{14,12},{16,18},{18,... | collective-permute-start | bytes 12582920 | tf_op jit(solution)/shard_map/ppermute | solution.py:194
  4.5 17.5 %collective-permute-start = (bf16[2,512,256]{2,1,0:T(8,128)(2,1)S(1)}, bf16[2,512,256]{2,1,0:T(8,128)(2,1)S(1)}, u32[]{:S(2)}, u32[]{:S(2)}) collective-permute-start(bf16[2,512,256]{2,1,0:T(8,128)(2,1)S(1)} %get-tuple-element.105.refs_0_), channel_id=1, source_target_pairs={{0,8},{2,10},{4,12},{6,14},{8,16},{10,18},{12,20},{14,22},{16,24},... | collective-permute-start | bytes 1572872 | tf_op jit(solution)/shard_map/ppermute | solution.py:192
  7.2 14.8 %collective-permute-start.1 = (bf16[2,512,256]{2,1,0:T(8,128)(2,1)S(1)}, bf16[2,512,256]{2,1,0:T(8,128)(2,1)S(1)}, u32[]{:S(2)}, u32[]{:S(2)}) collective-permute-start(bf16[2,512,256]{2,1,0:T(8,128)(2,1)S(1)} %get-tuple-element.105.refs_0_), channel_id=1, source_target_pairs={{0,4},{2,6},{4,0},{6,2},{8,12},{10,14},{12,8},{14,10},{16,20},{18,... | collective-permute-start | bytes 1572872 | tf_op jit(solution)/shard_map/ppermute | solution.py:193
  8.7 27.7 %collective-permute-start.6 = (bf16[2,512,256]{2,1,0:T(8,128)(2,1)}, bf16[2,512,256]{2,1,0:T(8,128)(2,1)S(1)}, u32[]{:S(2)}, u32[]{:S(2)}) collective-permute-start(bf16[2,512,256]{2,1,0:T(8,128)(2,1)} %collective-permute-done.4.refs_1_), channel_id=1, source_target_pairs={{0,8},{2,10},{4,12},{6,14},{8,16},{10,18},{12,20},{14,22},{16,24},... | collective-permute-start | bytes 1572872 | tf_op jit(solution)/shard_map/ppermute | solution.py:192
  10.3 26.2 %collective-permute-start.7 = (bf16[2,512,256]{2,1,0:T(8,128)(2,1)}, bf16[2,512,256]{2,1,0:T(8,128)(2,1)S(1)}, u32[]{:S(2)}, u32[]{:S(2)}) collective-permute-start(bf16[2,512,256]{2,1,0:T(8,128)(2,1)} %collective-permute-done.4.refs_1_), channel_id=1, source_target_pairs={{0,4},{2,6},{4,0},{6,2},{8,12},{10,14},{12,8},{14,10},{16,20},{18,... | collective-permute-start | bytes 1572872 | tf_op jit(solution)/shard_map/ppermute | solution.py:193
  22.0 34.6 %collective-permute-start.2 = (bf16[2,512,256]{2,1,0:T(8,128)(2,1)S(1)}, bf16[2,512,256]{2,1,0:T(8,128)(2,1)S(1)}, u32[]{:S(2)}, u32[]{:S(2)}) collective-permute-start(bf16[2,512,256]{2,1,0:T(8,128)(2,1)S(1)} %collective-permute-done.refs_1_), channel_id=1, source_target_pairs={{0,8},{2,10},{4,12},{6,14},{8,16},{10,18},{12,20},{14,22},{16,24},... | collective-permute-start | bytes 1572872 | tf_op jit(solution)/shard_map/ppermute | solution.py:192
  23.6 33.1 %collective-permute-start.3 = (bf16[2,512,256]{2,1,0:T(8,128)(2,1)S(1)}, bf16[2,512,256]{2,1,0:T(8,128)(2,1)}, u32[]{:S(2)}, u32[]{:S(2)}) collective-permute-start(bf16[2,512,256]{2,1,0:T(8,128)(2,1)S(1)} %collective-permute-done.refs_1_), channel_id=1, source_target_pairs={{0,4},{2,6},{4,0},{6,2},{8,12},{10,14},{12,8},{14,10},{16,20},{18,... | collective-permute-start | bytes 1572872 | tf_op jit(solution)/shard_map/ppermute | solution.py:193
  25.1 2.2 %copy-start = (bf16[512,4096]{1,0:T(8,128)(2,1)S(1)}, bf16[512,4096]{1,0:T(8,128)(2,1)}, u32[]{:S(2)}) copy-start(bf16[512,4096]{1,0:T(8,128)(2,1)} %own.17) | copy-start | bytes 12582916
  30.9 7.7 %copy-start.9 = (s32[128,8]{0,1:T(8,128)S(1)}, s32[128,8]{0,1:T(8,128)}, u32[]{:S(2)}) copy-start(s32[128,8]{0,1:T(8,128)} %param.11) | copy-start | bytes 12292
  30.9 7.7 %copy-start.10 = (f32[128,8]{0,1:T(8,128)S(1)}, f32[128,8]{0,1:T(8,128)}, u32[]{:S(2)}) copy-start(f32[128,8]{0,1:T(8,128)} %param.12) | copy-start | bytes 12292
  30.9 12.8 %copy-start.8 = (s32[1024]{0:T(1024)S(1)}, s32[1024]{0:T(1024)}, u32[]{:S(2)}) copy-start(s32[1024]{0:T(1024)} %param.10) | copy-start | bytes 12292
  36.4 25.6 %collective-permute-start.13 = (bf16[2,512,256]{2,1,0:T(8,128)(2,1)S(1)}, bf16[2,512,256]{2,1,0:T(8,128)(2,1)S(1)}, u32[]{:S(2)}, u32[]{:S(2)}) collective-permute-start(bf16[2,512,256]{2,1,0:T(8,128)(2,1)S(1)} %collective-permute-done.6.refs_1_), channel_id=1, source_target_pairs={{0,8},{2,10},{4,12},{6,14},{8,16},{10,18},{12,20},{14,22},{16,24},... | collective-permute-start | bytes 1572872 | tf_op jit(solution)/shard_map/ppermute | solution.py:192
  38.0 24.0 %collective-permute-start.14 = (bf16[2,512,256]{2,1,0:T(8,128)(2,1)S(1)}, bf16[2,512,256]{2,1,0:T(8,128)(2,1)S(1)}, u32[]{:S(2)}, u32[]{:S(2)}) collective-permute-start(bf16[2,512,256]{2,1,0:T(8,128)(2,1)S(1)} %collective-permute-done.6.refs_1_), channel_id=1, source_target_pairs={{0,4},{2,6},{4,0},{6,2},{8,12},{10,14},{12,8},{14,10},{16,20},{18,... | collective-permute-start | bytes 1572872 | tf_op jit(solution)/shard_map/ppermute | solution.py:193
  38.6 3.7 %collective-permute-start.8 = (f32[2,8,128]{2,1,0:T(8,128)S(1)}, f32[2,8,128]{2,1,0:T(8,128)S(1)}, u32[]{:S(2)}, u32[]{:S(2)}) collective-permute-start(f32[2,8,128]{2,1,0:T(8,128)S(1)} %pad_maximum_fusion.refs_0_), channel_id=1, source_target_pairs={{0,1},{1,0},{2,3},{3,2},{4,5},{5,4},{6,7},{7,6},{8,9},{9,8},{10,11... | collective-permute-start | bytes 24584 | tf_op jit(solution)/shard_map/ppermute | solution.py:195
  42.3 1.2 %collective-permute-start.9 = (f32[2,8,128]{2,1,0:T(8,128)S(1)}, f32[2,8,128]{2,1,0:T(8,128)S(1)}, u32[]{:S(2)}, u32[]{:S(2)}) collective-permute-start(f32[2,8,128]{2,1,0:T(8,128)S(1)} %pad_maximum_fusion.refs_0_), channel_id=1, source_target_pairs={{0,2},{2,0},{4,6},{6,4},{8,10},{10,8},{12,14},{14,12},{16,18},{18,... | collective-permute-start | bytes 24584 | tf_op jit(solution)/shard_map/ppermute | solution.py:194
  43.5 13.1 %collective-permute-start.10 = (f32[2,8,128]{2,1,0:T(8,128)S(1)}, f32[2,8,128]{2,1,0:T(8,128)S(1)}, u32[]{:S(2)}, u32[]{:S(2)}) collective-permute-start(f32[2,8,128]{2,1,0:T(8,128)S(1)} %collective-permute-done.8.refs_1_), channel_id=1, source_target_pairs={{0,2},{2,0},{4,6},{6,4},{8,10},{10,8},{12,14},{14,12},{16,18},{18,... | collective-permute-start | bytes 24584 | tf_op jit(solution)/shard_map/ppermute | solution.py:194
  48.7 2.2 %copy-start.1 = (bf16[512,4096]{1,0:T(8,128)(2,1)S(1)}, bf16[512,4096]{1,0:T(8,128)(2,1)}, u32[]{:S(2)}) copy-start(bf16[512,4096]{1,0:T(8,128)(2,1)} %own.17) | copy-start | bytes 12582916
  50.9 2.2 %copy-start.4 = (f32[2,512,1024]{2,1,0:T(8,128)S(1)}, f32[2,512,1024]{2,1,0:T(8,128)}, u32[]{:S(2)}) copy-start(f32[2,512,1024]{2,1,0:T(8,128)} %copy-done.3) | copy-start | bytes 12582916
  56.6 7.8 %copy-start.2 = (bf16[512,4096]{1,0:T(8,128)(2,1)S(1)}, bf16[512,4096]{1,0:T(8,128)(2,1)}, u32[]{:S(2)}) copy-start(bf16[512,4096]{1,0:T(8,128)(2,1)} %own.17) | copy-start | bytes 12582916
  56.7 16.6 %collective-permute-start.11 = (bf16[2,512,256]{2,1,0:T(8,128)(2,1)S(1)}, bf16[2,512,256]{2,1,0:T(8,128)(2,1)S(1)}, u32[]{:S(2)}, u32[]{:S(2)}) collective-permute-start(bf16[2,512,256]{2,1,0:T(8,128)(2,1)S(1)} %collective-permute-done.2.refs_1_), channel_id=1, source_target_pairs={{0,8},{2,10},{4,12},{6,14},{8,16},{10,18},{12,20},{14,22},{16,24},... | collective-permute-start | bytes 1572872 | tf_op jit(solution)/shard_map/ppermute | solution.py:192
  56.8 16.5 %collective-permute-start.12 = (bf16[2,512,256]{2,1,0:T(8,128)(2,1)S(1)}, bf16[2,512,256]{2,1,0:T(8,128)(2,1)S(1)}, u32[]{:S(2)}, u32[]{:S(2)}) collective-permute-start(bf16[2,512,256]{2,1,0:T(8,128)(2,1)S(1)} %collective-permute-done.2.refs_1_), channel_id=1, source_target_pairs={{0,4},{2,6},{4,0},{6,2},{8,12},{10,14},{12,8},{14,10},{16,20},{18,... | collective-permute-start | bytes 1572872 | tf_op jit(solution)/shard_map/ppermute | solution.py:193
  62.0 21.9 %collective-permute-start.16 = (bf16[2,512,256]{2,1,0:T(8,128)(2,1)S(1)}, bf16[2,512,256]{2,1,0:T(8,128)(2,1)S(1)}, u32[]{:S(2)}, u32[]{:S(2)}) collective-permute-start(bf16[2,512,256]{2,1,0:T(8,128)(2,1)S(1)} %collective-permute-done.13.refs_1_), channel_id=1, source_target_pairs={{0,8},{2,10},{4,12},{6,14},{8,16},{10,18},{12,20},{14,22},{16,24},... | collective-permute-start | bytes 1572872 | tf_op jit(solution)/shard_map/ppermute | solution.py:192
  64.0 19.9 %collective-permute-start.17 = (bf16[2,512,256]{2,1,0:T(8,128)(2,1)S(1)}, bf16[2,512,256]{2,1,0:T(8,128)(2,1)S(1)}, u32[]{:S(2)}, u32[]{:S(2)}) collective-permute-start(bf16[2,512,256]{2,1,0:T(8,128)(2,1)S(1)} %collective-permute-done.13.refs_1_), channel_id=1, source_target_pairs={{0,4},{2,6},{4,0},{6,2},{8,12},{10,14},{12,8},{14,10},{16,20},{18,... | collective-permute-start | bytes 1572872 | tf_op jit(solution)/shard_map/ppermute | solution.py:193
  73.2 23.1 %collective-permute-start.15 = (bf16[2,512,256]{2,1,0:T(8,128)(2,1)S(1)}, bf16[2,512,256]{2,1,0:T(8,128)(2,1)S(1)}, u32[]{:S(2)}, u32[]{:S(2)}) collective-permute-start(bf16[2,512,256]{2,1,0:T(8,128)(2,1)S(1)} %collective-permute-done.11.refs_1_), channel_id=1, source_target_pairs={{0,4},{2,6},{4,0},{6,2},{8,12},{10,14},{12,8},{14,10},{16,20},{18,... | collective-permute-start | bytes 1572872 | tf_op jit(solution)/shard_map/ppermute | solution.py:193
  83.9 15.2 %collective-permute-start.18 = (bf16[2,512,256]{2,1,0:T(8,128)(2,1)S(1)}, bf16[2,512,256]{2,1,0:T(8,128)(2,1)S(1)}, u32[]{:S(2)}, u32[]{:S(2)}) collective-permute-start(bf16[2,512,256]{2,1,0:T(8,128)(2,1)S(1)} %collective-permute-done.17.refs_0_), channel_id=1, source_target_pairs={{0,8},{2,10},{4,12},{6,14},{8,16},{10,18},{12,20},{14,22},{16,24},... | collective-permute-start | bytes 1572872 | tf_op jit(solution)/shard_map/ppermute | solution.py:192
  90.1 2.2 %copy-start.6 = (f32[2,512,1024]{2,1,0:T(8,128)S(1)}, f32[2,512,1024]{2,1,0:T(8,128)}, u32[]{:S(2)}) copy-start(f32[2,512,1024]{2,1,0:T(8,128)} %copy-done.5) | copy-start | bytes 12582916
  96.3 5.6 %copy-start.7 = (f32[2,512,1024]{2,1,0:T(8,128)S(1)}, f32[2,512,1024]{2,1,0:T(8,128)}, u32[]{:S(2)}) copy-start(f32[2,512,1024]{2,1,0:T(8,128)} %copy-done.5) | copy-start | bytes 12582916
  101.8 4.8 %collective-permute-start.19 = (f32[256,512]{1,0:T(8,128)S(1)}, f32[256,512]{1,0:T(8,128)S(1)}, u32[]{:S(2)}, u32[]{:S(2)}) collective-permute-start(f32[256,512]{1,0:T(8,128)S(1)} %get-tuple-element.99), channel_id=1, source_target_pairs={{0,2},{2,0},{4,6},{6,4},{8,10},{10,8},{12,14},{14,12},{16,18},{18,... | collective-permute-start | bytes 1572872 | tf_op jit(solution)/shard_map/ppermute | solution.py:194
  106.0 2.2 %collective-permute-start.21 = (f32[8,512]{1,0:T(8,128)S(1)}, f32[8,512]{1,0:T(8,128)S(1)}, u32[]{:S(2)}, u32[]{:S(2)}) collective-permute-start(f32[8,512]{1,0:T(8,128)S(1)} %get-tuple-element.103), channel_id=1, source_target_pairs={{0,2},{2,0},{4,6},{6,4},{8,10},{10,8},{12,14},{14,12},{16,18},{18,... | collective-permute-start | bytes 49160 | tf_op jit(solution)/shard_map/ppermute | solution.py:194
  106.6 6.4 %collective-permute-start.20 = (bf16[128,512]{1,0:T(8,128)(2,1)S(1)}, bf16[128,512]{1,0:T(8,128)(2,1)S(1)}, u32[]{:S(2)}, u32[]{:S(2)}) collective-permute-start(bf16[128,512]{1,0:T(8,128)(2,1)S(1)} %fusion), channel_id=1, source_target_pairs={{0,1},{1,0},{2,3},{3,2},{4,5},{5,4},{6,7},{7,6},{8,9},{9,8},{10,11... | collective-permute-start | bytes 393224 | tf_op jit(solution)/shard_map/ppermute | solution.py:195
  108.2 4.2 %collective-permute-start.22 = (f32[8,512]{1,0:T(8,128)S(1)}, f32[8,512]{1,0:T(8,128)S(1)}, u32[]{:S(2)}, u32[]{:S(2)}) collective-permute-start(f32[8,512]{1,0:T(8,128)S(1)} %add.81), channel_id=1, source_target_pairs={{0,1},{1,0},{2,3},{3,2},{4,5},{5,4},{6,7},{7,6},{8,9},{9,8},{10,11... | collective-permute-start | bytes 49160 | tf_op jit(solution)/shard_map/ppermute | solution.py:195
  (2 other events, 4.0 us)

commit v3 on v2

--- a/solution.py
+++ b/solution.py
@@ -39,62 +39,89 @@
 
 VMEM = pl.BlockSpec(memory_space=pltpu.VMEM)
 SMEM = pl.BlockSpec(memory_space=pltpu.SMEM)
-
-
-def on_chip(body, out_shapes, operands, name, aliases=None):
+HBM = pl.BlockSpec(memory_space=pltpu.HBM)
+
+
+def on_chip(
+    body, out_shapes, idx, operands, name, both=(), columns=0, modes=0, aliases=None, keep_columns=False
+):
     outs = [pltpu.VMEM(shape, dtype) for shape, dtype in out_shapes]
+    scratch = []
+    if both:
+        rows = both[0].shape[0]
+        scratch = [pltpu.SemaphoreType.DMA((2, columns))]
+        if not keep_columns:
+            scratch.insert(0, pltpu.VMEM((2, columns, rows, modes), BF16))
+    aliases = {1 + len(both) + i: o for i, o in (aliases or {}).items()}
     return pl.pallas_call(
         body,
         out_shape=outs,
-        in_specs=[SMEM] + [VMEM] * (len(operands) - 1),
+        in_specs=[SMEM] + [HBM] * len(both) + [VMEM] * len(operands),
         out_specs=[VMEM] * len(outs),
-        input_output_aliases=aliases or {},
+        scratch_shapes=scratch,
+        input_output_aliases=aliases,
         compiler_params=pltpu.CompilerParams(vmem_limit_bytes=16 << 20),
         cost_estimate=pl.CostEstimate(flops=1000, bytes_accessed=1000, transcendentals=0),
         name=name,
-    )(*operands)
-
-
-def column(ref, index, modes, here=slice(None)):
-    return ref[here, pl.ds(pl.multiple_of(index * modes, modes), modes)]
-
-
-def added(total, blocks, first, idx, shape_refs, here):
-    for b, panel in enumerate(blocks):
-        parts, lines, modes = panel.shape
-        flat = panel[...].reshape(parts * lines, modes)
-        term = nt(flat, column(shape_refs, idx[first + b], modes, here))
-        total = term if total is None else total + term
-    return total
-
-
-def row_tiles(shape_refs):
-    for g, table in enumerate(shape_refs):
-        rows = table.shape[0]
-        width = min(rows, 256)
+    )(idx, *both, *operands)
+
+
+def pinned(value):
+    return pltpu.with_memory_space_constraint(value, pltpu.VMEM)
+
+
+def fetch(idx, first, both, buffer, sems):
+    _, columns, _, modes = buffer.shape
+    copies = {}
+    for g, table in enumerate(both):
+        for b in range(columns):
+            at = pl.ds(pl.multiple_of(idx[first + b] * modes, modes), modes)
+            copies[g, b] = pltpu.make_async_copy(table.at[:, at], buffer.at[g, b], sems.at[g, b])
+    for copy in copies.values():
+        copy.start()
+    return copies
+
+
+def row_tiles(rows):
+    width = min(rows, 256)
+    for g in range(2):
         for r in range(0, rows, width):
-            yield table, pl.ds(r, width), pl.ds(g * rows + r, width)
+            yield g, pl.ds(r, width), pl.ds(g * rows + r, width)
+
+
+def flat(panel):
+    if isinstance(panel, tuple):
+        return jnp.concatenate([part[0] for part in panel], axis=0)
+    return panel[...].reshape(-1, panel.shape[2])
 
 
 def spectra_body(first, count, carried, idx, own, other, *refs):
-    blocks, out = refs[:count], refs[-1]
+    blocks, (out, buffer, sems) = refs[:count], refs[-3:]
     parts, lines, _ = out.shape
-    for table, here, there in row_tiles((own, other)):
+    copies = fetch(idx, first, (own, other), buffer, sems)
+    for g, here, there in row_tiles(own.shape[0]):
+        if here.start == 0:
+            for b in range(count):
+                copies[g, b].wait()
         total = out[:, :, there].reshape(parts * lines, -1) if carried else None
-        total = added(total, blocks, first, idx, table, here)
+        for b, panel in enumerate(blocks):
+            term = nt(flat(panel), buffer[g, b, here, :])
+            total = term if total is None else total + term
         out[:, :, there] = total.reshape(parts, lines, -1)
 
 
 def add_spectra(blocks, first, idx, both, spectra):
-    parts, lines, _ = blocks[0].shape
-    operands = [idx, *both, *blocks]
-    aliases = {}
+    parts, lines, modes = blocks[0].shape
+    count = len(blocks)
+    operands, aliases = list(blocks), {}
     if spectra is not None:
-        aliases = {len(operands): 0}
-        operands.append(spectra)
-    body = functools.partial(spectra_body, first, len(blocks), spectra is not None)
+        aliases = {count: 0}
+        operands.append(pinned(spectra))
+    body = functools.partial(spectra_body, first, count, spectra is not None)
     shape = (parts, lines, 2 * both[0].shape[0])
-    return on_chip(body, [(shape, F32)], operands, "add_spectra", aliases)[0]
+    return on_chip(
+        body, [(shape, F32)], idx, operands, "add_spectra", both, count, modes, aliases
+    )[0]
 
 
 def table_body(idx, harmonic, t_head, t_tail, weights):
@@ -120,13 +147,14 @@
 
 
 def weights_body(first, idx, own, other, *refs):
-    pairs, (w_head, w_tail, v_head, v_tail) = refs[:4], refs[4:]
+    pairs, (w_head, w_tail, v_head, v_tail, buffer, sems) = refs[:4], refs[4:]
+    copies = fetch(idx, first, (own, other), buffer, sems)
     elems = pairs[0].shape[2]
     modes = v_head.shape[1] // 2
     rows = own.shape[0]
     slots = lax.broadcasted_iota(jnp.int32, (elems, rows), 1).astype(F32)
     for p, pair in enumerate(pairs):
-        local, value = pair[0].T, pair[1].T
+        local, value = (pair[0] - idx[1 + p // 2].astype(F32)).T, pair[1].T
         weight = jnp.zeros((elems, rows), F32)
         for k in range(local.shape[1]):
             weight += jnp.where(local[:, k : k + 1] == slots, value[:, k : k + 1], 0.0)
@@ -134,10 +162,11 @@
         here = slice(p * elems, (p + 1) * elems)
         w_head[here, :] = head
         w_tail[here, :] = tail
-    for g, table in enumerate((own, other)):
+    for g in range(2):
         here = slice(2 * g * elems, 2 * (g + 1) * elems)
         for b in range(2):
-            part = column(table, idx[first + b], modes)
+            copies[g, b].wait()
+            part = buffer[g, b]
             head, tail = kernel_split(nn(w_head[here, :], part) + nn(w_tail[here, :], part))
             v_head[here, b * modes : (b + 1) * modes] = head
             v_tail[here, b * modes : (b + 1) * modes] = tail
@@ -157,31 +186,40 @@
         out[here, :] = nt(p_head, t_h) + nt(p_tail, t_h) + nt(p_head, t_tail[...])
 
 
-def last_body(idx, panel_a, panel_b, v_head, v_tail, t_head, t_tail, before, keep, give):
-    total = before[...]
-    for b, panel in enumerate((panel_a, panel_b)):
-        parts, lines, modes = panel.shape
-        here = slice(b * modes, (b + 1) * modes)
-        flat = panel[...].reshape(parts * lines, modes)
-        g_head, g_tail = kernel_split(nn(t_head[...], flat) + nn(t_tail[...], flat))
-        head = v_head[:, here]
-        total += nt(head, g_head) + nt(v_tail[:, here], g_head) + nt(head, g_tail)
+def time_term(panel, v_head, v_tail, t_head, t_tail):
+    g_head, g_tail = kernel_split(nn(t_head[...], panel) + nn(t_tail[...], panel))
+    return nt(v_head, g_head) + nt(v_tail, g_head) + nt(v_head, g_tail)
+
+
+def half_body(idx, real, imag, v_head, v_tail, columns, t_head, t_tail, spectra, stress, spectra_out, stress_out):
+    parts, lines, _ = spectra.shape
+    panel = flat((real, imag))
+    modes = panel.shape[1]
+    for g, here, there in row_tiles(columns.shape[2]):
+        total = spectra[:, :, there].reshape(parts * lines, -1) + nt(panel, columns[g, 0, here, :])
+        spectra_out[:, :, there] = total.reshape(parts, lines, -1)
+    term = time_term(panel, v_head[:, :modes], v_tail[:, :modes], t_head, t_tail)
+    stress_out[...] = stress[...] + term
+
+
+def last_body(idx, real, imag, v_head, v_tail, t_head, t_tail, before, keep, give):
+    panel = flat((real, imag))
+    modes = panel.shape[1]
+    total = before[...] + time_term(panel, v_head[:, modes:], v_tail[:, modes:], t_head, t_tail)
     half = total.shape[0] // 2
     keep[...] = total[:half]
     give[...] = total[half:]
 
 
-def moment_body(first, idx, own, other, panel_a, panel_b, spectra, weights, keep, give):
+def moment_body(idx, real, imag, columns, spectra, weights, keep, give):
     parts, lines, _ = spectra.shape
-    rows = own.shape[0]
-    for table, here, there in row_tiles((own, other)):
-        total = spectra[:, :, there].reshape(parts * lines, -1)
-        total = added(total, (panel_a, panel_b), first, idx, table, here)
+    panel = flat((real, imag))
+    for g, here, there in row_tiles(columns.shape[2]):
+        total = spectra[:, :, there].reshape(parts * lines, -1) + nt(panel, columns[g, 1, here, :])
         total = total * total
         power = total[:lines] + total[lines:]
         sums = [jnp.sum(power * weights[:, k : k + 1], axis=0, keepdims=True) for k in range(4)]
-        out = keep if there.start < rows else give
-        out[:, here] = jnp.concatenate(sums + sums, axis=0)
+        (give if g else keep)[:, here] = jnp.concatenate(sums + sums, axis=0)
 
 
 def paired_shards(n_mode, panels, shapes, harmonic, connect, recovery, *, steps):
@@ -206,44 +244,42 @@
     wanted += [(layers - 1, 1, 0), (layers - 1, 1, 1)]
     back, flip, half = (jnp.array(column, dtype=jnp.int32) for column in zip(*wanted))
     index = (((layer - back) % layers) * 2 + (side + flip) % 2) * 2 + (core + half) % 2
-    idx = jnp.concatenate([core[None], index]).astype(jnp.int32)
-    last = len(wanted) - 1
+    bases = jnp.stack([core, place * rows, (place + 1 - 2 * core) * rows])
+    last = len(wanted) + 1
 
     mine = lax.dynamic_slice(panels, (0, core * lines, 0), (parts, lines, modes))
     theirs = lax.dynamic_slice(panels, (0, (1 - core) * lines, 0), (parts, lines, modes))
     z = [[mine], [mate(theirs)]]
     x = [[], []]
-    z[1][0], shapes_in = tie((z[1][0], shapes))
+    z[1][0], shapes_in, index, bases, harmonic, connect, recovery = tie(
+        (z[1][0], shapes, index, bases, harmonic, connect, recovery)
+    )
+    idx = jnp.concatenate([bases, index]).astype(jnp.int32)
+    packed = jnp.stack([connect.astype(F32).T, recovery.T])
     both = (shapes, mate(shapes_in))
-
-    def prepare(idx, harmonic, connect, recovery):
-        table = [((steps, 2 * lines), BF16)] * 2 + [((lines, 8), F32)]
-        *t, weights = on_chip(table_body, table, [idx, harmonic.reshape(1, -1)], "table")
-        packed = jnp.stack([(connect - place * rows).astype(F32).T, recovery.T])
-        across_node = peer(packed)
-        pairs = [packed, across_node, mate(packed), mate(across_node)]
-        return t, weights, pairs
-
+    out = [((steps, 2 * lines), BF16)] * 2 + [((lines, 8), F32)]
+    *t, weights = on_chip(table_body, out, idx, [harmonic.reshape(1, -1)], "table")
+    across_node = peer(packed)
+    pairs = [packed, across_node, mate(packed)]
+    z[1][0], t, weights, pairs = tie((z[1][0], t, weights, pairs))
+    pairs.append(mate(pairs[1]))
     spectra = None
-    at = 1
+    at = 3
     for s in range(layers - 1):
         for h in range(2):
             moved, swapped = ring(z[h][-1]), across(z[h][-1])
             if s == 0 and h == 0:
-                moved, swapped, idx, harmonic, connect, recovery = tie(
-                    (moved, swapped, idx, harmonic, connect, recovery)
-                )
-                t, weights, pairs = prepare(idx, harmonic, connect, recovery)
+                moved, swapped = tie((moved, swapped))
                 spectra = add_spectra([z[0][0], z[1][0]], at, idx, both, None)
                 at += 2
             elif s == 1 and h == 0:
-                moved, swapped, spectra, t, weights, pairs = tie(
-                    (moved, swapped, spectra, t, weights, pairs)
+                moved, swapped, spectra, pairs = tie((moved, swapped, spectra, pairs))
+                out = [((4 * elems, rows), BF16)] * 2 + [((4 * elems, 2 * modes), BF16)] * 2
+                out.append(((2, 2, rows, modes), BF16))
+                body = functools.partial(weights_body, last)
+                w_and_v = on_chip(
+                    body, out, idx, pairs, "weights", both, 2, modes, keep_columns=True
                 )
-                shape = (4 * elems, rows), (4 * elems, 2 * modes)
-                outs = [(shape[0], BF16)] * 2 + [(shape[1], BF16)] * 2
-                body = functools.partial(weights_body, last)
-                w_and_v = on_chip(body, outs, [idx, *both, *pairs], "weights")
             elif s == 2 and h == 0:
                 moved, swapped, spectra, w_and_v = tie((moved, swapped, spectra, w_and_v))
             else:
@@ -252,20 +288,23 @@
             x[h].append(swapped)
             spectra = add_spectra([swapped, moved], at, idx, both, spectra)
             at += 2
-    final = [across(z[0][-1]), ring(x[1][-1])]
-    w, v = w_and_v[:2], w_and_v[2:]
-    shape = (4 * elems, steps)
-    (stress,) = on_chip(stress_body, [(shape, F32)], [idx, spectra, *w, *t], "first_stress")
-    final[0], final[1], stress, spectra = tie((final[0], final[1], stress, spectra))
-    part = [((2 * elems, steps), F32)] * 2
-    keep, give = on_chip(last_body, part, [idx, *final, *v, *t, stress], "last_stress")
+    ends = [(across(z[h][-1][:1]), ring(x[h][-1][1:])) for h in range(2)]
+    w, v, columns = [pinned(a) for a in w_and_v[:2]], [pinned(a) for a in w_and_v[2:4]], pinned(w_and_v[4])
+    t = [pinned(a) for a in t]
+    out = [((4 * elems, steps), F32)]
+    (stress,) = on_chip(stress_body, out, idx, [pinned(spectra), *w, *t], "first_stress")
+    ends[0], stress, spectra = tie((ends[0], stress, spectra))
+    out.insert(0, (spectra.shape, F32))
+    operands = [*ends[0], *v, columns, *t, pinned(spectra), pinned(stress)]
+    spectra, stress = on_chip(half_body, out, idx, operands, "half_stress", aliases={7: 0, 8: 1})
+    ends[1], stress, spectra = tie((ends[1], stress, spectra))
+    out = [((2 * elems, steps), F32)] * 2
+    keep, give = on_chip(last_body, out, idx, [*ends[1], *v, *t, pinned(stress)], "last_stress")
     give, spectra = tie((give, spectra))
     got = mate(give)
-    part = [((8, rows), F32)] * 2
-    body = functools.partial(moment_body, last)
-    keep_m, give_m = on_chip(
-        body, part, [idx, *both, *final, spectra, weights], "moments"
-    )
+    out = [((8, rows), F32)] * 2
+    operands = [*ends[1], columns, pinned(spectra), pinned(weights)]
+    keep_m, give_m = on_chip(moment_body, out, idx, operands, "moments")
     send = (keep[elems:] + got[elems:]).astype(BF16)
     half = keep_m + mate(give_m)
     stress = (keep[:elems] + got[:elems]) + peer(send).astype(F32)

time: 114 us -> 104 us (0.912)
  waiting for transfers between devices: 28.3 us -> 38.5 us
  local copies, waits for them, and re-layouts: 14.1 us -> 4.23 us
  Pallas kernels: 45 us -> 36.8 us
  starting transfers between devices: 23.4 us -> 19.4 us
  other arithmetic: 2.17 us -> 3.62 us
    ppermute x7 -> x8, waiting for transfers between devices: 0.02 us -> 18.5 us  [paired_shards(): lax.ppermute(a, 'mode', [(i, i ^ 2) for i in range(n_mode)])]
    unnamed x22 -> x4, local copies, waits for them, and re-layouts: 12.8 us -> 2.87 us
    pallas_call x12 -> x13, Pallas kernels: 45 us -> 36.8 us  [on_chip(): pl.pallas_call(body, out_shape=outs, in_specs=[SMEM] + [HBM] * len(both)...]
    ppermute x7 -> x8, starting transfers between devices: 10.2 us -> 3.28 us  [paired_shards(): lax.ppermute(a, 'mode', [(i, (i + 4) % n_mode) for i in range(n_mode)])]
    ppermute x7 -> x8, waiting for transfers between devices: 19.8 us -> 15.6 us  [paired_shards(): lax.ppermute(a, 'mode', [(i, (i + 4) % n_mode) for i in range(n_mode)])]
    ppermute x7 -> x8, starting transfers between devices: 7.59 us -> 10.9 us  [paired_shards(): lax.ppermute(a, 'mode', [(i, i ^ 2) for i in range(n_mode)])]
    ppermute x6, waiting for transfers between devices: 2.85 us -> 0.77 us  [paired_shards(): lax.ppermute(a, 'mode', [(i, i ^ 1) for i in range(n_mode)])]
    ppermute x3, waiting for transfers between devices: 5.64 us -> 3.69 us  [paired_shards(): peer = lambda a: lax.ppermute(a, 'node', [(0, 1), (1, 0)])]
  transfers between devices with their start and end apart: 23 -> 25, of which waited for: 8 -> 13; matrix products, arithmetic and copies ran while one was open for 1% -> 3% of each run, Pallas kernels for 37% -> 33%
where the time goes in v3:
time: 104 us; the launch traced here: 103 us
  waiting for transfers between devices  38.5 us (37%)
  Pallas kernels  36.8 us (35%)
  starting transfers between devices  19.4 us (19%)
  local copies, waits for them, and re-layouts  4.23 us (4%)
  other arithmetic  3.62 us (3%)
    pallas_call x13, Pallas kernels, on_chip(): pl.pallas_call(body, out_shape=outs, in_specs=[SMEM] + [HBM] * len(both)...  36.8 us
    ppermute x8, waiting for transfers between devices, paired_shards(): lax.ppermute(a, 'mode', [(i, i ^ 2) for i in range(n_mode)])  18.5 us
    ppermute x8, waiting for transfers between devices, paired_shards(): lax.ppermute(a, 'mode', [(i, (i + 4) % n_mode) for i in range(n_mode)])  15.6 us
    ppermute x8, starting transfers between devices, paired_shards(): lax.ppermute(a, 'mode', [(i, i ^ 2) for i in range(n_mode)])  10.9 us
    ppermute x3, waiting for transfers between devices, paired_shards(): peer = lambda a: lax.ppermute(a, 'node', [(0, 1), (1, 0)])  3.69 us
    ppermute x3, starting transfers between devices, paired_shards(): peer = lambda a: lax.ppermute(a, 'node', [(0, 1), (1, 0)])  3.67 us
    ppermute x8, starting transfers between devices, paired_shards(): lax.ppermute(a, 'mode', [(i, (i + 4) % n_mode) for i in range(n_mode)])  3.28 us
    unnamed x4, local copies, waits for them, and re-layouts  2.87 us
  transfers between devices with their start and end apart: 25, of which 13 were waited for; matrix products, arithmetic and copies ran while one was open for 3% of the time, Pallas kernels for 33%

profile of v3, /device:TPU:0, one launch (start us, length us, event | category | flops | bytes accessed | tf_op | source)
XLA Modules:
  0.0 103.4 jit_solution(11720111733732558407)
XLA Ops:
  4.4 2.6 %collective-permute-start.7 = (bf16[2,512,256]{2,1,0:T(8,128)(2,1)S(1)}, bf16[2,512,256]{2,1,0:T(8,128)(2,1)S(1)}, u32[]{:S(2)}, u32[]{:S(2)}) collective-permute-start(bf16[2,512,256]{2,1,0:T(8,128)(2,1)S(1)} %get-tuple-element.130.refs_0_), channel_id=1, source_target_pairs={{0,4},{2,6},{4,0},{6,2},{8,12},{10,14},{12,8},{14,10},{16,20},{18,... | collective-permute-start | bytes 1572872 | tf_op jit(solution)/shard_map/ppermute | solution.py:231
  7.0 1.6 %collective-permute-start.6 = (bf16[2,512,256]{2,1,0:T(8,128)(2,1)S(1)}, bf16[2,512,256]{2,1,0:T(8,128)(2,1)S(1)}, u32[]{:S(2)}, u32[]{:S(2)}) collective-permute-start(bf16[2,512,256]{2,1,0:T(8,128)(2,1)S(1)} %get-tuple-element.130.refs_0_), channel_id=1, source_target_pairs={{0,8},{2,10},{4,12},{6,14},{8,16},{10,18},{12,20},{14,22},{16,24},... | collective-permute-start | bytes 1572872 | tf_op jit(solution)/shard_map/ppermute | solution.py:230
  10.0 1.5 %collective-permute-start.1 = (f32[2,8,128]{2,1,0:T(8,128)S(1)}, f32[2,8,128]{2,1,0:T(8,128)S(1)}, u32[]{:S(2)}, u32[]{:S(2)}) collective-permute-start(f32[2,8,128]{2,1,0:T(8,128)S(1)} %pad_maximum_fusion.refs_0_), channel_id=1, source_target_pairs={{0,1},{1,0},{2,3},{3,2},{4,5},{5,4},{6,7},{7,6},{8,9},{9,8},{10,11... | collective-permute-start | bytes 24584 | tf_op jit(solution)/shard_map/ppermute | solution.py:233
  12.2 5.0 %table.1 = (bf16[512,1024]{1,0:T(8,128)(2,1)S(1)}, bf16[512,1024]{1,0:T(8,128)(2,1)S(1)}, f32[512,8]{1,0:T(8,128)S(1)}) custom-call(s32[19]{0:T(128)S(1)} %pad_add_fusion.1.idx, s32[1,1024]{1,0:T(1,128)S(1)} %bitcast.11), custom_call_target="tpu_custom_call" | custom-call | flops 1000 | bytes 1000 | tf_op jit(solution)/shard_map/table/pallas_call | solution.py:56
  17.9 1.6 %collective-permute-start.3 = (bf16[2,512,256]{2,1,0:T(8,128)(2,1)S(1)}, bf16[2,512,256]{2,1,0:T(8,128)(2,1)S(1)}, u32[]{:S(2)}, u32[]{:S(2)}) collective-permute-start(bf16[2,512,256]{2,1,0:T(8,128)(2,1)S(1)} %collective-permute-done.refs_1_), channel_id=1, source_target_pairs={{0,8},{2,10},{4,12},{6,14},{8,16},{10,18},{12,20},{14,22},{16,24},... | collective-permute-start | bytes 1572872 | tf_op jit(solution)/shard_map/ppermute | solution.py:230
  19.5 3.7 %collective-permute-done.6.refs_1_ = bf16[2,512,256]{2,1,0:T(8,128)(2,1)S(1)} collective-permute-done((bf16[2,512,256]{2,1,0:T(8,128)(2,1)S(1)}, bf16[2,512,256]{2,1,0:T(8,128)(2,1)S(1)}, u32[]{:S(2)}, u32[]{:S(2)}) %collective-permute-start.6) | collective-permute-done | bytes 524320 | tf_op jit(solution)/shard_map/ppermute | solution.py:230
  23.3 2.2 %copy-done = bf16[512,4096]{1,0:T(8,128)(2,1)S(1)} copy-done((bf16[512,4096]{1,0:T(8,128)(2,1)S(1)}, bf16[512,4096]{1,0:T(8,128)(2,1)}, u32[]{:S(2)}) %copy-start) | copy-done | bytes 4194328
  25.5 2.2 %add_spectra.7.refs_2_ = f32[2,512,1024]{2,1,0:T(8,128)S(1)} custom-call(s32[19]{0:T(128)S(1)} %pad_add_fusion.1.idx, bf16[512,4096]{1,0:T(8,128)(2,1)S(1)} %copy-done, bf16[512,4096]{1,0:T(8,128)(2,1)S(1)} %collective-permute-done.5.other, bf16[2,512,256]{2,1,0:T(8,128)(2,1)S(1)} %get-tuple-element.130.refs_0_, ...), custom_call_target="tpu_custom_call" | custom-call | flops 1000 | bytes 1000 | tf_op jit(solution)/shard_map/add_spectra/pallas_call | solution.py:56
  27.7 2.2 %add_spectra.8.refs_2_ = f32[2,512,1024]{2,1,0:T(8,128)S(1)} custom-call(s32[19]{0:T(128)S(1)} %pad_add_fusion.1.idx, bf16[512,4096]{1,0:T(8,128)(2,1)S(1)} %copy-done, bf16[512,4096]{1,0:T(8,128)(2,1)S(1)} %collective-permute-done.5.other, bf16[2,512,256]{2,1,0:T(8,128)(2,1)S(1)} %collective-permute-done.7.refs_0_, ...), custom_call_target="tpu_custom_call", output_to_operand_aliasing={{}: (5, {})} | custom-call | flops 1000 | bytes 1000 | tf_op jit(solution)/shard_map/add_spectra/pallas_call | solution.py:56
  30.0 2.2 %collective-permute-done.4.refs_0_ = bf16[2,512,256]{2,1,0:T(8,128)(2,1)S(1)} collective-permute-done((bf16[2,512,256]{2,1,0:T(8,128)(2,1)S(1)}, bf16[2,512,256]{2,1,0:T(8,128)(2,1)S(1)}, u32[]{:S(2)}, u32[]{:S(2)}) %collective-permute-start.4) | collective-permute-done | bytes 524320 | tf_op jit(solution)/shard_map/ppermute | solution.py:231
  32.1 2.4 %collective-permute-done.3.refs_1_ = bf16[2,512,256]{2,1,0:T(8,128)(2,1)S(1)} collective-permute-done((bf16[2,512,256]{2,1,0:T(8,128)(2,1)S(1)}, bf16[2,512,256]{2,1,0:T(8,128)(2,1)S(1)}, u32[]{:S(2)}, u32[]{:S(2)}) %collective-permute-start.3) | collective-permute-done | bytes 524320 | tf_op jit(solution)/shard_map/ppermute | solution.py:230
  34.5 1.5 %collective-permute-start.9 = (bf16[2,512,256]{2,1,0:T(8,128)(2,1)S(1)}, bf16[2,512,256]{2,1,0:T(8,128)(2,1)S(1)}, u32[]{:S(2)}, u32[]{:S(2)}) collective-permute-start(bf16[2,512,256]{2,1,0:T(8,128)(2,1)S(1)} %collective-permute-done.3.refs_1_), channel_id=1, source_target_pairs={{0,4},{2,6},{4,0},{6,2},{8,12},{10,14},{12,8},{14,10},{16,20},{18,... | collective-permute-start | bytes 1572872 | tf_op jit(solution)/shard_map/ppermute | solution.py:231
  36.0 2.2 %add_spectra.9.refs_2_ = f32[2,512,1024]{2,1,0:T(8,128)S(1)} custom-call(s32[19]{0:T(128)S(1)} %pad_add_fusion.1.idx, bf16[512,4096]{1,0:T(8,128)(2,1)S(1)} %copy-done, bf16[512,4096]{1,0:T(8,128)(2,1)S(1)} %collective-permute-done.5.other, bf16[2,512,256]{2,1,0:T(8,128)(2,1)S(1)} %collective-permute-done.4.refs_0_, ...), custom_call_target="tpu_custom_call", output_to_operand_aliasing={{}: (5, {})} | custom-call | flops 1000 | bytes 1000 | tf_op jit(solution)/shard_map/add_spectra/pallas_call | solution.py:56
  38.2 5.1 %collective-permute-done.11.refs_0_ = bf16[2,512,256]{2,1,0:T(8,128)(2,1)S(1)} collective-permute-done((bf16[2,512,256]{2,1,0:T(8,128)(2,1)S(1)}, bf16[2,512,256]{2,1,0:T(8,128)(2,1)S(1)}, u32[]{:S(2)}, u32[]{:S(2)}) %collective-permute-start.11) | collective-permute-done | bytes 524320 | tf_op jit(solution)/shard_map/ppermute | solution.py:231
  43.4 2.4 %collective-permute-done.10.refs_1_ = bf16[2,512,256]{2,1,0:T(8,128)(2,1)S(1)} collective-permute-done((bf16[2,512,256]{2,1,0:T(8,128)(2,1)S(1)}, bf16[2,512,256]{2,1,0:T(8,128)(2,1)S(1)}, u32[]{:S(2)}, u32[]{:S(2)}) %collective-permute-start.10) | collective-permute-done | bytes 524320 | tf_op jit(solution)/shard_map/ppermute | solution.py:230
  47.2 2.2 %add_spectra.10.refs_2_ = f32[2,512,1024]{2,1,0:T(8,128)S(1)} custom-call(s32[19]{0:T(128)S(1)} %pad_add_fusion.1.idx, bf16[512,4096]{1,0:T(8,128)(2,1)S(1)} %copy-done, bf16[512,4096]{1,0:T(8,128)(2,1)S(1)} %collective-permute-done.5.other, bf16[2,512,256]{2,1,0:T(8,128)(2,1)S(1)} %collective-permute-done.11.refs_0_, ...), custom_call_target="tpu_custom_call", output_to_operand_aliasing={{}: (5, {})} | custom-call | flops 1000 | bytes 1000 | tf_op jit(solution)/shard_map/add_spectra/pallas_call | solution.py:56
  49.5 5.1 %collective-permute-done.9.refs_0_ = bf16[2,512,256]{2,1,0:T(8,128)(2,1)S(1)} collective-permute-done((bf16[2,512,256]{2,1,0:T(8,128)(2,1)S(1)}, bf16[2,512,256]{2,1,0:T(8,128)(2,1)S(1)}, u32[]{:S(2)}, u32[]{:S(2)}) %collective-permute-start.9) | collective-permute-done | bytes 524320 | tf_op jit(solution)/shard_map/ppermute | solution.py:231
  54.6 2.4 %collective-permute-done.8.refs_1_ = bf16[2,512,256]{2,1,0:T(8,128)(2,1)S(1)} collective-permute-done((bf16[2,512,256]{2,1,0:T(8,128)(2,1)S(1)}, bf16[2,512,256]{2,1,0:T(8,128)(2,1)S(1)}, u32[]{:S(2)}, u32[]{:S(2)}) %collective-permute-start.8) | collective-permute-done | bytes 524320 | tf_op jit(solution)/shard_map/ppermute | solution.py:230
  58.5 4.1 %weights.1 = (bf16[512,512]{1,0:T(8,128)(2,1)S(1)}, bf16[512,512]{1,0:T(8,128)(2,1)S(1)}, bf16[512,512]{1,0:T(8,128)(2,1)S(1)}, bf16[512,512]{1,0:T(8,128)(2,1)S(1)}, bf16[2,2,512,256]{3,2,1,0:T(8,128)(2,1)S(1)}) custom-call(s32[19]{0:T(128)S(1)} %pad_add_fusion.1.idx, bf16[512,4096]{1,0:T(8,128)(2,1)S(1)} %copy-done, ...), custom_call_target="tpu_custom_call" | custom-call | flops 1000 | bytes 1000 | tf_op jit(solution)/shard_map/weights/pallas_call | solution.py:56
  62.6 2.2 %add_spectra.11.refs_2_ = f32[2,512,1024]{2,1,0:T(8,128)S(1)} custom-call(s32[19]{0:T(128)S(1)} %pad_add_fusion.1.idx, bf16[512,4096]{1,0:T(8,128)(2,1)S(1)} %copy-done, bf16[512,4096]{1,0:T(8,128)(2,1)S(1)} %collective-permute-done.5.other, bf16[2,512,256]{2,1,0:T(8,128)(2,1)S(1)} %collective-permute-done.9.refs_0_, ...), custom_call_target="tpu_custom_call", output_to_operand_aliasing={{}: (5, {})} | custom-call | flops 1000 | bytes 1000 | tf_op jit(solution)/shard_map/add_spectra/pallas_call | solution.py:56
  65.9 2.4 %collective-permute-done.15.refs_1_ = bf16[2,512,256]{2,1,0:T(8,128)(2,1)S(1)} collective-permute-done((bf16[2,512,256]{2,1,0:T(8,128)(2,1)S(1)}, bf16[2,512,256]{2,1,0:T(8,128)(2,1)S(1)}, u32[]{:S(2)}, u32[]{:S(2)}) %collective-permute-start.15) | collective-permute-done | bytes 524320 | tf_op jit(solution)/shard_map/ppermute | solution.py:230
  68.3 1.6 %collective-permute-start.19 = (bf16[1,512,256]{2,1,0:T(8,128)(2,1)S(1)}, bf16[1,512,256]{2,1,0:T(8,128)(2,1)S(1)}, u32[]{:S(2)}, u32[]{:S(2)}) collective-permute-start(bf16[1,512,256]{2,1,0:T(8,128)(2,1)S(1)} %slice.26), channel_id=1, source_target_pairs={{0,4},{2,6},{4,0},{6,2},{8,12},{10,14},{12,8},{14,10},{16,20},{18,... | collective-permute-start | bytes 786440 | tf_op jit(solution)/shard_map/ppermute | solution.py:231
  69.9 2.2 %add_spectra.12.refs_2_ = f32[2,512,1024]{2,1,0:T(8,128)S(1)} custom-call(s32[19]{0:T(128)S(1)} %pad_add_fusion.1.idx, bf16[512,4096]{1,0:T(8,128)(2,1)S(1)} %copy-done, bf16[512,4096]{1,0:T(8,128)(2,1)S(1)} %collective-permute-done.5.other, bf16[2,512,256]{2,1,0:T(8,128)(2,1)S(1)} %collective-permute-done.16.refs_0_, ...), custom_call_target="tpu_custom_call", output_to_operand_aliasing={{}: (5, {})} | custom-call | flops 1000 | bytes 1000 | tf_op jit(solution)/shard_map/add_spectra/pallas_call | solution.py:56
  72.1 5.0 %collective-permute-done.14.refs_0_ = bf16[2,512,256]{2,1,0:T(8,128)(2,1)S(1)} collective-permute-done((bf16[2,512,256]{2,1,0:T(8,128)(2,1)S(1)}, bf16[2,512,256]{2,1,0:T(8,128)(2,1)S(1)}, u32[]{:S(2)}, u32[]{:S(2)}) %collective-permute-start.14) | collective-permute-done | bytes 524320 | tf_op jit(solution)/shard_map/ppermute | solution.py:231
  77.1 2.4 %collective-permute-done.13.refs_1_ = bf16[2,512,256]{2,1,0:T(8,128)(2,1)S(1)} collective-permute-done((bf16[2,512,256]{2,1,0:T(8,128)(2,1)S(1)}, bf16[2,512,256]{2,1,0:T(8,128)(2,1)S(1)}, u32[]{:S(2)}, u32[]{:S(2)}) %collective-permute-start.13) | collective-permute-done | bytes 524320 | tf_op jit(solution)/shard_map/ppermute | solution.py:230
  79.6 1.6 %collective-permute-start.17 = (bf16[1,512,256]{2,1,0:T(8,128)(2,1)S(1)}, bf16[1,512,256]{2,1,0:T(8,128)(2,1)S(1)}, u32[]{:S(2)}, u32[]{:S(2)}) collective-permute-start(bf16[1,512,256]{2,1,0:T(8,128)(2,1)S(1)} %slice.24), channel_id=1, source_target_pairs={{0,4},{2,6},{4,0},{6,2},{8,12},{10,14},{12,8},{14,10},{16,20},{18,... | collective-permute-start | bytes 786440 | tf_op jit(solution)/shard_map/ppermute | solution.py:231
  81.1 2.2 %add_spectra.13.spectra = f32[2,512,1024]{2,1,0:T(8,128)S(1)} custom-call(s32[19]{0:T(128)S(1)} %pad_add_fusion.1.idx, bf16[512,4096]{1,0:T(8,128)(2,1)S(1)} %copy-done, bf16[512,4096]{1,0:T(8,128)(2,1)S(1)} %collective-permute-done.5.other, bf16[2,512,256]{2,1,0:T(8,128)(2,1)S(1)} %collective-permute-done.14.refs_0_, ...), custom_call_target="tpu_custom_call", output_to_operand_aliasing={{}: (5, {})} | custom-call | flops 1000 | bytes 1000 | tf_op jit(solution)/shard_map/add_spectra/pallas_call | solution.py:56
  83.4 4.0 %first_stress.1.stress = f32[512,512]{1,0:T(8,128)S(1)} custom-call(s32[19]{0:T(128)S(1)} %pad_add_fusion.1.idx, f32[2,512,1024]{2,1,0:T(8,128)S(1)} %add_spectra.13.spectra, bf16[512,512]{1,0:T(8,128)(2,1)S(1)} %get-tuple-element.106.w_head, bf16[512,512]{1,0:T(8,128)(2,1)S(1)} %get-tuple-element.107.w_tail, ...), custom_call_target="tpu_custom_call" | custom-call | flops 1000 | bytes 1000 | tf_op jit(solution)/shard_map/first_stress/pallas_call | solution.py:56
  87.4 3.3 %half_stress.1 = (f32[2,512,1024]{2,1,0:T(8,128)S(1)}, f32[512,512]{1,0:T(8,128)S(1)}) custom-call(s32[19]{0:T(128)S(1)} %pad_add_fusion.1.idx, bf16[1,512,256]{2,1,0:T(8,128)(2,1)S(1)} %collective-permute-done.19.real, bf16[1,512,256]{2,1,0:T(8,128)(2,1)S(1)} %collective-permute-done.20.imag, ...), custom_call_target="tpu_custom_call", output_to_operand_aliasing={{0}: (8, {}), {1}: (9, {})} | custom-call | flops 1000 | bytes 1000 | tf_op jit(solution)/shard_map/half_stress/pallas_call | solution.py:56
  90.7 2.5 %last_stress.1 = (f32[256,512]{1,0:T(8,128)S(1)}, f32[256,512]{1,0:T(8,128)S(1)}) custom-call(s32[19]{0:T(128)S(1)} %pad_add_fusion.1.idx, bf16[1,512,256]{2,1,0:T(8,128)(2,1)S(1)} %collective-permute-done.17.real, bf16[1,512,256]{2,1,0:T(8,128)(2,1)S(1)} %collective-permute-done.18.imag, bf16[512,512]{1,0:T(8,128)(2,1)S(1)} %get-tuple-element.112.v_head, ...), custom_call_target="tpu_custom_call" | custom-call | flops 1000 | bytes 1000 | tf_op jit(solution)/shard_map/last_stress/pallas_call | solution.py:56
  93.3 2.3 %moments.1 = (f32[8,512]{1,0:T(8,128)S(1)}, f32[8,512]{1,0:T(8,128)S(1)}) custom-call(s32[19]{0:T(128)S(1)} %pad_add_fusion.1.idx, bf16[1,512,256]{2,1,0:T(8,128)(2,1)S(1)} %collective-permute-done.17.real, bf16[1,512,256]{2,1,0:T(8,128)(2,1)S(1)} %collective-permute-done.18.imag, bf16[2,2,512,256]{3,2,1,0:T(8,128)(2,1)S(1)} %get-tuple-element.114.columns, ...), custom_call_target="tpu_custom_call" | custom-call | flops 1000 | bytes 1000 | tf_op jit(solution)/shard_map/moments/pallas_call | solution.py:56
  98.3 3.7 %collective-permute-done.24 = f32[8,512]{1,0:T(8,128)S(1)} collective-permute-done((f32[8,512]{1,0:T(8,128)S(1)}, f32[8,512]{1,0:T(8,128)S(1)}, u32[]{:S(2)}, u32[]{:S(2)}) %collective-permute-start.24) | collective-permute-done | bytes 16416 | tf_op jit(solution)/shard_map/ppermute | solution.py:233
  (49 shorter events, 14.9 us)
Async XLA Ops:
  1.9 2.1 %collective-permute-start = (bf16[2,512,256]{2,1,0:T(8,128)(2,1)S(1)}, bf16[2,512,256]{2,1,0:T(8,128)(2,1)S(1)}, u32[]{:S(2)}, u32[]{:S(2)}) collective-permute-start(bf16[2,512,256]{2,1,0:T(8,128)(2,1)S(1)} %get-tuple-element.131), channel_id=1, source_target_pairs={{0,2},{2,0},{4,6},{6,4},{8,10},{10,8},{12,14},{14,12},{16,18},{18,... | collective-permute-start | bytes 1572872 | tf_op jit(solution)/shard_map/ppermute | solution.py:232
  4.0 19.3 %collective-permute-start.5 = (bf16[512,4096]{1,0:T(8,128)(2,1)}, bf16[512,4096]{1,0:T(8,128)(2,1)S(1)}, u32[]{:S(2)}, u32[]{:S(2)}) collective-permute-start(bf16[512,4096]{1,0:T(8,128)(2,1)} %own.15), channel_id=1, source_target_pairs={{0,2},{2,0},{4,6},{6,4},{8,10},{10,8},{12,14},{14,12},{16,18},{18,... | collective-permute-start | bytes 12582920 | tf_op jit(solution)/shard_map/ppermute | solution.py:232
  4.4 15.1 %collective-permute-start.7 = (bf16[2,512,256]{2,1,0:T(8,128)(2,1)S(1)}, bf16[2,512,256]{2,1,0:T(8,128)(2,1)S(1)}, u32[]{:S(2)}, u32[]{:S(2)}) collective-permute-start(bf16[2,512,256]{2,1,0:T(8,128)(2,1)S(1)} %get-tuple-element.130.refs_0_), channel_id=1, source_target_pairs={{0,4},{2,6},{4,0},{6,2},{8,12},{10,14},{12,8},{14,10},{16,20},{18,... | collective-permute-start | bytes 1572872 | tf_op jit(solution)/shard_map/ppermute | solution.py:231
  7.0 16.2 %collective-permute-start.6 = (bf16[2,512,256]{2,1,0:T(8,128)(2,1)S(1)}, bf16[2,512,256]{2,1,0:T(8,128)(2,1)S(1)}, u32[]{:S(2)}, u32[]{:S(2)}) collective-permute-start(bf16[2,512,256]{2,1,0:T(8,128)(2,1)S(1)} %get-tuple-element.130.refs_0_), channel_id=1, source_target_pairs={{0,8},{2,10},{4,12},{6,14},{8,16},{10,18},{12,20},{14,22},{16,24},... | collective-permute-start | bytes 1572872 | tf_op jit(solution)/shard_map/ppermute | solution.py:230
  10.0 7.3 %collective-permute-start.2 = (f32[2,8,128]{2,1,0:T(8,128)S(1)}, f32[2,8,128]{2,1,0:T(8,128)S(1)}, u32[]{:S(2)}, u32[]{:S(2)}) collective-permute-start(f32[2,8,128]{2,1,0:T(8,128)S(1)} %pad_maximum_fusion.refs_0_), channel_id=1, source_target_pairs={{0,2},{2,0},{4,6},{6,4},{8,10},{10,8},{12,14},{14,12},{16,18},{18,... | collective-permute-start | bytes 24584 | tf_op jit(solution)/shard_map/ppermute | solution.py:232
  10.0 7.4 %collective-permute-start.1 = (f32[2,8,128]{2,1,0:T(8,128)S(1)}, f32[2,8,128]{2,1,0:T(8,128)S(1)}, u32[]{:S(2)}, u32[]{:S(2)}) collective-permute-start(f32[2,8,128]{2,1,0:T(8,128)S(1)} %pad_maximum_fusion.refs_0_), channel_id=1, source_target_pairs={{0,1},{1,0},{2,3},{3,2},{4,5},{5,4},{6,7},{7,6},{8,9},{9,8},{10,11... | collective-permute-start | bytes 24584 | tf_op jit(solution)/shard_map/ppermute | solution.py:233
  11.6 0.7 copy-start.1
  17.3 14.8 %collective-permute-start.4 = (bf16[2,512,256]{2,1,0:T(8,128)(2,1)S(1)}, bf16[2,512,256]{2,1,0:T(8,128)(2,1)S(1)}, u32[]{:S(2)}, u32[]{:S(2)}) collective-permute-start(bf16[2,512,256]{2,1,0:T(8,128)(2,1)S(1)} %collective-permute-done.refs_1_), channel_id=1, source_target_pairs={{0,4},{2,6},{4,0},{6,2},{8,12},{10,14},{12,8},{14,10},{16,20},{18,... | collective-permute-start | bytes 1572872 | tf_op jit(solution)/shard_map/ppermute | solution.py:231
  17.9 16.6 %collective-permute-start.3 = (bf16[2,512,256]{2,1,0:T(8,128)(2,1)S(1)}, bf16[2,512,256]{2,1,0:T(8,128)(2,1)S(1)}, u32[]{:S(2)}, u32[]{:S(2)}) collective-permute-start(bf16[2,512,256]{2,1,0:T(8,128)(2,1)S(1)} %collective-permute-done.refs_1_), channel_id=1, source_target_pairs={{0,8},{2,10},{4,12},{6,14},{8,16},{10,18},{12,20},{14,22},{16,24},... | collective-permute-start | bytes 1572872 | tf_op jit(solution)/shard_map/ppermute | solution.py:230
  23.2 20.2 %collective-permute-start.11 = (bf16[2,512,256]{2,1,0:T(8,128)(2,1)S(1)}, bf16[2,512,256]{2,1,0:T(8,128)(2,1)S(1)}, u32[]{:S(2)}, u32[]{:S(2)}) collective-permute-start(bf16[2,512,256]{2,1,0:T(8,128)(2,1)S(1)} %collective-permute-done.6.refs_1_), channel_id=1, source_target_pairs={{0,4},{2,6},{4,0},{6,2},{8,12},{10,14},{12,8},{14,10},{16,20},{18,... | collective-permute-start | bytes 1572872 | tf_op jit(solution)/shard_map/ppermute | solution.py:231
  23.3 22.4 %collective-permute-start.10 = (bf16[2,512,256]{2,1,0:T(8,128)(2,1)S(1)}, bf16[2,512,256]{2,1,0:T(8,128)(2,1)S(1)}, u32[]{:S(2)}, u32[]{:S(2)}) collective-permute-start(bf16[2,512,256]{2,1,0:T(8,128)(2,1)S(1)} %collective-permute-done.6.refs_1_), channel_id=1, source_target_pairs={{0,8},{2,10},{4,12},{6,14},{8,16},{10,18},{12,20},{14,22},{16,24},... | collective-permute-start | bytes 1572872 | tf_op jit(solution)/shard_map/ppermute | solution.py:230
  23.3 2.2 %copy-start = (bf16[512,4096]{1,0:T(8,128)(2,1)S(1)}, bf16[512,4096]{1,0:T(8,128)(2,1)}, u32[]{:S(2)}) copy-start(bf16[512,4096]{1,0:T(8,128)(2,1)} %own.15) | copy-start | bytes 12582916
  34.5 20.1 %collective-permute-start.9 = (bf16[2,512,256]{2,1,0:T(8,128)(2,1)S(1)}, bf16[2,512,256]{2,1,0:T(8,128)(2,1)S(1)}, u32[]{:S(2)}, u32[]{:S(2)}) collective-permute-start(bf16[2,512,256]{2,1,0:T(8,128)(2,1)S(1)} %collective-permute-done.3.refs_1_), channel_id=1, source_target_pairs={{0,4},{2,6},{4,0},{6,2},{8,12},{10,14},{12,8},{14,10},{16,20},{18,... | collective-permute-start | bytes 1572872 | tf_op jit(solution)/shard_map/ppermute | solution.py:231
  36.0 21.0 %collective-permute-start.8 = (bf16[2,512,256]{2,1,0:T(8,128)(2,1)S(1)}, bf16[2,512,256]{2,1,0:T(8,128)(2,1)S(1)}, u32[]{:S(2)}, u32[]{:S(2)}) collective-permute-start(bf16[2,512,256]{2,1,0:T(8,128)(2,1)S(1)} %collective-permute-done.3.refs_1_), channel_id=1, source_target_pairs={{0,8},{2,10},{4,12},{6,14},{8,16},{10,18},{12,20},{14,22},{16,24},... | collective-permute-start | bytes 1572872 | tf_op jit(solution)/shard_map/ppermute | solution.py:230
  36.0 2.2 %collective-permute-start.12 = (f32[2,8,128]{2,1,0:T(8,128)S(1)}, f32[2,8,128]{2,1,0:T(8,128)S(1)}, u32[]{:S(2)}, u32[]{:S(2)}) collective-permute-start(f32[2,8,128]{2,1,0:T(8,128)S(1)} %collective-permute-done.1.refs_1_), channel_id=1, source_target_pairs={{0,2},{2,0},{4,6},{6,4},{8,10},{10,8},{12,14},{14,12},{16,18},{18,... | collective-permute-start | bytes 24584 | tf_op jit(solution)/shard_map/ppermute | solution.py:232
  45.8 20.1 %collective-permute-start.16 = (bf16[2,512,256]{2,1,0:T(8,128)(2,1)S(1)}, bf16[2,512,256]{2,1,0:T(8,128)(2,1)S(1)}, u32[]{:S(2)}, u32[]{:S(2)}) collective-permute-start(bf16[2,512,256]{2,1,0:T(8,128)(2,1)S(1)} %collective-permute-done.10.refs_1_), channel_id=1, source_target_pairs={{0,4},{2,6},{4,0},{6,2},{8,12},{10,14},{12,8},{14,10},{16,20},{18,... | collective-permute-start | bytes 1572872 | tf_op jit(solution)/shard_map/ppermute | solution.py:231
  47.2 21.0 %collective-permute-start.15 = (bf16[2,512,256]{2,1,0:T(8,128)(2,1)S(1)}, bf16[2,512,256]{2,1,0:T(8,128)(2,1)S(1)}, u32[]{:S(2)}, u32[]{:S(2)}) collective-permute-start(bf16[2,512,256]{2,1,0:T(8,128)(2,1)S(1)} %collective-permute-done.10.refs_1_), channel_id=1, source_target_pairs={{0,8},{2,10},{4,12},{6,14},{8,16},{10,18},{12,20},{14,22},{16,24},... | collective-permute-start | bytes 1572872 | tf_op jit(solution)/shard_map/ppermute | solution.py:230
  57.0 20.1 %collective-permute-start.14 = (bf16[2,512,256]{2,1,0:T(8,128)(2,1)S(1)}, bf16[2,512,256]{2,1,0:T(8,128)(2,1)S(1)}, u32[]{:S(2)}, u32[]{:S(2)}) collective-permute-start(bf16[2,512,256]{2,1,0:T(8,128)(2,1)S(1)} %collective-permute-done.8.refs_1_), channel_id=1, source_target_pairs={{0,4},{2,6},{4,0},{6,2},{8,12},{10,14},{12,8},{14,10},{16,20},{18,... | collective-permute-start | bytes 1572872 | tf_op jit(solution)/shard_map/ppermute | solution.py:231
  58.5 21.0 %collective-permute-start.13 = (bf16[2,512,256]{2,1,0:T(8,128)(2,1)S(1)}, bf16[2,512,256]{2,1,0:T(8,128)(2,1)S(1)}, u32[]{:S(2)}, u32[]{:S(2)}) collective-permute-start(bf16[2,512,256]{2,1,0:T(8,128)(2,1)S(1)} %collective-permute-done.8.refs_1_), channel_id=1, source_target_pairs={{0,8},{2,10},{4,12},{6,14},{8,16},{10,18},{12,20},{14,22},{16,24},... | collective-permute-start | bytes 1572872 | tf_op jit(solution)/shard_map/ppermute | solution.py:230
  68.3 19.1 %collective-permute-start.20 = (bf16[1,512,256]{2,1,0:T(8,128)(2,1)S(1)}, bf16[1,512,256]{2,1,0:T(8,128)(2,1)S(1)}, u32[]{:S(2)}, u32[]{:S(2)}) collective-permute-start(bf16[1,512,256]{2,1,0:T(8,128)(2,1)S(1)} %slice.27), channel_id=1, source_target_pairs={{0,8},{2,10},{4,12},{6,14},{8,16},{10,18},{12,20},{14,22},{16,24},... | collective-permute-start | bytes 786440 | tf_op jit(solution)/shard_map/ppermute | solution.py:230
  68.3 19.1 %collective-permute-start.19 = (bf16[1,512,256]{2,1,0:T(8,128)(2,1)S(1)}, bf16[1,512,256]{2,1,0:T(8,128)(2,1)S(1)}, u32[]{:S(2)}, u32[]{:S(2)}) collective-permute-start(bf16[1,512,256]{2,1,0:T(8,128)(2,1)S(1)} %slice.26), channel_id=1, source_target_pairs={{0,4},{2,6},{4,0},{6,2},{8,12},{10,14},{12,8},{14,10},{16,20},{18,... | collective-permute-start | bytes 786440 | tf_op jit(solution)/shard_map/ppermute | solution.py:231
  79.5 11.2 %collective-permute-start.18 = (bf16[1,512,256]{2,1,0:T(8,128)(2,1)S(1)}, bf16[1,512,256]{2,1,0:T(8,128)(2,1)S(1)}, u32[]{:S(2)}, u32[]{:S(2)}) collective-permute-start(bf16[1,512,256]{2,1,0:T(8,128)(2,1)S(1)} %slice.25), channel_id=1, source_target_pairs={{0,8},{2,10},{4,12},{6,14},{8,16},{10,18},{12,20},{14,22},{16,24},... | collective-permute-start | bytes 786440 | tf_op jit(solution)/shard_map/ppermute | solution.py:230
  79.6 11.1 %collective-permute-start.17 = (bf16[1,512,256]{2,1,0:T(8,128)(2,1)S(1)}, bf16[1,512,256]{2,1,0:T(8,128)(2,1)S(1)}, u32[]{:S(2)}, u32[]{:S(2)}) collective-permute-start(bf16[1,512,256]{2,1,0:T(8,128)(2,1)S(1)} %slice.24), channel_id=1, source_target_pairs={{0,4},{2,6},{4,0},{6,2},{8,12},{10,14},{12,8},{14,10},{16,20},{18,... | collective-permute-start | bytes 786440 | tf_op jit(solution)/shard_map/ppermute | solution.py:231
  93.2 3.0 %collective-permute-start.21 = (f32[256,512]{1,0:T(8,128)S(1)}, f32[256,512]{1,0:T(8,128)S(1)}, u32[]{:S(2)}, u32[]{:S(2)}) collective-permute-start(f32[256,512]{1,0:T(8,128)S(1)} %get-tuple-element.125), channel_id=1, source_target_pairs={{0,2},{2,0},{4,6},{6,4},{8,10},{10,8},{12,14},{14,12},{16,18},{18,... | collective-permute-start | bytes 1572872 | tf_op jit(solution)/shard_map/ppermute | solution.py:232
  95.6 1.7 %collective-permute-start.23 = (f32[8,512]{1,0:T(8,128)S(1)}, f32[8,512]{1,0:T(8,128)S(1)}, u32[]{:S(2)}, u32[]{:S(2)}) collective-permute-start(f32[8,512]{1,0:T(8,128)S(1)} %get-tuple-element.129), channel_id=1, source_target_pairs={{0,2},{2,0},{4,6},{6,4},{8,10},{10,8},{12,14},{14,12},{16,18},{18,... | collective-permute-start | bytes 49160 | tf_op jit(solution)/shard_map/ppermute | solution.py:232
  96.2 6.4 %collective-permute-start.22 = (bf16[128,512]{1,0:T(8,128)(2,1)S(1)}, bf16[128,512]{1,0:T(8,128)(2,1)S(1)}, u32[]{:S(2)}, u32[]{:S(2)}) collective-permute-start(bf16[128,512]{1,0:T(8,128)(2,1)S(1)} %fusion), channel_id=1, source_target_pairs={{0,1},{1,0},{2,3},{3,2},{4,5},{5,4},{6,7},{7,6},{8,9},{9,8},{10,11... | collective-permute-start | bytes 393224 | tf_op jit(solution)/shard_map/ppermute | solution.py:233
  97.3 4.8 %collective-permute-start.24 = (f32[8,512]{1,0:T(8,128)S(1)}, f32[8,512]{1,0:T(8,128)S(1)}, u32[]{:S(2)}, u32[]{:S(2)}) collective-permute-start(f32[8,512]{1,0:T(8,128)S(1)} %add.85), channel_id=1, source_target_pairs={{0,1},{1,0},{2,3},{3,2},{4,5},{5,4},{6,7},{7,6},{8,9},{9,8},{10,11... | collective-permute-start | bytes 49160 | tf_op jit(solution)/shard_map/ppermute | solution.py:233

commit v4 on v3

v4 whole, which is shorter than its diff:
```python
import functools
import math

import jax
import jax.numpy as jnp
from jax import lax
from jax.experimental import pallas as pl
from jax.experimental.pallas import tpu as pltpu
from jax.sharding import PartitionSpec as P

HARM = 4096
F32 = jnp.float32
BF16 = jnp.bfloat16


def moment_weights(harmonic, lines):
    ratios = harmonic.astype(F32) / HARM
    squared = ratios * ratios
    return jnp.stack([jnp.ones_like(ratios), ratios, squared, squared * squared]) / lines


def nt(a, b):
    return lax.dot_general(a, b, (((1,), (1,)), ((), ())), preferred_element_type=F32)


def nn(a, b):
    return jnp.dot(a, b, preferred_element_type=F32)


def kernel_split(value):
    head = value.astype(BF16)
    return head, (value - head.astype(F32)).astype(BF16)


VMEM = pl.BlockSpec(memory_space=pltpu.VMEM)
HBM = pl.BlockSpec(memory_space=pltpu.HBM)


def on_chip(
    body, out_shapes, operands, name, both=(), columns=0, modes=0, aliases=None, keep_columns=False, flops=1000
):
    outs = [pltpu.VMEM(shape, dtype) for shape, dtype in out_shapes]
    scratch = []
    if both:
        rows = both[0].shape[0]
        scratch = [pltpu.SemaphoreType.DMA((2, columns))]
        if not keep_columns:
            scratch.insert(0, pltpu.VMEM((2, columns, rows, modes), BF16))
    aliases = {len(both) + i: o for i, o in (aliases or {}).items()}
    return pl.pallas_call(
        body,
        out_shape=outs,
        in_specs=[HBM] * len(both) + [VMEM] * len(operands),
        out_specs=[VMEM] * len(outs),
        scratch_shapes=scratch,
        input_output_aliases=aliases,
        compiler_params=pltpu.CompilerParams(vmem_limit_bytes=16 << 20),
        cost_estimate=pl.CostEstimate(flops=flops, bytes_accessed=1000, transcendentals=0),
        name=name,
    )(*both, *operands)


def pinned(value):
    return pltpu.with_memory_space_constraint(value, pltpu.VMEM)


def fetch(n_mode, wanted, both, buffer, sems):
    modes = buffer.shape[3]
    place = lax.axis_index("mode")
    layers = n_mode // 4
    layer, side, core = lax.div(place, 4), lax.rem(lax.div(place, 2), 2), lax.rem(place, 2)
    copies = {}
    for b, (back, flip, half) in enumerate(wanted):
        at = lax.rem(layer + (layers - back), layers) * 4
        at = at + lax.rem(side + flip, 2) * 2 + lax.rem(core + half, 2)
        at = pl.ds(pl.multiple_of(at * modes, modes), modes)
        for g, table in enumerate(both):
            copies[g, b] = pltpu.make_async_copy(table.at[:, at], buffer.at[g, b], sems.at[g, b])
    for copy in copies.values():
        copy.start()
    return copies


def row_tiles(rows):
    width = min(rows, 256)
    for g in range(2):
        for r in range(0, rows, width):
            yield g, pl.ds(r, width), pl.ds(g * rows + r, width)


def flat(panel):
    if isinstance(panel, tuple):
        return jnp.concatenate([piece[c] for c in range(2) for piece in panel], axis=0)
    return panel[...].reshape(-1, panel.shape[2])


def spectra_body(n_mode, wanted, carried, own, other, *refs):
    count = len(wanted)
    blocks, (out, buffer, sems) = refs[:count], refs[-3:]
    parts, lines, _ = out.shape
    copies = fetch(n_mode, wanted, (own, other), buffer, sems)
    for g, here, there in row_tiles(own.shape[0]):
        if here.start == 0:
            for b in range(count):
                copies[g, b].wait()
        total = out[:, :, there].reshape(parts * lines, -1) if carried else None
        for b, panel in enumerate(blocks):
            term = nt(flat(panel), buffer[g, b, here, :])
            total = term if total is None else total + term
        out[:, :, there] = total.reshape(parts, lines, -1)


def add_spectra(n_mode, blocks, wanted, both, spectra):
    parts, lines, modes = blocks[0].shape
    count = len(blocks)
    operands, aliases = list(blocks), {}
    if spectra is not None:
        aliases = {count: 0}
        operands.append(pinned(spectra))
    body = functools.partial(spectra_body, n_mode, wanted, spectra is not None)
    shape = (parts, lines, 2 * both[0].shape[0])
    return on_chip(body, [(shape, F32)], operands, "add_spectra", both, count, modes, aliases)[0]


def cos_sin(phases):
    turn = (phases + HARM // 8) >> 10
    x = (phases - (turn << 10)).astype(F32) * (2.0 * math.pi / HARM)
    xx = x * x
    sine = x * (1.0 + xx * (-1 / 6 + xx * (1 / 120 + xx * (-1 / 5040 + xx * (1 / 362880)))))
    cosine = 1.0 + xx * (-1 / 2 + xx * (1 / 24 + xx * (-1 / 720 + xx * (1 / 40320 - xx / 3628800))))
    odd = (turn & 1) == 1
    turn = turn & 3
    first, second = jnp.where(odd, sine, cosine), jnp.where(odd, cosine, sine)
    minus_cos = (turn == 1) | (turn == 2)
    return jnp.where(minus_cos, -first, first), jnp.where(turn >= 2, -second, second)


def table_body(harmonic, table, weights):
    steps, lines = table.shape[0] // 2, table.shape[1] // 2
    total_lines = harmonic.shape[1] * 2
    core = lax.rem(lax.axis_index("mode"), 2)
    mine = harmonic[:, pl.ds(pl.multiple_of(core * lines, lines), lines)]
    ratios = mine.astype(F32) * (1.0 / HARM)
    squared = ratios * ratios
    ones = jnp.ones_like(ratios)
    rows = [ones, ratios, squared, squared * squared] * 2
    weights[...] = (jnp.concatenate(rows, axis=0) * (1.0 / total_lines)).T
    scale = math.sqrt(2.0 / total_lines)
    tile = 32

    def fill(i, _):
        here = pl.multiple_of(i * tile, tile)
        ids = lax.broadcasted_iota(jnp.int32, (tile, lines), 0) + here
        cosine, sine = cos_sin((ids * mine) & (HARM - 1))
        for at, value in ((0, scale * cosine), (lines, -scale * sine)):
            head, tail = kernel_split(value)
            table[pl.ds(here, tile), at : at + lines] = head
            table[pl.ds(steps + here, tile), at : at + lines] = tail
        return 0

    lax.fori_loop(0, steps // tile, fill, 0)


def weights_body(n_mode, wanted, own, other, *refs):
    pairs, (w, v, buffer, sems) = refs[:4], refs[4:]
    copies = fetch(n_mode, wanted, (own, other), buffer, sems)
    elems = pairs[0].shape[2]
    modes = buffer.shape[3]
    rows = own.shape[0]
    place = lax.axis_index("mode")
    bases = (place * rows, (place + 1 - 2 * lax.rem(place, 2)) * rows)
    slots = lax.broadcasted_iota(jnp.int32, (elems, rows), 1).astype(F32)
    for p, pair in enumerate(pairs):
        local, value = (pair[0] - bases[p // 2].astype(F32)).T, pair[1].T
        weight = jnp.zeros((elems, rows), F32)
        for k in range(local.shape[1]):
            weight += jnp.where(local[:, k : k + 1] == slots, value[:, k : k + 1], 0.0)
        head, tail = kernel_split(weight)
        w[p * elems : (p + 1) * elems, :] = head
        w[(4 + p) * elems : (5 + p) * elems, :] = tail
    for g in range(2):
        head_rows = slice(2 * g * elems, 2 * (g + 1) * elems)
        tail_rows = slice((4 + 2 * g) * elems, (6 + 2 * g) * elems)
        for b in range(len(wanted)):
            copies[g, b].wait()
            part = buffer[g, b]
            head, tail = kernel_split(nn(w[head_rows, :], part) + nn(w[tail_rows, :], part))
            v[head_rows, b * modes : (b + 1) * modes] = head
            v[tail_rows, b * modes : (b + 1) * modes] = tail


def stress_body(spectra, w, table, out):
    parts, lines, both = spectra.shape
    rows, elems = both // 2, out.shape[0] // 2
    steps = out.shape[1]
    for g in range(2):
        here = slice(g * elems, (g + 1) * elems)
        values = spectra[:, :, g * rows : (g + 1) * rows].reshape(parts * lines, rows)
        s_head, s_tail = kernel_split(values)
        w_head, w_tail = w[here, :], w[(2 + g) * elems : (3 + g) * elems, :]
        picked = nt(w_head, s_head) + nt(w_head, s_tail) + nt(w_tail, s_head)
        p_head, p_tail = kernel_split(picked)
        t_head = table[:steps]
        out[here, :] = nt(p_head, t_head) + nt(p_tail, t_head) + nt(p_head, table[steps:])


def time_term(panel, v, table):
    steps, elems = table.shape[0] // 2, v.shape[0] // 2
    grid = nn(table[...], panel)
    g_head, g_tail = kernel_split(grid[:steps] + grid[steps:])
    total = nt(v, g_head)
    return total[:elems] + total[elems:] + nt(v[:elems], g_tail)


def half_body(near, far, v, columns, table, spectra, stress, spectra_out, stress_out):
    parts, lines, _ = spectra.shape
    panel = flat((near, far))
    for g, here, there in row_tiles(columns.shape[2]):
        total = spectra[:, :, there].reshape(parts * lines, -1) + nt(panel, columns[g, 0, here, :])
        spectra_out[:, :, there] = total.reshape(parts, lines, -1)
    stress_out[...] = stress[...] + time_term(panel, v[:, : panel.shape[1]], table)


def last_body(near, far, v, table, before, keep, give):
    panel = flat((near, far))
    total = before[...] + time_term(panel, v[:, panel.shape[1] :], table)
    half = total.shape[0] // 2
    keep[...] = total[:half]
    give[...] = total[half:]


def moment_body(near, far, columns, spectra, weights, keep, give):
    parts, lines, _ = spectra.shape
    panel = flat((near, far))
    for g, here, there in row_tiles(columns.shape[2]):
        total = spectra[:, :, there].reshape(parts * lines, -1) + nt(panel, columns[g, 1, here, :])
        total = total * total
        power = total[:lines] + total[lines:]
        sums = [jnp.sum(power * weights[:, k : k + 1], axis=0, keepdims=True) for k in range(4)]
        (give if g else keep)[:, here] = jnp.concatenate(sums + sums, axis=0)


def paired_shards(n_mode, panels, shapes, harmonic, connect, recovery, *, steps):
    tie = lax.optimization_barrier
    core = lax.axis_index("mode") % 2
    layers = n_mode // 4
    ring = lambda a: lax.ppermute(a, "mode", [(i, (i + 4) % n_mode) for i in range(n_mode)])
    across = lambda a: lax.ppermute(a, "mode", [(i, i ^ 2) for i in range(n_mode)])
    mate = lambda a: lax.ppermute(a, "mode", [(i, i ^ 1) for i in range(n_mode)])
    peer = lambda a: lax.ppermute(a, "node", [(0, 1), (1, 0)])

    parts, both_lines, modes = panels.shape
    lines = both_lines // 2
    rows = shapes.shape[0]
    elems = connect.shape[0]

    mine = lax.dynamic_slice(panels, (0, core * lines, 0), (parts, lines, modes))
    theirs = lax.dynamic_slice(panels, (0, (1 - core) * lines, 0), (parts, lines, modes))
    z = [[mine], [mate(theirs)]]
    x = [[], []]
    both = (shapes, mate(shapes))
    out = [((2 * steps, 2 * lines), BF16), ((lines, 8), F32)]
    table, weights = on_chip(table_body, out, [harmonic.reshape(1, -1)], "table", flops=5 * 10**9)
    z[1][0], table, weights = tie((z[1][0], table, weights))

    spectra = None
    for s in range(layers - 1):
        for h in range(2):
            swapped = across(z[h][-1])
            moved = ring(z[h][-1])
            if s == 0 and h == 0:
                moved, swapped = tie((moved, swapped))
                blocks, wanted = [z[0][0], z[1][0]], [(0, 0, 0), (0, 0, 1)]
                spectra = add_spectra(n_mode, blocks, wanted, both, None)
            elif s == 1 and h == 0:
                moved, swapped, spectra, connect, recovery = tie(
                    (moved, swapped, spectra, connect, recovery)
                )
                packed = jnp.stack([connect.astype(F32).T, recovery.T])
                pairs = [packed, peer(packed), mate(packed)]
                pairs.append(mate(pairs[1]))
            elif s == 1 and h == 1:
                moved, swapped, spectra, pairs = tie((moved, swapped, spectra, pairs))
                out = [((8 * elems, rows), BF16), ((8 * elems, 2 * modes), BF16)]
                out.append(((2, 2, rows, modes), BF16))
                wanted = [(layers - 1, 1, 0), (layers - 1, 1, 1)]
                body = functools.partial(weights_body, n_mode, wanted)
                w, v, columns = on_chip(
                    body, out, pairs, "weights", both, 2, modes, keep_columns=True
                )
            elif s == 2 and h == 0:
                moved, swapped, spectra, w, v, columns = tie((moved, swapped, spectra, w, v, columns))
            else:
                moved, swapped, spectra = tie((moved, swapped, spectra))
            z[h].append(moved)
            x[h].append(swapped)
            wanted = [(s, 1, h), (s + 1, 0, h)]
            spectra = add_spectra(n_mode, [swapped, moved], wanted, both, spectra)
    cut = lines * 18 // 32
    ends = [(across(z[h][-1][:, :cut]), ring(x[h][-1][:, cut:])) for h in range(2)]
    w, v, columns, table = [pinned(a) for a in (w, v, columns, table)]
    out = [((4 * elems, steps), F32)]
    (stress,) = on_chip(stress_body, out, [pinned(spectra), w, table], "first_stress")
    ends[0], stress, spectra = tie((ends[0], stress, spectra))
    out.insert(0, (spectra.shape, F32))
    operands = [*ends[0], v, columns, table, pinned(spectra), pinned(stress)]
    spectra, stress = on_chip(half_body, out, operands, "half_stress", aliases={5: 0, 6: 1}, flops=5 * 10**9)
    ends[1], stress, spectra = tie((ends[1], stress, spectra))
    out = [((2 * elems, steps), F32)] * 2
    keep, give = on_chip(last_body, out, [*ends[1], v, table, pinned(stress)], "last_stress")
    give, spectra = tie((give, spectra))
    got = mate(give)
    out = [((8, rows), F32)] * 2
    operands = [*ends[1], columns, pinned(spectra), pinned(weights)]
    keep_m, give_m = on_chip(moment_body, out, operands, "moments")
    send = (keep[elems:] + got[elems:]).astype(BF16)
    half = keep_m + mate(give_m)
    stress = (keep[:elems] + got[:elems]) + peer(send).astype(F32)
    moments = half + peer(half)
    start = lax.axis_index("node") * (rows // 2)
    return stress, lax.dynamic_slice(moments, (0, start), (4, rows // 2))


def plain_shards(panels, shapes, harmonic, connect, recovery, *, steps, total_lines):
    highest = lax.Precision.HIGHEST
    rows_mode = shapes.shape[0]
    spectra = jnp.einsum(
        "cfm,rm->cfr",
        lax.all_gather(panels, "mode", axis=2, tiled=True),
        shapes,
        preferred_element_type=F32,
    )
    step_ids = jnp.arange(steps, dtype=jnp.int32)
    phases = harmonic[:, None] * step_ids[None, :] % HARM
    angles = phases.astype(F32) * (2.0 * math.pi / HARM)
    weights = moment_weights(harmonic, total_lines)
    history = jnp.einsum("fr,ft->rt", spectra[0], jnp.cos(angles), precision=highest)
    history = history - jnp.einsum("fr,ft->rt", spectra[1], jnp.sin(angles), precision=highest)
    power = spectra[0] * spectra[0] + spectra[1] * spectra[1]
    history = math.sqrt(2.0 / total_lines) * history
    moments = jnp.dot(weights, power, precision=highest)
    history = lax.psum_scatter(history, "node", scatter_dimension=0, tiled=True)
    moments = lax.psum_scatter(moments, "node", scatter_dimension=1, tiled=True)
    rows_in = lax.all_gather(history.astype(BF16), "node", axis=0, tiled=True)
    local = connect - lax.axis_index("mode") * rows_mode
    slots = jnp.arange(rows_mode, dtype=jnp.int32)
    hit = local[:, :, None] == slots[None, None, :]
    weight = jnp.sum(jnp.where(hit, recovery[:, :, None], 0.0), axis=1)
    stress = jnp.dot(weight, rows_in, preferred_element_type=F32, precision=highest)
    return stress, moments


STEPS = 512


def solution(mesh):
    n_mode, n_node = mesh.shape["mode"], mesh.shape["node"]

    def shards(panels, *rest):
        if n_node == 2 and n_mode % 4 == 0 and n_mode >= 8:
            return paired_shards(n_mode, panels, *rest, steps=STEPS)
        return plain_shards(panels, *rest, steps=STEPS, total_lines=panels.shape[1] * n_node)

    return jax.shard_map(
        shards,
        mesh=mesh,
        in_specs=(
            P(None, "node", "mode"),
            P("mode", None),
            P("node"),
            P(("mode", "node"), None),
            P(("mode", "node"), None),
        ),
        out_specs=(P(("mode", "node"), None), P(None, ("mode", "node"))),
        check_vma=False,
    )
```

time: 104 us -> 98.7 us (0.949)
  waiting for transfers between devices: 38.5 us -> 50.1 us
  Pallas kernels: 36.8 us -> 28.2 us
  starting transfers between devices: 19.4 us -> 15.8 us
  other arithmetic: 3.62 us -> 1.39 us
  local copies, waits for them, and re-layouts: 4.23 us -> 2.04 us
    pallas_call x13, Pallas kernels: 36.8 us -> 28.2 us  [on_chip(): pl.pallas_call(body, out_shape=outs, in_specs=[HBM] * len(both) + [VMEM]...]
    ppermute x8, waiting for transfers between devices: 15.6 us -> 23.4 us  [paired_shards(): lax.ppermute(a, 'mode', [(i, (i + 4) % n_mode) for i in range(n_mode)])]
    ppermute x8, starting transfers between devices: 10.9 us -> 6.56 us  [paired_shards(): lax.ppermute(a, 'mode', [(i, i ^ 2) for i in range(n_mode)])]
    unnamed x4 -> x8, local copies, waits for them, and re-layouts: 2.87 us -> 0.7 us
    ppermute x8, waiting for transfers between devices: 18.5 us -> 20.3 us  [paired_shards(): lax.ppermute(a, 'mode', [(i, i ^ 2) for i in range(n_mode)])]
    ppermute x3, waiting for transfers between devices: 3.69 us -> 5.21 us  [paired_shards(): peer = lambda a: lax.ppermute(a, 'node', [(0, 1), (1, 0)])]
    another operation x2, other arithmetic: 1.38 us -> 0.01 us  [paired_shards(): packed = jnp.stack([connect.astype(F32).T, recovery.T])]
  transfers between devices with their start and end apart: 25 -> 25, of which waited for: 13 -> 15; matrix products, arithmetic and copies ran while one was open for 3% -> 2% of each run, Pallas kernels for 33% -> 27%
where the time goes in v4:
time: 98.7 us; the launch traced here: 98.4 us
  waiting for transfers between devices  50.1 us (51%)
  Pallas kernels  28.2 us (29%)
  starting transfers between devices  15.8 us (16%)
  local copies, waits for them, and re-layouts  2.04 us (2%)
  other arithmetic  1.39 us (1%)
    pallas_call x13, Pallas kernels, on_chip(): pl.pallas_call(body, out_shape=outs, in_specs=[HBM] * len(both) + [VMEM]...  28.2 us
    ppermute x8, waiting for transfers between devices, paired_shards(): lax.ppermute(a, 'mode', [(i, (i + 4) % n_mode) for i in range(n_mode)])  23.4 us
    ppermute x8, waiting for transfers between devices, paired_shards(): lax.ppermute(a, 'mode', [(i, i ^ 2) for i in range(n_mode)])  20.3 us
    ppermute x8, starting transfers between devices, paired_shards(): lax.ppermute(a, 'mode', [(i, i ^ 2) for i in range(n_mode)])  6.56 us
    ppermute x3, waiting for transfers between devices, paired_shards(): peer = lambda a: lax.ppermute(a, 'node', [(0, 1), (1, 0)])  5.21 us
    ppermute x3, starting transfers between devices, paired_shards(): peer = lambda a: lax.ppermute(a, 'node', [(0, 1), (1, 0)])  4.29 us
    ppermute x8, starting transfers between devices, paired_shards(): lax.ppermute(a, 'mode', [(i, (i + 4) % n_mode) for i in range(n_mode)])  3.62 us
  transfers between devices with their start and end apart: 25, of which 15 were waited for; matrix products, arithmetic and copies ran while one was open for 2% of the time, Pallas kernels for 27%

profile of v4, /device:TPU:0, one launch (start us, length us, event | category | flops | bytes accessed | tf_op | source)
XLA Modules:
  0.0 98.4 jit_solution(13733853174946524154)
XLA Ops:
  2.5 2.9 %collective-permute-start.5 = (bf16[2,512,256]{2,1,0:T(8,128)(2,1)S(1)}, bf16[2,512,256]{2,1,0:T(8,128)(2,1)S(1)}, u32[]{:S(2)}, u32[]{:S(2)}) collective-permute-start(bf16[2,512,256]{2,1,0:T(8,128)(2,1)S(1)} %get-tuple-element.102.refs_0_), channel_id=1, source_target_pairs={{0,4},{2,6},{4,0},{6,2},{8,12},{10,14},{12,8},{14,10},{16,20},{18,... | collective-permute-start | bytes 1572872 | tf_op jit(solution)/shard_map/ppermute | solution.py:248
  5.5 1.6 %collective-permute-start.4 = (bf16[2,512,256]{2,1,0:T(8,128)(2,1)S(1)}, bf16[2,512,256]{2,1,0:T(8,128)(2,1)S(1)}, u32[]{:S(2)}, u32[]{:S(2)}) collective-permute-start(bf16[2,512,256]{2,1,0:T(8,128)(2,1)S(1)} %get-tuple-element.102.refs_0_), channel_id=1, source_target_pairs={{0,8},{2,10},{4,12},{6,14},{8,16},{10,18},{12,20},{14,22},{16,24},... | collective-permute-start | bytes 1572872 | tf_op jit(solution)/shard_map/ppermute | solution.py:247
  7.7 2.0 %table.1 = (bf16[1024,1024]{1,0:T(8,128)(2,1)S(1)}, f32[512,8]{1,0:T(8,128)S(1)}) custom-call(s32[1,1024]{1,0:T(1,128)S(1)} %bitcast.8), custom_call_target="tpu_custom_call" | custom-call | flops 5000000000 | bytes 1000 | tf_op jit(solution)/shard_map/table/pallas_call | solution.py:50
  9.8 1.8 %collective-permute-start.2 = (bf16[2,512,256]{2,1,0:T(8,128)(2,1)S(1)}, bf16[2,512,256]{2,1,0:T(8,128)(2,1)S(1)}, u32[]{:S(2)}, u32[]{:S(2)}) collective-permute-start(bf16[2,512,256]{2,1,0:T(8,128)(2,1)S(1)} %collective-permute-done.refs_1_), channel_id=1, source_target_pairs={{0,4},{2,6},{4,0},{6,2},{8,12},{10,14},{12,8},{14,10},{16,20},{18,... | collective-permute-start | bytes 1572872 | tf_op jit(solution)/shard_map/ppermute | solution.py:248
  11.5 1.6 %collective-permute-start.1 = (bf16[2,512,256]{2,1,0:T(8,128)(2,1)S(1)}, bf16[2,512,256]{2,1,0:T(8,128)(2,1)S(1)}, u32[]{:S(2)}, u32[]{:S(2)}) collective-permute-start(bf16[2,512,256]{2,1,0:T(8,128)(2,1)S(1)} %collective-permute-done.refs_1_), channel_id=1, source_target_pairs={{0,8},{2,10},{4,12},{6,14},{8,16},{10,18},{12,20},{14,22},{16,24},... | collective-permute-start | bytes 1572872 | tf_op jit(solution)/shard_map/ppermute | solution.py:247
  13.1 5.1 %collective-permute-done.5.refs_0_ = bf16[2,512,256]{2,1,0:T(8,128)(2,1)S(1)} collective-permute-done((bf16[2,512,256]{2,1,0:T(8,128)(2,1)S(1)}, bf16[2,512,256]{2,1,0:T(8,128)(2,1)S(1)}, u32[]{:S(2)}, u32[]{:S(2)}) %collective-permute-start.5) | collective-permute-done | bytes 524320 | tf_op jit(solution)/shard_map/ppermute | solution.py:248
  18.2 3.9 %collective-permute-done.4.refs_1_ = bf16[2,512,256]{2,1,0:T(8,128)(2,1)S(1)} collective-permute-done((bf16[2,512,256]{2,1,0:T(8,128)(2,1)S(1)}, bf16[2,512,256]{2,1,0:T(8,128)(2,1)S(1)}, u32[]{:S(2)}, u32[]{:S(2)}) %collective-permute-start.4) | collective-permute-done | bytes 524320 | tf_op jit(solution)/shard_map/ppermute | solution.py:247
  22.4 1.9 %add_spectra.7.refs_2_ = f32[2,512,1024]{2,1,0:T(8,128)S(1)} custom-call(bf16[512,4096]{1,0:T(8,128)(2,1)S(1)} %copy-done, bf16[512,4096]{1,0:T(8,128)(2,1)} %collective-permute-done.3.other, bf16[2,512,256]{2,1,0:T(8,128)(2,1)S(1)} %get-tuple-element.102.refs_0_, bf16[2,512,256]{2,1,0:T(8,128)(2,1)S(1)} %collective-permute-done.refs_1_), custom_call_target="tpu_custom_call" | custom-call | flops 1000 | bytes 1000 | tf_op jit(solution)/shard_map/add_spectra/pallas_call | solution.py:50
  24.3 1.9 %add_spectra.8.refs_2_ = f32[2,512,1024]{2,1,0:T(8,128)S(1)} custom-call(bf16[512,4096]{1,0:T(8,128)(2,1)S(1)} %copy-done, bf16[512,4096]{1,0:T(8,128)(2,1)} %collective-permute-done.3.other, bf16[2,512,256]{2,1,0:T(8,128)(2,1)S(1)} %collective-permute-done.5.refs_0_, ...), custom_call_target="tpu_custom_call", output_to_operand_aliasing={{}: (4, {})} | custom-call | flops 1000 | bytes 1000 | tf_op jit(solution)/shard_map/add_spectra/pallas_call | solution.py:50
  26.2 3.2 %collective-permute-done.2.refs_0_ = bf16[2,512,256]{2,1,0:T(8,128)(2,1)S(1)} collective-permute-done((bf16[2,512,256]{2,1,0:T(8,128)(2,1)S(1)}, bf16[2,512,256]{2,1,0:T(8,128)(2,1)S(1)}, u32[]{:S(2)}, u32[]{:S(2)}) %collective-permute-start.2) | collective-permute-done | bytes 524320 | tf_op jit(solution)/shard_map/ppermute | solution.py:248
  29.4 3.9 %collective-permute-done.1.refs_1_ = bf16[2,512,256]{2,1,0:T(8,128)(2,1)S(1)} collective-permute-done((bf16[2,512,256]{2,1,0:T(8,128)(2,1)S(1)}, bf16[2,512,256]{2,1,0:T(8,128)(2,1)S(1)}, u32[]{:S(2)}, u32[]{:S(2)}) %collective-permute-start.1) | collective-permute-done | bytes 524320 | tf_op jit(solution)/shard_map/ppermute | solution.py:247
  33.6 1.9 %add_spectra.9.refs_2_ = f32[2,512,1024]{2,1,0:T(8,128)S(1)} custom-call(bf16[512,4096]{1,0:T(8,128)(2,1)S(1)} %copy-done, bf16[512,4096]{1,0:T(8,128)(2,1)} %collective-permute-done.3.other, bf16[2,512,256]{2,1,0:T(8,128)(2,1)S(1)} %collective-permute-done.2.refs_0_, ...), custom_call_target="tpu_custom_call", output_to_operand_aliasing={{}: (4, {})} | custom-call | flops 1000 | bytes 1000 | tf_op jit(solution)/shard_map/add_spectra/pallas_call | solution.py:50
  35.5 5.2 %collective-permute-done.9.refs_0_ = bf16[2,512,256]{2,1,0:T(8,128)(2,1)S(1)} collective-permute-done((bf16[2,512,256]{2,1,0:T(8,128)(2,1)S(1)}, bf16[2,512,256]{2,1,0:T(8,128)(2,1)S(1)}, u32[]{:S(2)}, u32[]{:S(2)}) %collective-permute-start.9) | collective-permute-done | bytes 524320 | tf_op jit(solution)/shard_map/ppermute | solution.py:248
  40.7 3.9 %collective-permute-done.8.refs_1_ = bf16[2,512,256]{2,1,0:T(8,128)(2,1)S(1)} collective-permute-done((bf16[2,512,256]{2,1,0:T(8,128)(2,1)S(1)}, bf16[2,512,256]{2,1,0:T(8,128)(2,1)S(1)}, u32[]{:S(2)}, u32[]{:S(2)}) %collective-permute-start.8) | collective-permute-done | bytes 524320 | tf_op jit(solution)/shard_map/ppermute | solution.py:247
  46.1 1.7 %collective-permute-start.10 = (f32[2,8,128]{2,1,0:T(8,128)S(1)}, f32[2,8,128]{2,1,0:T(8,128)S(1)}, u32[]{:S(2)}, u32[]{:S(2)}) collective-permute-start(f32[2,8,128]{2,1,0:T(8,128)S(1)} %pad_maximum_fusion.refs_0_), channel_id=1, source_target_pairs={{0,1},{1,0},{2,3},{3,2},{4,5},{5,4},{6,7},{7,6},{8,9},{9,8},{10,11... | collective-permute-start | bytes 24584 | tf_op jit(solution)/shard_map/ppermute | solution.py:250
  47.9 1.9 %collective-permute-done.10.refs_1_ = f32[2,8,128]{2,1,0:T(8,128)S(1)} collective-permute-done((f32[2,8,128]{2,1,0:T(8,128)S(1)}, f32[2,8,128]{2,1,0:T(8,128)S(1)}, u32[]{:S(2)}, u32[]{:S(2)}) %collective-permute-start.10) | collective-permute-done | bytes 8224 | tf_op jit(solution)/shard_map/ppermute | solution.py:250
  49.8 1.9 %add_spectra.10.refs_2_ = f32[2,512,1024]{2,1,0:T(8,128)S(1)} custom-call(bf16[512,4096]{1,0:T(8,128)(2,1)S(1)} %copy-done, bf16[512,4096]{1,0:T(8,128)(2,1)} %collective-permute-done.3.other, bf16[2,512,256]{2,1,0:T(8,128)(2,1)S(1)} %collective-permute-done.9.refs_0_, ...), custom_call_target="tpu_custom_call", output_to_operand_aliasing={{}: (4, {})} | custom-call | flops 1000 | bytes 1000 | tf_op jit(solution)/shard_map/add_spectra/pallas_call | solution.py:50
  51.9 3.9 %collective-permute-done.6.refs_1_ = bf16[2,512,256]{2,1,0:T(8,128)(2,1)S(1)} collective-permute-done((bf16[2,512,256]{2,1,0:T(8,128)(2,1)S(1)}, bf16[2,512,256]{2,1,0:T(8,128)(2,1)S(1)}, u32[]{:S(2)}, u32[]{:S(2)}) %collective-permute-start.6) | collective-permute-done | bytes 524320 | tf_op jit(solution)/shard_map/ppermute | solution.py:247
  56.1 1.9 %add_spectra.11.refs_2_ = f32[2,512,1024]{2,1,0:T(8,128)S(1)} custom-call(bf16[512,4096]{1,0:T(8,128)(2,1)S(1)} %copy-done, bf16[512,4096]{1,0:T(8,128)(2,1)} %collective-permute-done.3.other, bf16[2,512,256]{2,1,0:T(8,128)(2,1)S(1)} %collective-permute-done.7.refs_0_, ...), custom_call_target="tpu_custom_call", output_to_operand_aliasing={{}: (4, {})} | custom-call | flops 1000 | bytes 1000 | tf_op jit(solution)/shard_map/add_spectra/pallas_call | solution.py:50
  58.0 3.5 %weights.1 = (bf16[1024,512]{1,0:T(8,128)(2,1)S(1)}, bf16[1024,512]{1,0:T(8,128)(2,1)S(1)}, bf16[2,2,512,256]{3,2,1,0:T(8,128)(2,1)S(1)}) custom-call(bf16[512,4096]{1,0:T(8,128)(2,1)S(1)} %copy-done, bf16[512,4096]{1,0:T(8,128)(2,1)} %collective-permute-done.3.other, f32[2,8,128]{2,1,0:T(8,128)S(1)} %pad_maximum_fusion.refs_0_, ...), custom_call_target="tpu_custom_call" | custom-call | flops 1000 | bytes 1000 | tf_op jit(solution)/shard_map/weights/pallas_call | solution.py:50
  61.5 1.6 %collective-permute-done.16.refs_0_ = bf16[2,512,256]{2,1,0:T(8,128)(2,1)S(1)} collective-permute-done((bf16[2,512,256]{2,1,0:T(8,128)(2,1)S(1)}, bf16[2,512,256]{2,1,0:T(8,128)(2,1)S(1)}, u32[]{:S(2)}, u32[]{:S(2)}) %collective-permute-start.16) | collective-permute-done | bytes 524320 | tf_op jit(solution)/shard_map/ppermute | solution.py:248
  63.1 3.9 %collective-permute-done.15.refs_1_ = bf16[2,512,256]{2,1,0:T(8,128)(2,1)S(1)} collective-permute-done((bf16[2,512,256]{2,1,0:T(8,128)(2,1)S(1)}, bf16[2,512,256]{2,1,0:T(8,128)(2,1)S(1)}, u32[]{:S(2)}, u32[]{:S(2)}) %collective-permute-start.15) | collective-permute-done | bytes 524320 | tf_op jit(solution)/shard_map/ppermute | solution.py:247
  67.5 1.9 %add_spectra.12.refs_2_ = f32[2,512,1024]{2,1,0:T(8,128)S(1)} custom-call(bf16[512,4096]{1,0:T(8,128)(2,1)S(1)} %copy-done, bf16[512,4096]{1,0:T(8,128)(2,1)} %collective-permute-done.3.other, bf16[2,512,256]{2,1,0:T(8,128)(2,1)S(1)} %collective-permute-done.16.refs_0_, ...), custom_call_target="tpu_custom_call", output_to_operand_aliasing={{}: (4, {})} | custom-call | flops 1000 | bytes 1000 | tf_op jit(solution)/shard_map/add_spectra/pallas_call | solution.py:50
  69.4 5.0 %collective-permute-done.14.refs_0_ = bf16[2,512,256]{2,1,0:T(8,128)(2,1)S(1)} collective-permute-done((bf16[2,512,256]{2,1,0:T(8,128)(2,1)S(1)}, bf16[2,512,256]{2,1,0:T(8,128)(2,1)S(1)}, u32[]{:S(2)}, u32[]{:S(2)}) %collective-permute-start.14) | collective-permute-done | bytes 524320 | tf_op jit(solution)/shard_map/ppermute | solution.py:248
  74.4 3.9 %collective-permute-done.13.refs_1_ = bf16[2,512,256]{2,1,0:T(8,128)(2,1)S(1)} collective-permute-done((bf16[2,512,256]{2,1,0:T(8,128)(2,1)S(1)}, bf16[2,512,256]{2,1,0:T(8,128)(2,1)S(1)}, u32[]{:S(2)}, u32[]{:S(2)}) %collective-permute-start.13) | collective-permute-done | bytes 524320 | tf_op jit(solution)/shard_map/ppermute | solution.py:247
  78.9 1.9 %add_spectra.13.spectra = f32[2,512,1024]{2,1,0:T(8,128)S(1)} custom-call(bf16[512,4096]{1,0:T(8,128)(2,1)S(1)} %copy-done, bf16[512,4096]{1,0:T(8,128)(2,1)} %collective-permute-done.3.other, bf16[2,512,256]{2,1,0:T(8,128)(2,1)S(1)} %collective-permute-done.14.refs_0_, ...), custom_call_target="tpu_custom_call", output_to_operand_aliasing={{}: (4, {})} | custom-call | flops 1000 | bytes 1000 | tf_op jit(solution)/shard_map/add_spectra/pallas_call | solution.py:50
  80.8 3.5 %first_stress.1.stress = f32[512,512]{1,0:T(8,128)S(1)} custom-call(f32[2,512,1024]{2,1,0:T(8,128)S(1)} %add_spectra.13.spectra, bf16[1024,512]{1,0:T(8,128)(2,1)S(1)} %get-tuple-element.81.w, bf16[1024,1024]{1,0:T(8,128)(2,1)S(1)} %get-tuple-element.82.table), custom_call_target="tpu_custom_call" | custom-call | flops 1000 | bytes 1000 | tf_op jit(solution)/shard_map/first_stress/pallas_call | solution.py:50
  84.3 2.7 %half_stress.1 = (f32[2,512,1024]{2,1,0:T(8,128)S(1)}, f32[512,512]{1,0:T(8,128)S(1)}) custom-call(bf16[2,288,256]{2,1,0:T(8,128)(2,1)S(1)} %collective-permute-done.19.near, bf16[2,224,256]{2,1,0:T(8,128)(2,1)S(1)} %collective-permute-done.20.far, bf16[1024,512]{1,0:T(8,128)(2,1)S(1)} %get-tuple-element.85.v, ...), custom_call_target="tpu_custom_call", output_to_operand_aliasing={{0}: (5, {}), {1}: (6, {})} | custom-call | flops 5000000000 | bytes 1000 | tf_op jit(solution)/shard_map/half_stress/pallas_call | solution.py:50
  87.0 2.0 %last_stress.1 = (f32[256,512]{1,0:T(8,128)S(1)}, f32[256,512]{1,0:T(8,128)S(1)}) custom-call(bf16[2,288,256]{2,1,0:T(8,128)(2,1)S(1)} %collective-permute-done.17.near, bf16[2,224,256]{2,1,0:T(8,128)(2,1)S(1)} %collective-permute-done.18.far, bf16[1024,512]{1,0:T(8,128)(2,1)S(1)} %get-tuple-element.85.v, bf16[1024,1024]{1,0:T(8,128)(2,1)S(1)} %get-tuple-element.82.table, ...), custom_call_target="tpu_custom_call" | custom-call | flops 1000 | bytes 1000 | tf_op jit(solution)/shard_map/last_stress/pallas_call | solution.py:50
  89.0 1.5 %moments.1 = (f32[8,512]{1,0:T(8,128)S(1)}, f32[8,512]{1,0:T(8,128)S(1)}) custom-call(bf16[2,288,256]{2,1,0:T(8,128)(2,1)S(1)} %collective-permute-done.17.near, bf16[2,224,256]{2,1,0:T(8,128)(2,1)S(1)} %collective-permute-done.18.far, bf16[2,2,512,256]{3,2,1,0:T(8,128)(2,1)S(1)} %get-tuple-element.86.columns, ...), custom_call_target="tpu_custom_call" | custom-call | flops 1000 | bytes 1000 | tf_op jit(solution)/shard_map/moments/pallas_call | solution.py:50
  91.2 1.8 %collective-permute-start.22 = (bf16[128,512]{1,0:T(8,128)(2,1)S(1)}, bf16[128,512]{1,0:T(8,128)(2,1)S(1)}, u32[]{:S(2)}, u32[]{:S(2)}) collective-permute-start(bf16[128,512]{1,0:T(8,128)(2,1)S(1)} %fusion), channel_id=1, source_target_pairs={{0,1},{1,0},{2,3},{3,2},{4,5},{5,4},{6,7},{7,6},{8,9},{9,8},{10,11... | collective-permute-start | bytes 393224 | tf_op jit(solution)/shard_map/ppermute | solution.py:250
  93.7 3.3 %collective-permute-done.24 = f32[8,512]{1,0:T(8,128)S(1)} collective-permute-done((f32[8,512]{1,0:T(8,128)S(1)}, f32[8,512]{1,0:T(8,128)S(1)}, u32[]{:S(2)}, u32[]{:S(2)}) %collective-permute-start.24) | collective-permute-done | bytes 16416 | tf_op jit(solution)/shard_map/ppermute | solution.py:250
  (50 shorter events, 9.3 us)
Async XLA Ops:
  0.6 21.8 %collective-permute-start.3 = (bf16[512,4096]{1,0:T(8,128)(2,1)}, bf16[512,4096]{1,0:T(8,128)(2,1)}, u32[]{:S(2)}, u32[]{:S(2)}) collective-permute-start(bf16[512,4096]{1,0:T(8,128)(2,1)} %own.15), channel_id=1, source_target_pairs={{0,2},{2,0},{4,6},{6,4},{8,10},{10,8},{12,14},{14,12},{16,18},{18,... | collective-permute-start | bytes 12582920 | tf_op jit(solution)/shard_map/ppermute | solution.py:249
  2.4 7.3 %collective-permute-start = (bf16[2,512,256]{2,1,0:T(8,128)(2,1)S(1)}, bf16[2,512,256]{2,1,0:T(8,128)(2,1)S(1)}, u32[]{:S(2)}, u32[]{:S(2)}) collective-permute-start(bf16[2,512,256]{2,1,0:T(8,128)(2,1)S(1)} %get-tuple-element.103), channel_id=1, source_target_pairs={{0,2},{2,0},{4,6},{6,4},{8,10},{10,8},{12,14},{14,12},{16,18},{18,... | collective-permute-start | bytes 1572872 | tf_op jit(solution)/shard_map/ppermute | solution.py:249
  2.5 15.7 %collective-permute-start.5 = (bf16[2,512,256]{2,1,0:T(8,128)(2,1)S(1)}, bf16[2,512,256]{2,1,0:T(8,128)(2,1)S(1)}, u32[]{:S(2)}, u32[]{:S(2)}) collective-permute-start(bf16[2,512,256]{2,1,0:T(8,128)(2,1)S(1)} %get-tuple-element.102.refs_0_), channel_id=1, source_target_pairs={{0,4},{2,6},{4,0},{6,2},{8,12},{10,14},{12,8},{14,10},{16,20},{18,... | collective-permute-start | bytes 1572872 | tf_op jit(solution)/shard_map/ppermute | solution.py:248
  5.5 16.6 %collective-permute-start.4 = (bf16[2,512,256]{2,1,0:T(8,128)(2,1)S(1)}, bf16[2,512,256]{2,1,0:T(8,128)(2,1)S(1)}, u32[]{:S(2)}, u32[]{:S(2)}) collective-permute-start(bf16[2,512,256]{2,1,0:T(8,128)(2,1)S(1)} %get-tuple-element.102.refs_0_), channel_id=1, source_target_pairs={{0,8},{2,10},{4,12},{6,14},{8,16},{10,18},{12,20},{14,22},{16,24},... | collective-permute-start | bytes 1572872 | tf_op jit(solution)/shard_map/ppermute | solution.py:247
  7.1 0.7 copy-start.1
  7.7 14.7 %copy-start = (bf16[512,4096]{1,0:T(8,128)(2,1)S(1)}, bf16[512,4096]{1,0:T(8,128)(2,1)}, u32[]{:S(2)}) copy-start(bf16[512,4096]{1,0:T(8,128)(2,1)} %own.15) | copy-start | bytes 12582916
  9.8 19.7 %collective-permute-start.2 = (bf16[2,512,256]{2,1,0:T(8,128)(2,1)S(1)}, bf16[2,512,256]{2,1,0:T(8,128)(2,1)S(1)}, u32[]{:S(2)}, u32[]{:S(2)}) collective-permute-start(bf16[2,512,256]{2,1,0:T(8,128)(2,1)S(1)} %collective-permute-done.refs_1_), channel_id=1, source_target_pairs={{0,4},{2,6},{4,0},{6,2},{8,12},{10,14},{12,8},{14,10},{16,20},{18,... | collective-permute-start | bytes 1572872 | tf_op jit(solution)/shard_map/ppermute | solution.py:248
  11.5 21.8 %collective-permute-start.1 = (bf16[2,512,256]{2,1,0:T(8,128)(2,1)S(1)}, bf16[2,512,256]{2,1,0:T(8,128)(2,1)S(1)}, u32[]{:S(2)}, u32[]{:S(2)}) collective-permute-start(bf16[2,512,256]{2,1,0:T(8,128)(2,1)S(1)} %collective-permute-done.refs_1_), channel_id=1, source_target_pairs={{0,8},{2,10},{4,12},{6,14},{8,16},{10,18},{12,20},{14,22},{16,24},... | collective-permute-start | bytes 1572872 | tf_op jit(solution)/shard_map/ppermute | solution.py:247
  22.1 18.6 %collective-permute-start.9 = (bf16[2,512,256]{2,1,0:T(8,128)(2,1)S(1)}, bf16[2,512,256]{2,1,0:T(8,128)(2,1)S(1)}, u32[]{:S(2)}, u32[]{:S(2)}) collective-permute-start(bf16[2,512,256]{2,1,0:T(8,128)(2,1)S(1)} %collective-permute-done.4.refs_1_), channel_id=1, source_target_pairs={{0,4},{2,6},{4,0},{6,2},{8,12},{10,14},{12,8},{14,10},{16,20},{18,... | collective-permute-start | bytes 1572872 | tf_op jit(solution)/shard_map/ppermute | solution.py:248
  22.4 22.2 %collective-permute-start.8 = (bf16[2,512,256]{2,1,0:T(8,128)(2,1)S(1)}, bf16[2,512,256]{2,1,0:T(8,128)(2,1)S(1)}, u32[]{:S(2)}, u32[]{:S(2)}) collective-permute-start(bf16[2,512,256]{2,1,0:T(8,128)(2,1)S(1)} %collective-permute-done.4.refs_1_), channel_id=1, source_target_pairs={{0,8},{2,10},{4,12},{6,14},{8,16},{10,18},{12,20},{14,22},{16,24},... | collective-permute-start | bytes 1572872 | tf_op jit(solution)/shard_map/ppermute | solution.py:247
  26.2 18.7 %copy-start.2 = (s32[128,8]{0,1:T(8,128)S(1)}, s32[128,8]{0,1:T(8,128)}, u32[]{:S(2)}) copy-start(s32[128,8]{0,1:T(8,128)} %param.8) | copy-start | bytes 12292
  26.2 18.7 %copy-start.3 = (f32[128,8]{0,1:T(8,128)S(1)}, f32[128,8]{0,1:T(8,128)}, u32[]{:S(2)}) copy-start(f32[128,8]{0,1:T(8,128)} %param.9) | copy-start | bytes 12292
  33.3 18.6 %collective-permute-start.7 = (bf16[2,512,256]{2,1,0:T(8,128)(2,1)S(1)}, bf16[2,512,256]{2,1,0:T(8,128)(2,1)S(1)}, u32[]{:S(2)}, u32[]{:S(2)}) collective-permute-start(bf16[2,512,256]{2,1,0:T(8,128)(2,1)S(1)} %collective-permute-done.1.refs_1_), channel_id=1, source_target_pairs={{0,4},{2,6},{4,0},{6,2},{8,12},{10,14},{12,8},{14,10},{16,20},{18,... | collective-permute-start | bytes 1572872 | tf_op jit(solution)/shard_map/ppermute | solution.py:248
  33.6 22.2 %collective-permute-start.6 = (bf16[2,512,256]{2,1,0:T(8,128)(2,1)S(1)}, bf16[2,512,256]{2,1,0:T(8,128)(2,1)S(1)}, u32[]{:S(2)}, u32[]{:S(2)}) collective-permute-start(bf16[2,512,256]{2,1,0:T(8,128)(2,1)S(1)} %collective-permute-done.1.refs_1_), channel_id=1, source_target_pairs={{0,8},{2,10},{4,12},{6,14},{8,16},{10,18},{12,20},{14,22},{16,24},... | collective-permute-start | bytes 1572872 | tf_op jit(solution)/shard_map/ppermute | solution.py:247
  44.6 18.6 %collective-permute-start.16 = (bf16[2,512,256]{2,1,0:T(8,128)(2,1)S(1)}, bf16[2,512,256]{2,1,0:T(8,128)(2,1)S(1)}, u32[]{:S(2)}, u32[]{:S(2)}) collective-permute-start(bf16[2,512,256]{2,1,0:T(8,128)(2,1)S(1)} %collective-permute-done.8.refs_1_), channel_id=1, source_target_pairs={{0,4},{2,6},{4,0},{6,2},{8,12},{10,14},{12,8},{14,10},{16,20},{18,... | collective-permute-start | bytes 1572872 | tf_op jit(solution)/shard_map/ppermute | solution.py:248
  44.8 22.2 %collective-permute-start.15 = (bf16[2,512,256]{2,1,0:T(8,128)(2,1)S(1)}, bf16[2,512,256]{2,1,0:T(8,128)(2,1)S(1)}, u32[]{:S(2)}, u32[]{:S(2)}) collective-permute-start(bf16[2,512,256]{2,1,0:T(8,128)(2,1)S(1)} %collective-permute-done.8.refs_1_), channel_id=1, source_target_pairs={{0,8},{2,10},{4,12},{6,14},{8,16},{10,18},{12,20},{14,22},{16,24},... | collective-permute-start | bytes 1572872 | tf_op jit(solution)/shard_map/ppermute | solution.py:247
  44.9 1.2 %collective-permute-start.11 = (f32[2,8,128]{2,1,0:T(8,128)S(1)}, f32[2,8,128]{2,1,0:T(8,128)S(1)}, u32[]{:S(2)}, u32[]{:S(2)}) collective-permute-start(f32[2,8,128]{2,1,0:T(8,128)S(1)} %pad_maximum_fusion.refs_0_), channel_id=1, source_target_pairs={{0,2},{2,0},{4,6},{6,4},{8,10},{10,8},{12,14},{14,12},{16,18},{18,... | collective-permute-start | bytes 24584 | tf_op jit(solution)/shard_map/ppermute | solution.py:249
  46.1 3.7 %collective-permute-start.10 = (f32[2,8,128]{2,1,0:T(8,128)S(1)}, f32[2,8,128]{2,1,0:T(8,128)S(1)}, u32[]{:S(2)}, u32[]{:S(2)}) collective-permute-start(f32[2,8,128]{2,1,0:T(8,128)S(1)} %pad_maximum_fusion.refs_0_), channel_id=1, source_target_pairs={{0,1},{1,0},{2,3},{3,2},{4,5},{5,4},{6,7},{7,6},{8,9},{9,8},{10,11... | collective-permute-start | bytes 24584 | tf_op jit(solution)/shard_map/ppermute | solution.py:250
  49.8 1.9 %collective-permute-start.12 = (f32[2,8,128]{2,1,0:T(8,128)S(1)}, f32[2,8,128]{2,1,0:T(8,128)S(1)}, u32[]{:S(2)}, u32[]{:S(2)}) collective-permute-start(f32[2,8,128]{2,1,0:T(8,128)S(1)} %collective-permute-done.10.refs_1_), channel_id=1, source_target_pairs={{0,2},{2,0},{4,6},{6,4},{8,10},{10,8},{12,14},{14,12},{16,18},{18,... | collective-permute-start | bytes 24584 | tf_op jit(solution)/shard_map/ppermute | solution.py:249
  55.8 18.6 %collective-permute-start.14 = (bf16[2,512,256]{2,1,0:T(8,128)(2,1)S(1)}, bf16[2,512,256]{2,1,0:T(8,128)(2,1)S(1)}, u32[]{:S(2)}, u32[]{:S(2)}) collective-permute-start(bf16[2,512,256]{2,1,0:T(8,128)(2,1)S(1)} %collective-permute-done.6.refs_1_), channel_id=1, source_target_pairs={{0,4},{2,6},{4,0},{6,2},{8,12},{10,14},{12,8},{14,10},{16,20},{18,... | collective-permute-start | bytes 1572872 | tf_op jit(solution)/shard_map/ppermute | solution.py:248
  56.1 22.2 %collective-permute-start.13 = (bf16[2,512,256]{2,1,0:T(8,128)(2,1)S(1)}, bf16[2,512,256]{2,1,0:T(8,128)(2,1)S(1)}, u32[]{:S(2)}, u32[]{:S(2)}) collective-permute-start(bf16[2,512,256]{2,1,0:T(8,128)(2,1)S(1)} %collective-permute-done.6.refs_1_), channel_id=1, source_target_pairs={{0,8},{2,10},{4,12},{6,14},{8,16},{10,18},{12,20},{14,22},{16,24},... | collective-permute-start | bytes 1572872 | tf_op jit(solution)/shard_map/ppermute | solution.py:247
  67.1 17.2 %collective-permute-start.19 = (bf16[2,288,256]{2,1,0:T(8,128)(2,1)S(1)}, bf16[2,288,256]{2,1,0:T(8,128)(2,1)S(1)}, u32[]{:S(2)}, u32[]{:S(2)}) collective-permute-start(bf16[2,288,256]{2,1,0:T(8,128)(2,1)S(1)} %slice.26), channel_id=1, source_target_pairs={{0,4},{2,6},{4,0},{6,2},{8,12},{10,14},{12,8},{14,10},{16,20},{18,... | collective-permute-start | bytes 884744 | tf_op jit(solution)/shard_map/ppermute | solution.py:248
  67.4 16.8 %collective-permute-start.20 = (bf16[2,224,256]{2,1,0:T(8,128)(2,1)S(1)}, bf16[2,224,256]{2,1,0:T(8,128)(2,1)S(1)}, u32[]{:S(2)}, u32[]{:S(2)}) collective-permute-start(bf16[2,224,256]{2,1,0:T(8,128)(2,1)S(1)} %slice.27), channel_id=1, source_target_pairs={{0,8},{2,10},{4,12},{6,14},{8,16},{10,18},{12,20},{14,22},{16,24},... | collective-permute-start | bytes 688136 | tf_op jit(solution)/shard_map/ppermute | solution.py:247
  78.3 8.7 %collective-permute-start.18 = (bf16[2,224,256]{2,1,0:T(8,128)(2,1)S(1)}, bf16[2,224,256]{2,1,0:T(8,128)(2,1)S(1)}, u32[]{:S(2)}, u32[]{:S(2)}) collective-permute-start(bf16[2,224,256]{2,1,0:T(8,128)(2,1)S(1)} %slice.25), channel_id=1, source_target_pairs={{0,8},{2,10},{4,12},{6,14},{8,16},{10,18},{12,20},{14,22},{16,24},... | collective-permute-start | bytes 688136 | tf_op jit(solution)/shard_map/ppermute | solution.py:247
  78.6 8.4 %collective-permute-start.17 = (bf16[2,288,256]{2,1,0:T(8,128)(2,1)S(1)}, bf16[2,288,256]{2,1,0:T(8,128)(2,1)S(1)}, u32[]{:S(2)}, u32[]{:S(2)}) collective-permute-start(bf16[2,288,256]{2,1,0:T(8,128)(2,1)S(1)} %slice.24), channel_id=1, source_target_pairs={{0,4},{2,6},{4,0},{6,2},{8,12},{10,14},{12,8},{14,10},{16,20},{18,... | collective-permute-start | bytes 884744 | tf_op jit(solution)/shard_map/ppermute | solution.py:248
  89.0 2.2 %collective-permute-start.21 = (f32[256,512]{1,0:T(8,128)S(1)}, f32[256,512]{1,0:T(8,128)S(1)}, u32[]{:S(2)}, u32[]{:S(2)}) collective-permute-start(f32[256,512]{1,0:T(8,128)S(1)} %get-tuple-element.97), channel_id=1, source_target_pairs={{0,2},{2,0},{4,6},{6,4},{8,10},{10,8},{12,14},{14,12},{16,18},{18,... | collective-permute-start | bytes 1572872 | tf_op jit(solution)/shard_map/ppermute | solution.py:249
  90.6 2.4 %collective-permute-start.23 = (f32[8,512]{1,0:T(8,128)S(1)}, f32[8,512]{1,0:T(8,128)S(1)}, u32[]{:S(2)}, u32[]{:S(2)}) collective-permute-start(f32[8,512]{1,0:T(8,128)S(1)} %get-tuple-element.101), channel_id=1, source_target_pairs={{0,2},{2,0},{4,6},{6,4},{8,10},{10,8},{12,14},{14,12},{16,18},{18,... | collective-permute-start | bytes 49160 | tf_op jit(solution)/shard_map/ppermute | solution.py:249
  91.2 6.4 %collective-permute-start.22 = (bf16[128,512]{1,0:T(8,128)(2,1)S(1)}, bf16[128,512]{1,0:T(8,128)(2,1)S(1)}, u32[]{:S(2)}, u32[]{:S(2)}) collective-permute-start(bf16[128,512]{1,0:T(8,128)(2,1)S(1)} %fusion), channel_id=1, source_target_pairs={{0,1},{1,0},{2,3},{3,2},{4,5},{5,4},{6,7},{7,6},{8,9},{9,8},{10,11... | collective-permute-start | bytes 393224 | tf_op jit(solution)/shard_map/ppermute | solution.py:250
  93.0 4.0 %collective-permute-start.24 = (f32[8,512]{1,0:T(8,128)S(1)}, f32[8,512]{1,0:T(8,128)S(1)}, u32[]{:S(2)}, u32[]{:S(2)}) collective-permute-start(f32[8,512]{1,0:T(8,128)S(1)} %add.34), channel_id=1, source_target_pairs={{0,1},{1,0},{2,3},{3,2},{4,5},{5,4},{6,7},{7,6},{8,9},{9,8},{10,11... | collective-permute-start | bytes 49160 | tf_op jit(solution)/shard_map/ppermute | solution.py:250

commit v5 on v4

--- a/solution.py
+++ b/solution.py
@@ -64,6 +64,14 @@
     return pltpu.with_memory_space_constraint(value, pltpu.VMEM)
 
 
+def ring_layer(at, layers):
+    return jnp.where(2 * at < layers, 2 * at, 2 * (layers - at) - 1)
+
+
+def ring_place(layer, layers):
+    return jnp.where(layer % 2 == 0, layer // 2, layers - (layer + 1) // 2)
+
+
 def fetch(n_mode, wanted, both, buffer, sems):
     modes = buffer.shape[3]
     place = lax.axis_index("mode")
@@ -71,7 +79,7 @@
     layer, side, core = lax.div(place, 4), lax.rem(lax.div(place, 2), 2), lax.rem(place, 2)
     copies = {}
     for b, (back, flip, half) in enumerate(wanted):
-        at = lax.rem(layer + (layers - back), layers) * 4
+        at = ring_layer(lax.rem(ring_place(layer, layers) + (layers - back), layers), layers) * 4
         at = at + lax.rem(side + flip, 2) * 2 + lax.rem(core + half, 2)
         at = pl.ds(pl.multiple_of(at * modes, modes), modes)
         for g, table in enumerate(both):
@@ -165,7 +173,6 @@
     pairs, (w, v, buffer, sems) = refs[:4], refs[4:]
     copies = fetch(n_mode, wanted, (own, other), buffer, sems)
     elems = pairs[0].shape[2]
-    modes = buffer.shape[3]
     rows = own.shape[0]
     place = lax.axis_index("mode")
     bases = (place * rows, (place + 1 - 2 * lax.rem(place, 2)) * rows)
@@ -183,19 +190,23 @@
         tail_rows = slice((4 + 2 * g) * elems, (6 + 2 * g) * elems)
         for b in range(len(wanted)):
             copies[g, b].wait()
-            part = buffer[g, b]
-            head, tail = kernel_split(nn(w[head_rows, :], part) + nn(w[tail_rows, :], part))
-            v[head_rows, b * modes : (b + 1) * modes] = head
-            v[tail_rows, b * modes : (b + 1) * modes] = tail
-
-
-def stress_body(spectra, w, table, out):
+        part = buffer[g, len(wanted) - 1]
+        head, tail = kernel_split(nn(w[head_rows, :], part) + nn(w[tail_rows, :], part))
+        v[head_rows, :] = head
+        v[tail_rows, :] = tail
+
+
+def stress_body(near, far, columns, spectra, w, table, spectra_out, out):
     parts, lines, both = spectra.shape
     rows, elems = both // 2, out.shape[0] // 2
     steps = out.shape[1]
+    panel = flat((near, far))
+    for g, here, there in row_tiles(rows):
+        total = spectra[:, :, there].reshape(parts * lines, -1) + nt(panel, columns[g, 0, here, :])
+        spectra_out[:, :, there] = total.reshape(parts, lines, -1)
     for g in range(2):
         here = slice(g * elems, (g + 1) * elems)
-        values = spectra[:, :, g * rows : (g + 1) * rows].reshape(parts * lines, rows)
+        values = spectra_out[:, :, g * rows : (g + 1) * rows].reshape(parts * lines, rows)
         s_head, s_tail = kernel_split(values)
         w_head, w_tail = w[here, :], w[(2 + g) * elems : (3 + g) * elems, :]
         picked = nt(w_head, s_head) + nt(w_head, s_tail) + nt(w_tail, s_head)
@@ -212,18 +223,9 @@
     return total[:elems] + total[elems:] + nt(v[:elems], g_tail)
 
 
-def half_body(near, far, v, columns, table, spectra, stress, spectra_out, stress_out):
-    parts, lines, _ = spectra.shape
-    panel = flat((near, far))
-    for g, here, there in row_tiles(columns.shape[2]):
-        total = spectra[:, :, there].reshape(parts * lines, -1) + nt(panel, columns[g, 0, here, :])
-        spectra_out[:, :, there] = total.reshape(parts, lines, -1)
-    stress_out[...] = stress[...] + time_term(panel, v[:, : panel.shape[1]], table)
-
-
 def last_body(near, far, v, table, before, keep, give):
     panel = flat((near, far))
-    total = before[...] + time_term(panel, v[:, panel.shape[1] :], table)
+    total = before[...] + time_term(panel, v[...], table)
     half = total.shape[0] // 2
     keep[...] = total[:half]
     give[...] = total[half:]
@@ -244,7 +246,9 @@
     tie = lax.optimization_barrier
     core = lax.axis_index("mode") % 2
     layers = n_mode // 4
-    ring = lambda a: lax.ppermute(a, "mode", [(i, (i + 4) % n_mode) for i in range(n_mode)])
+    order = [*range(0, layers, 2), *reversed(range(1, layers, 2))]
+    after = {layer: order[(i + 1) % layers] for i, layer in enumerate(order)}
+    ring = lambda a: lax.ppermute(a, "mode", [(i, after[i // 4] * 4 + i % 4) for i in range(n_mode)])
     across = lambda a: lax.ppermute(a, "mode", [(i, i ^ 2) for i in range(n_mode)])
     mate = lambda a: lax.ppermute(a, "mode", [(i, i ^ 1) for i in range(n_mode)])
     peer = lambda a: lax.ppermute(a, "node", [(0, 1), (1, 0)])
@@ -260,7 +264,7 @@
     x = [[], []]
     both = (shapes, mate(shapes))
     out = [((2 * steps, 2 * lines), BF16), ((lines, 8), F32)]
-    table, weights = on_chip(table_body, out, [harmonic.reshape(1, -1)], "table", flops=5 * 10**9)
+    table, weights = on_chip(table_body, out, [harmonic.reshape(1, -1)], "table", flops=10**11)
     z[1][0], table, weights = tie((z[1][0], table, weights))
 
     spectra = None
@@ -281,7 +285,7 @@
                 pairs.append(mate(pairs[1]))
             elif s == 1 and h == 1:
                 moved, swapped, spectra, pairs = tie((moved, swapped, spectra, pairs))
-                out = [((8 * elems, rows), BF16), ((8 * elems, 2 * modes), BF16)]
+                out = [((8 * elems, rows), BF16), ((8 * elems, modes), BF16)]
                 out.append(((2, 2, rows, modes), BF16))
                 wanted = [(layers - 1, 1, 0), (layers - 1, 1, 1)]
                 body = functools.partial(weights_body, n_mode, wanted)
@@ -296,15 +300,15 @@
             x[h].append(swapped)
             wanted = [(s, 1, h), (s + 1, 0, h)]
             spectra = add_spectra(n_mode, [swapped, moved], wanted, both, spectra)
-    cut = lines * 18 // 32
+    cut = lines // 2
     ends = [(across(z[h][-1][:, :cut]), ring(x[h][-1][:, cut:])) for h in range(2)]
     w, v, columns, table = [pinned(a) for a in (w, v, columns, table)]
-    out = [((4 * elems, steps), F32)]
-    (stress,) = on_chip(stress_body, out, [pinned(spectra), w, table], "first_stress")
-    ends[0], stress, spectra = tie((ends[0], stress, spectra))
-    out.insert(0, (spectra.shape, F32))
-    operands = [*ends[0], v, columns, table, pinned(spectra), pinned(stress)]
-    spectra, stress = on_chip(half_body, out, operands, "half_stress", aliases={5: 0, 6: 1}, flops=5 * 10**9)
+    ends[0], spectra = tie((ends[0], spectra))
+    out = [(spectra.shape, F32), ((4 * elems, steps), F32)]
+    operands = [*ends[0], columns, pinned(spectra), w, table]
+    spectra, stress = on_chip(
+        stress_body, out, operands, "first_stress", aliases={3: 0}, flops=5 * 10**9
+    )
     ends[1], stress, spectra = tie((ends[1], stress, spectra))
     out = [((2 * elems, steps), F32)] * 2
     keep, give = on_chip(last_body, out, [*ends[1], v, table, pinned(stress)], "last_stress")

time: 98.7 us -> 97.9 us (level)
  starting transfers between devices: 15.8 us -> 36.6 us
  waiting for transfers between devices: 50.1 us -> 32.4 us
  Pallas kernels: 28.2 us -> 24.4 us
    ppermute x8, starting transfers between devices: 3.62 us -> 24.4 us  [paired_shards(): lax.ppermute(a, 'mode', [(i, after[i // 4] * 4 + i % 4) for i in range(n_...]
    ppermute x8, waiting for transfers between devices: 23.4 us -> 11.7 us  [paired_shards(): lax.ppermute(a, 'mode', [(i, after[i // 4] * 4 + i % 4) for i in range(n_...]
    ppermute x8, waiting for transfers between devices: 20.3 us -> 13.8 us  [paired_shards(): lax.ppermute(a, 'mode', [(i, i ^ 2) for i in range(n_mode)])]
    pallas_call x13 -> x12, Pallas kernels: 28.2 us -> 24.4 us  [on_chip(): pl.pallas_call(body, out_shape=outs, in_specs=[HBM] * len(both) + [VMEM]...]
  transfers between devices with their start and end apart: 25 -> 25, of which waited for: 15 -> 14; matrix products, arithmetic and copies ran while one was open for 2% -> 1% of each run, Pallas kernels for 27% -> 23%
where the time goes in v5:
time: 97.9 us; the launch traced here: 97.7 us
  starting transfers between devices  36.6 us (37%)
  waiting for transfers between devices  32.4 us (33%)
  Pallas kernels  24.4 us (25%)
  local copies, waits for them, and re-layouts  2.06 us (2%)
  other arithmetic  1.39 us (1%)
    ppermute x8, starting transfers between devices, paired_shards(): lax.ppermute(a, 'mode', [(i, after[i // 4] * 4 + i % 4) for i in range(n_...  24.4 us
    pallas_call x12, Pallas kernels, on_chip(): pl.pallas_call(body, out_shape=outs, in_specs=[HBM] * len(both) + [VMEM]...  24.4 us
    ppermute x8, waiting for transfers between devices, paired_shards(): lax.ppermute(a, 'mode', [(i, i ^ 2) for i in range(n_mode)])  13.8 us
    ppermute x8, waiting for transfers between devices, paired_shards(): lax.ppermute(a, 'mode', [(i, after[i // 4] * 4 + i % 4) for i in range(n_...  11.7 us
    ppermute x8, starting transfers between devices, paired_shards(): lax.ppermute(a, 'mode', [(i, i ^ 2) for i in range(n_mode)])  7.14 us
    ppermute x3, waiting for transfers between devices, paired_shards(): peer = lambda a: lax.ppermute(a, 'node', [(0, 1), (1, 0)])  5.65 us
    ppermute x3, starting transfers between devices, paired_shards(): peer = lambda a: lax.ppermute(a, 'node', [(0, 1), (1, 0)])  3.84 us
  transfers between devices with their start and end apart: 25, of which 14 were waited for; matrix products, arithmetic and copies ran while one was open for 1% of the time, Pallas kernels for 23%

profile of v5, /device:TPU:0, one launch (start us, length us, event | category | flops | bytes accessed | tf_op | source)
XLA Modules:
  0.0 97.7 jit_solution(11787605753054838043)
XLA Ops:
  1.9 3.0 %collective-permute-start.5 = (bf16[2,512,256]{2,1,0:T(8,128)(2,1)S(1)}, bf16[2,512,256]{2,1,0:T(8,128)(2,1)S(1)}, u32[]{:S(2)}, u32[]{:S(2)}) collective-permute-start(bf16[2,512,256]{2,1,0:T(8,128)(2,1)S(1)} %get-tuple-element.100.refs_0_), channel_id=1, source_target_pairs={{0,4},{2,6},{4,0},{6,2},{8,12},{10,14},{12,8},{14,10},{16,20},{18,... | collective-permute-start | bytes 1572872 | tf_op jit(solution)/shard_map/ppermute | solution.py:252
  4.9 2.6 %collective-permute-start.4 = (bf16[2,512,256]{2,1,0:T(8,128)(2,1)S(1)}, bf16[2,512,256]{2,1,0:T(8,128)(2,1)S(1)}, u32[]{:S(2)}, u32[]{:S(2)}) collective-permute-start(bf16[2,512,256]{2,1,0:T(8,128)(2,1)S(1)} %get-tuple-element.100.refs_0_), channel_id=1, source_target_pairs={{0,16},{2,18},{4,20},{6,22},{8,0},{10,2},{12,4},{14,6},{16,24},{18... | collective-permute-start | bytes 1572872 | tf_op jit(solution)/shard_map/ppermute | solution.py:251
  8.7 2.0 %table.1 = (bf16[1024,1024]{1,0:T(8,128)(2,1)S(1)}, f32[512,8]{1,0:T(8,128)S(1)}) custom-call(s32[1,1024]{1,0:T(1,128)S(1)} %bitcast.8), custom_call_target="tpu_custom_call" | custom-call | flops 99999997952 | bytes 1000 | tf_op jit(solution)/shard_map/table/pallas_call | solution.py:50
  11.4 1.6 %collective-permute-start.1 = (bf16[2,512,256]{2,1,0:T(8,128)(2,1)S(1)}, bf16[2,512,256]{2,1,0:T(8,128)(2,1)S(1)}, u32[]{:S(2)}, u32[]{:S(2)}) collective-permute-start(bf16[2,512,256]{2,1,0:T(8,128)(2,1)S(1)} %collective-permute-done.refs_1_), channel_id=1, source_target_pairs={{0,16},{2,18},{4,20},{6,22},{8,0},{10,2},{12,4},{14,6},{16,24},{18... | collective-permute-start | bytes 1572872 | tf_op jit(solution)/shard_map/ppermute | solution.py:251
  12.9 4.8 %collective-permute-done.5.refs_0_ = bf16[2,512,256]{2,1,0:T(8,128)(2,1)S(1)} collective-permute-done((bf16[2,512,256]{2,1,0:T(8,128)(2,1)S(1)}, bf16[2,512,256]{2,1,0:T(8,128)(2,1)S(1)}, u32[]{:S(2)}, u32[]{:S(2)}) %collective-permute-start.5) | collective-permute-done | bytes 524320 | tf_op jit(solution)/shard_map/ppermute | solution.py:252
  17.7 2.2 %collective-permute-done.4.refs_1_ = bf16[2,512,256]{2,1,0:T(8,128)(2,1)S(1)} collective-permute-done((bf16[2,512,256]{2,1,0:T(8,128)(2,1)S(1)}, bf16[2,512,256]{2,1,0:T(8,128)(2,1)S(1)}, u32[]{:S(2)}, u32[]{:S(2)}) %collective-permute-start.4) | collective-permute-done | bytes 524320 | tf_op jit(solution)/shard_map/ppermute | solution.py:251
  20.4 3.4 %collective-permute-start.8 = (bf16[2,512,256]{2,1,0:T(8,128)(2,1)S(1)}, bf16[2,512,256]{2,1,0:T(8,128)(2,1)S(1)}, u32[]{:S(2)}, u32[]{:S(2)}) collective-permute-start(bf16[2,512,256]{2,1,0:T(8,128)(2,1)S(1)} %collective-permute-done.4.refs_1_), channel_id=1, source_target_pairs={{0,16},{2,18},{4,20},{6,22},{8,0},{10,2},{12,4},{14,6},{16,24},{18... | collective-permute-start | bytes 1572872 | tf_op jit(solution)/shard_map/ppermute | solution.py:251
  23.8 1.7 %add_spectra.7.refs_2_ = f32[2,512,1024]{2,1,0:T(8,128)S(1)} custom-call(bf16[512,4096]{1,0:T(8,128)(2,1)S(1)} %copy-done, bf16[512,4096]{1,0:T(8,128)(2,1)S(1)} %collective-permute-done.3.other, bf16[2,512,256]{2,1,0:T(8,128)(2,1)S(1)} %get-tuple-element.100.refs_0_, bf16[2,512,256]{2,1,0:T(8,128)(2,1)S(1)} %collective-permute-done.refs_1_), custom_call_target="tpu_custom_call" | custom-call | flops 1000 | bytes 1000 | tf_op jit(solution)/shard_map/add_spectra/pallas_call | solution.py:50
  25.5 1.7 %add_spectra.8.refs_2_ = f32[2,512,1024]{2,1,0:T(8,128)S(1)} custom-call(bf16[512,4096]{1,0:T(8,128)(2,1)S(1)} %copy-done, bf16[512,4096]{1,0:T(8,128)(2,1)S(1)} %collective-permute-done.3.other, bf16[2,512,256]{2,1,0:T(8,128)(2,1)S(1)} %collective-permute-done.5.refs_0_, ...), custom_call_target="tpu_custom_call", output_to_operand_aliasing={{}: (4, {})} | custom-call | flops 1000 | bytes 1000 | tf_op jit(solution)/shard_map/add_spectra/pallas_call | solution.py:50
  27.2 1.7 %collective-permute-done.2.refs_0_ = bf16[2,512,256]{2,1,0:T(8,128)(2,1)S(1)} collective-permute-done((bf16[2,512,256]{2,1,0:T(8,128)(2,1)S(1)}, bf16[2,512,256]{2,1,0:T(8,128)(2,1)S(1)}, u32[]{:S(2)}, u32[]{:S(2)}) %collective-permute-start.2) | collective-permute-done | bytes 524320 | tf_op jit(solution)/shard_map/ppermute | solution.py:252
  28.9 2.2 %collective-permute-done.1.refs_1_ = bf16[2,512,256]{2,1,0:T(8,128)(2,1)S(1)} collective-permute-done((bf16[2,512,256]{2,1,0:T(8,128)(2,1)S(1)}, bf16[2,512,256]{2,1,0:T(8,128)(2,1)S(1)}, u32[]{:S(2)}, u32[]{:S(2)}) %collective-permute-start.1) | collective-permute-done | bytes 524320 | tf_op jit(solution)/shard_map/ppermute | solution.py:251
  31.7 3.4 %collective-permute-start.6 = (bf16[2,512,256]{2,1,0:T(8,128)(2,1)S(1)}, bf16[2,512,256]{2,1,0:T(8,128)(2,1)S(1)}, u32[]{:S(2)}, u32[]{:S(2)}) collective-permute-start(bf16[2,512,256]{2,1,0:T(8,128)(2,1)S(1)} %collective-permute-done.1.refs_1_), channel_id=1, source_target_pairs={{0,16},{2,18},{4,20},{6,22},{8,0},{10,2},{12,4},{14,6},{16,24},{18... | collective-permute-start | bytes 1572872 | tf_op jit(solution)/shard_map/ppermute | solution.py:251
  35.0 1.7 %add_spectra.9.refs_2_ = f32[2,512,1024]{2,1,0:T(8,128)S(1)} custom-call(bf16[512,4096]{1,0:T(8,128)(2,1)S(1)} %copy-done, bf16[512,4096]{1,0:T(8,128)(2,1)S(1)} %collective-permute-done.3.other, bf16[2,512,256]{2,1,0:T(8,128)(2,1)S(1)} %collective-permute-done.2.refs_0_, ...), custom_call_target="tpu_custom_call", output_to_operand_aliasing={{}: (4, {})} | custom-call | flops 1000 | bytes 1000 | tf_op jit(solution)/shard_map/add_spectra/pallas_call | solution.py:50
  36.7 3.4 %collective-permute-done.9.refs_0_ = bf16[2,512,256]{2,1,0:T(8,128)(2,1)S(1)} collective-permute-done((bf16[2,512,256]{2,1,0:T(8,128)(2,1)S(1)}, bf16[2,512,256]{2,1,0:T(8,128)(2,1)S(1)}, u32[]{:S(2)}, u32[]{:S(2)}) %collective-permute-start.9) | collective-permute-done | bytes 524320 | tf_op jit(solution)/shard_map/ppermute | solution.py:252
  40.2 2.2 %collective-permute-done.8.refs_1_ = bf16[2,512,256]{2,1,0:T(8,128)(2,1)S(1)} collective-permute-done((bf16[2,512,256]{2,1,0:T(8,128)(2,1)S(1)}, bf16[2,512,256]{2,1,0:T(8,128)(2,1)S(1)}, u32[]{:S(2)}, u32[]{:S(2)}) %collective-permute-start.8) | collective-permute-done | bytes 524320 | tf_op jit(solution)/shard_map/ppermute | solution.py:251
  42.9 3.4 %collective-permute-start.15 = (bf16[2,512,256]{2,1,0:T(8,128)(2,1)S(1)}, bf16[2,512,256]{2,1,0:T(8,128)(2,1)S(1)}, u32[]{:S(2)}, u32[]{:S(2)}) collective-permute-start(bf16[2,512,256]{2,1,0:T(8,128)(2,1)S(1)} %collective-permute-done.8.refs_1_), channel_id=1, source_target_pairs={{0,16},{2,18},{4,20},{6,22},{8,0},{10,2},{12,4},{14,6},{16,24},{18... | collective-permute-start | bytes 1572872 | tf_op jit(solution)/shard_map/ppermute | solution.py:251
  49.1 2.1 %collective-permute-done.10.refs_1_ = f32[2,8,128]{2,1,0:T(8,128)S(1)} collective-permute-done((f32[2,8,128]{2,1,0:T(8,128)S(1)}, f32[2,8,128]{2,1,0:T(8,128)S(1)}, u32[]{:S(2)}, u32[]{:S(2)}) %collective-permute-start.10) | collective-permute-done | bytes 8224 | tf_op jit(solution)/shard_map/ppermute | solution.py:254
  51.2 1.7 %add_spectra.10.refs_2_ = f32[2,512,1024]{2,1,0:T(8,128)S(1)} custom-call(bf16[512,4096]{1,0:T(8,128)(2,1)S(1)} %copy-done, bf16[512,4096]{1,0:T(8,128)(2,1)S(1)} %collective-permute-done.3.other, bf16[2,512,256]{2,1,0:T(8,128)(2,1)S(1)} %collective-permute-done.9.refs_0_, ...), custom_call_target="tpu_custom_call", output_to_operand_aliasing={{}: (4, {})} | custom-call | flops 1000 | bytes 1000 | tf_op jit(solution)/shard_map/add_spectra/pallas_call | solution.py:50
  54.5 3.1 %collective-permute-start.13 = (bf16[2,512,256]{2,1,0:T(8,128)(2,1)S(1)}, bf16[2,512,256]{2,1,0:T(8,128)(2,1)S(1)}, u32[]{:S(2)}, u32[]{:S(2)}) collective-permute-start(bf16[2,512,256]{2,1,0:T(8,128)(2,1)S(1)} %collective-permute-done.6.refs_1_), channel_id=1, source_target_pairs={{0,16},{2,18},{4,20},{6,22},{8,0},{10,2},{12,4},{14,6},{16,24},{18... | collective-permute-start | bytes 1572872 | tf_op jit(solution)/shard_map/ppermute | solution.py:251
  57.5 1.7 %add_spectra.11.refs_2_ = f32[2,512,1024]{2,1,0:T(8,128)S(1)} custom-call(bf16[512,4096]{1,0:T(8,128)(2,1)S(1)} %copy-done, bf16[512,4096]{1,0:T(8,128)(2,1)S(1)} %collective-permute-done.3.other, bf16[2,512,256]{2,1,0:T(8,128)(2,1)S(1)} %collective-permute-done.7.refs_0_, ...), custom_call_target="tpu_custom_call", output_to_operand_aliasing={{}: (4, {})} | custom-call | flops 1000 | bytes 1000 | tf_op jit(solution)/shard_map/add_spectra/pallas_call | solution.py:50
  59.2 2.8 %weights.1 = (bf16[1024,512]{1,0:T(8,128)(2,1)S(1)}, bf16[1024,256]{1,0:T(8,128)(2,1)S(1)}, bf16[2,2,512,256]{3,2,1,0:T(8,128)(2,1)S(1)}) custom-call(bf16[512,4096]{1,0:T(8,128)(2,1)S(1)} %copy-done, bf16[512,4096]{1,0:T(8,128)(2,1)S(1)} %collective-permute-done.3.other, f32[2,8,128]{2,1,0:T(8,128)S(1)} %pad_maximum_fusion.refs_0_, ...), custom_call_target="tpu_custom_call" | custom-call | flops 1000 | bytes 1000 | tf_op jit(solution)/shard_map/weights/pallas_call | solution.py:50
  62.6 2.2 %collective-permute-done.15.refs_1_ = bf16[2,512,256]{2,1,0:T(8,128)(2,1)S(1)} collective-permute-done((bf16[2,512,256]{2,1,0:T(8,128)(2,1)S(1)}, bf16[2,512,256]{2,1,0:T(8,128)(2,1)S(1)}, u32[]{:S(2)}, u32[]{:S(2)}) %collective-permute-start.15) | collective-permute-done | bytes 524320 | tf_op jit(solution)/shard_map/ppermute | solution.py:251
  64.9 3.4 %collective-permute-start.20 = (bf16[2,256,256]{2,1,0:T(8,128)(2,1)S(1)}, bf16[2,256,256]{2,1,0:T(8,128)(2,1)S(1)}, u32[]{:S(2)}, u32[]{:S(2)}) collective-permute-start(bf16[2,256,256]{2,1,0:T(8,128)(2,1)S(1)} %slice.27), channel_id=1, source_target_pairs={{0,16},{2,18},{4,20},{6,22},{8,0},{10,2},{12,4},{14,6},{16,24},{18... | collective-permute-start | bytes 786440 | tf_op jit(solution)/shard_map/ppermute | solution.py:251
  68.9 1.7 %add_spectra.12.refs_2_ = f32[2,512,1024]{2,1,0:T(8,128)S(1)} custom-call(bf16[512,4096]{1,0:T(8,128)(2,1)S(1)} %copy-done, bf16[512,4096]{1,0:T(8,128)(2,1)S(1)} %collective-permute-done.3.other, bf16[2,512,256]{2,1,0:T(8,128)(2,1)S(1)} %collective-permute-done.16.refs_0_, ...), custom_call_target="tpu_custom_call", output_to_operand_aliasing={{}: (4, {})} | custom-call | flops 1000 | bytes 1000 | tf_op jit(solution)/shard_map/add_spectra/pallas_call | solution.py:50
  70.5 3.3 %collective-permute-done.14.refs_0_ = bf16[2,512,256]{2,1,0:T(8,128)(2,1)S(1)} collective-permute-done((bf16[2,512,256]{2,1,0:T(8,128)(2,1)S(1)}, bf16[2,512,256]{2,1,0:T(8,128)(2,1)S(1)}, u32[]{:S(2)}, u32[]{:S(2)}) %collective-permute-start.14) | collective-permute-done | bytes 524320 | tf_op jit(solution)/shard_map/ppermute | solution.py:252
  73.9 2.2 %collective-permute-done.13.refs_1_ = bf16[2,512,256]{2,1,0:T(8,128)(2,1)S(1)} collective-permute-done((bf16[2,512,256]{2,1,0:T(8,128)(2,1)S(1)}, bf16[2,512,256]{2,1,0:T(8,128)(2,1)S(1)}, u32[]{:S(2)}, u32[]{:S(2)}) %collective-permute-start.13) | collective-permute-done | bytes 524320 | tf_op jit(solution)/shard_map/ppermute | solution.py:251
  76.1 3.6 %collective-permute-start.18 = (bf16[2,256,256]{2,1,0:T(8,128)(2,1)S(1)}, bf16[2,256,256]{2,1,0:T(8,128)(2,1)S(1)}, u32[]{:S(2)}, u32[]{:S(2)}) collective-permute-start(bf16[2,256,256]{2,1,0:T(8,128)(2,1)S(1)} %slice.25), channel_id=1, source_target_pairs={{0,16},{2,18},{4,20},{6,22},{8,0},{10,2},{12,4},{14,6},{16,24},{18... | collective-permute-start | bytes 786440 | tf_op jit(solution)/shard_map/ppermute | solution.py:251
  80.3 1.7 %add_spectra.13.spectra = f32[2,512,1024]{2,1,0:T(8,128)S(1)} custom-call(bf16[512,4096]{1,0:T(8,128)(2,1)S(1)} %copy-done, bf16[512,4096]{1,0:T(8,128)(2,1)S(1)} %collective-permute-done.3.other, bf16[2,512,256]{2,1,0:T(8,128)(2,1)S(1)} %collective-permute-done.14.refs_0_, ...), custom_call_target="tpu_custom_call", output_to_operand_aliasing={{}: (4, {})} | custom-call | flops 1000 | bytes 1000 | tf_op jit(solution)/shard_map/add_spectra/pallas_call | solution.py:50
  82.0 4.3 %first_stress.1 = (f32[2,512,1024]{2,1,0:T(8,128)S(1)}, f32[512,512]{1,0:T(8,128)S(1)}) custom-call(bf16[2,256,256]{2,1,0:T(8,128)(2,1)S(1)} %collective-permute-done.19.near, bf16[2,256,256]{2,1,0:T(8,128)(2,1)S(1)} %collective-permute-done.20.far, bf16[2,2,512,256]{3,2,1,0:T(8,128)(2,1)S(1)} %get-tuple-element.82.columns, ...), custom_call_target="tpu_custom_call", output_to_operand_aliasing={{0}: (3, {})} | custom-call | flops 5000000000 | bytes 1000 | tf_op jit(solution)/shard_map/first_stress/pallas_call | solution.py:50
  86.3 2.0 %last_stress.1 = (f32[256,512]{1,0:T(8,128)S(1)}, f32[256,512]{1,0:T(8,128)S(1)}) custom-call(bf16[2,256,256]{2,1,0:T(8,128)(2,1)S(1)} %collective-permute-done.17.near, bf16[2,256,256]{2,1,0:T(8,128)(2,1)S(1)} %collective-permute-done.18.far, bf16[1024,256]{1,0:T(8,128)(2,1)S(1)} %get-tuple-element.90.v, bf16[1024,1024]{1,0:T(8,128)(2,1)S(1)} %get-tuple-element.85.table, ...), custom_call_target="tpu_custom_call" | custom-call | flops 1000 | bytes 1000 | tf_op jit(solution)/shard_map/last_stress/pallas_call | solution.py:50
  90.5 1.6 %collective-permute-start.22 = (bf16[128,512]{1,0:T(8,128)(2,1)S(1)}, bf16[128,512]{1,0:T(8,128)(2,1)S(1)}, u32[]{:S(2)}, u32[]{:S(2)}) collective-permute-start(bf16[128,512]{1,0:T(8,128)(2,1)S(1)} %fusion), channel_id=1, source_target_pairs={{0,1},{1,0},{2,3},{3,2},{4,5},{5,4},{6,7},{7,6},{8,9},{9,8},{10,11... | collective-permute-start | bytes 393224 | tf_op jit(solution)/shard_map/ppermute | solution.py:254
  92.8 3.5 %collective-permute-done.24 = f32[8,512]{1,0:T(8,128)S(1)} collective-permute-done((f32[8,512]{1,0:T(8,128)S(1)}, f32[8,512]{1,0:T(8,128)S(1)}, u32[]{:S(2)}, u32[]{:S(2)}) %collective-permute-start.24) | collective-permute-done | bytes 16416 | tf_op jit(solution)/shard_map/ppermute | solution.py:254
  (49 shorter events, 15.1 us)
Async XLA Ops:
  1.9 15.8 %collective-permute-start.5 = (bf16[2,512,256]{2,1,0:T(8,128)(2,1)S(1)}, bf16[2,512,256]{2,1,0:T(8,128)(2,1)S(1)}, u32[]{:S(2)}, u32[]{:S(2)}) collective-permute-start(bf16[2,512,256]{2,1,0:T(8,128)(2,1)S(1)} %get-tuple-element.100.refs_0_), channel_id=1, source_target_pairs={{0,4},{2,6},{4,0},{6,2},{8,12},{10,14},{12,8},{14,10},{16,20},{18,... | collective-permute-start | bytes 1572872 | tf_op jit(solution)/shard_map/ppermute | solution.py:252
  4.9 15.0 %collective-permute-start.4 = (bf16[2,512,256]{2,1,0:T(8,128)(2,1)S(1)}, bf16[2,512,256]{2,1,0:T(8,128)(2,1)S(1)}, u32[]{:S(2)}, u32[]{:S(2)}) collective-permute-start(bf16[2,512,256]{2,1,0:T(8,128)(2,1)S(1)} %get-tuple-element.100.refs_0_), channel_id=1, source_target_pairs={{0,16},{2,18},{4,20},{6,22},{8,0},{10,2},{12,4},{14,6},{16,24},{18... | collective-permute-start | bytes 1572872 | tf_op jit(solution)/shard_map/ppermute | solution.py:251
  7.5 3.2 %collective-permute-start = (bf16[2,512,256]{2,1,0:T(8,128)(2,1)S(1)}, bf16[2,512,256]{2,1,0:T(8,128)(2,1)S(1)}, u32[]{:S(2)}, u32[]{:S(2)}) collective-permute-start(bf16[2,512,256]{2,1,0:T(8,128)(2,1)S(1)} %get-tuple-element.101), channel_id=1, source_target_pairs={{0,2},{2,0},{4,6},{6,4},{8,10},{10,8},{12,14},{14,12},{16,18},{18,... | collective-permute-start | bytes 1572872 | tf_op jit(solution)/shard_map/ppermute | solution.py:253
  7.5 16.3 %collective-permute-start.3 = (bf16[512,4096]{1,0:T(8,128)(2,1)}, bf16[512,4096]{1,0:T(8,128)(2,1)S(1)}, u32[]{:S(2)}, u32[]{:S(2)}) collective-permute-start(bf16[512,4096]{1,0:T(8,128)(2,1)} %own.15), channel_id=1, source_target_pairs={{0,2},{2,0},{4,6},{6,4},{8,10},{10,8},{12,14},{14,12},{16,18},{18,... | collective-permute-start | bytes 12582920 | tf_op jit(solution)/shard_map/ppermute | solution.py:253
  8.0 0.7 copy-start.1
  8.7 15.1 %copy-start = (bf16[512,4096]{1,0:T(8,128)(2,1)S(1)}, bf16[512,4096]{1,0:T(8,128)(2,1)}, u32[]{:S(2)}) copy-start(bf16[512,4096]{1,0:T(8,128)(2,1)} %own.15) | copy-start | bytes 12582916
  10.8 18.2 %collective-permute-start.2 = (bf16[2,512,256]{2,1,0:T(8,128)(2,1)S(1)}, bf16[2,512,256]{2,1,0:T(8,128)(2,1)S(1)}, u32[]{:S(2)}, u32[]{:S(2)}) collective-permute-start(bf16[2,512,256]{2,1,0:T(8,128)(2,1)S(1)} %collective-permute-done.refs_1_), channel_id=1, source_target_pairs={{0,4},{2,6},{4,0},{6,2},{8,12},{10,14},{12,8},{14,10},{16,20},{18,... | collective-permute-start | bytes 1572872 | tf_op jit(solution)/shard_map/ppermute | solution.py:252
  11.4 19.8 %collective-permute-start.1 = (bf16[2,512,256]{2,1,0:T(8,128)(2,1)S(1)}, bf16[2,512,256]{2,1,0:T(8,128)(2,1)S(1)}, u32[]{:S(2)}, u32[]{:S(2)}) collective-permute-start(bf16[2,512,256]{2,1,0:T(8,128)(2,1)S(1)} %collective-permute-done.refs_1_), channel_id=1, source_target_pairs={{0,16},{2,18},{4,20},{6,22},{8,0},{10,2},{12,4},{14,6},{16,24},{18... | collective-permute-start | bytes 1572872 | tf_op jit(solution)/shard_map/ppermute | solution.py:251
  19.9 20.3 %collective-permute-start.9 = (bf16[2,512,256]{2,1,0:T(8,128)(2,1)S(1)}, bf16[2,512,256]{2,1,0:T(8,128)(2,1)S(1)}, u32[]{:S(2)}, u32[]{:S(2)}) collective-permute-start(bf16[2,512,256]{2,1,0:T(8,128)(2,1)S(1)} %collective-permute-done.4.refs_1_), channel_id=1, source_target_pairs={{0,4},{2,6},{4,0},{6,2},{8,12},{10,14},{12,8},{14,10},{16,20},{18,... | collective-permute-start | bytes 1572872 | tf_op jit(solution)/shard_map/ppermute | solution.py:252
  20.4 21.9 %collective-permute-start.8 = (bf16[2,512,256]{2,1,0:T(8,128)(2,1)S(1)}, bf16[2,512,256]{2,1,0:T(8,128)(2,1)S(1)}, u32[]{:S(2)}, u32[]{:S(2)}) collective-permute-start(bf16[2,512,256]{2,1,0:T(8,128)(2,1)S(1)} %collective-permute-done.4.refs_1_), channel_id=1, source_target_pairs={{0,16},{2,18},{4,20},{6,22},{8,0},{10,2},{12,4},{14,6},{16,24},{18... | collective-permute-start | bytes 1572872 | tf_op jit(solution)/shard_map/ppermute | solution.py:251
  27.2 19.1 %copy-start.2 = (s32[128,8]{0,1:T(8,128)S(1)}, s32[128,8]{0,1:T(8,128)}, u32[]{:S(2)}) copy-start(s32[128,8]{0,1:T(8,128)} %param.8) | copy-start | bytes 12292
  27.2 19.1 %copy-start.3 = (f32[128,8]{0,1:T(8,128)S(1)}, f32[128,8]{0,1:T(8,128)}, u32[]{:S(2)}) copy-start(f32[128,8]{0,1:T(8,128)} %param.9) | copy-start | bytes 12292
  31.1 21.8 %collective-permute-start.7 = (bf16[2,512,256]{2,1,0:T(8,128)(2,1)S(1)}, bf16[2,512,256]{2,1,0:T(8,128)(2,1)S(1)}, u32[]{:S(2)}, u32[]{:S(2)}) collective-permute-start(bf16[2,512,256]{2,1,0:T(8,128)(2,1)S(1)} %collective-permute-done.1.refs_1_), channel_id=1, source_target_pairs={{0,4},{2,6},{4,0},{6,2},{8,12},{10,14},{12,8},{14,10},{16,20},{18,... | collective-permute-start | bytes 1572872 | tf_op jit(solution)/shard_map/ppermute | solution.py:252
  31.7 21.9 %collective-permute-start.6 = (bf16[2,512,256]{2,1,0:T(8,128)(2,1)S(1)}, bf16[2,512,256]{2,1,0:T(8,128)(2,1)S(1)}, u32[]{:S(2)}, u32[]{:S(2)}) collective-permute-start(bf16[2,512,256]{2,1,0:T(8,128)(2,1)S(1)} %collective-permute-done.1.refs_1_), channel_id=1, source_target_pairs={{0,16},{2,18},{4,20},{6,22},{8,0},{10,2},{12,4},{14,6},{16,24},{18... | collective-permute-start | bytes 1572872 | tf_op jit(solution)/shard_map/ppermute | solution.py:251
  42.4 20.3 %collective-permute-start.16 = (bf16[2,512,256]{2,1,0:T(8,128)(2,1)S(1)}, bf16[2,512,256]{2,1,0:T(8,128)(2,1)S(1)}, u32[]{:S(2)}, u32[]{:S(2)}) collective-permute-start(bf16[2,512,256]{2,1,0:T(8,128)(2,1)S(1)} %collective-permute-done.8.refs_1_), channel_id=1, source_target_pairs={{0,4},{2,6},{4,0},{6,2},{8,12},{10,14},{12,8},{14,10},{16,20},{18,... | collective-permute-start | bytes 1572872 | tf_op jit(solution)/shard_map/ppermute | solution.py:252
  42.9 21.9 %collective-permute-start.15 = (bf16[2,512,256]{2,1,0:T(8,128)(2,1)S(1)}, bf16[2,512,256]{2,1,0:T(8,128)(2,1)S(1)}, u32[]{:S(2)}, u32[]{:S(2)}) collective-permute-start(bf16[2,512,256]{2,1,0:T(8,128)(2,1)S(1)} %collective-permute-done.8.refs_1_), channel_id=1, source_target_pairs={{0,16},{2,18},{4,20},{6,22},{8,0},{10,2},{12,4},{14,6},{16,24},{18... | collective-permute-start | bytes 1572872 | tf_op jit(solution)/shard_map/ppermute | solution.py:251
  46.3 1.2 %collective-permute-start.11 = (f32[2,8,128]{2,1,0:T(8,128)S(1)}, f32[2,8,128]{2,1,0:T(8,128)S(1)}, u32[]{:S(2)}, u32[]{:S(2)}) collective-permute-start(f32[2,8,128]{2,1,0:T(8,128)S(1)} %pad_maximum_fusion.refs_0_), channel_id=1, source_target_pairs={{0,2},{2,0},{4,6},{6,4},{8,10},{10,8},{12,14},{14,12},{16,18},{18,... | collective-permute-start | bytes 24584 | tf_op jit(solution)/shard_map/ppermute | solution.py:253
  47.5 3.7 %collective-permute-start.10 = (f32[2,8,128]{2,1,0:T(8,128)S(1)}, f32[2,8,128]{2,1,0:T(8,128)S(1)}, u32[]{:S(2)}, u32[]{:S(2)}) collective-permute-start(f32[2,8,128]{2,1,0:T(8,128)S(1)} %pad_maximum_fusion.refs_0_), channel_id=1, source_target_pairs={{0,1},{1,0},{2,3},{3,2},{4,5},{5,4},{6,7},{7,6},{8,9},{9,8},{10,11... | collective-permute-start | bytes 24584 | tf_op jit(solution)/shard_map/ppermute | solution.py:254
  51.2 1.7 %collective-permute-start.12 = (f32[2,8,128]{2,1,0:T(8,128)S(1)}, f32[2,8,128]{2,1,0:T(8,128)S(1)}, u32[]{:S(2)}, u32[]{:S(2)}) collective-permute-start(f32[2,8,128]{2,1,0:T(8,128)S(1)} %collective-permute-done.10.refs_1_), channel_id=1, source_target_pairs={{0,2},{2,0},{4,6},{6,4},{8,10},{10,8},{12,14},{14,12},{16,18},{18,... | collective-permute-start | bytes 24584 | tf_op jit(solution)/shard_map/ppermute | solution.py:253
  53.6 20.3 %collective-permute-start.14 = (bf16[2,512,256]{2,1,0:T(8,128)(2,1)S(1)}, bf16[2,512,256]{2,1,0:T(8,128)(2,1)S(1)}, u32[]{:S(2)}, u32[]{:S(2)}) collective-permute-start(bf16[2,512,256]{2,1,0:T(8,128)(2,1)S(1)} %collective-permute-done.6.refs_1_), channel_id=1, source_target_pairs={{0,4},{2,6},{4,0},{6,2},{8,12},{10,14},{12,8},{14,10},{16,20},{18,... | collective-permute-start | bytes 1572872 | tf_op jit(solution)/shard_map/ppermute | solution.py:252
  54.5 21.6 %collective-permute-start.13 = (bf16[2,512,256]{2,1,0:T(8,128)(2,1)S(1)}, bf16[2,512,256]{2,1,0:T(8,128)(2,1)S(1)}, u32[]{:S(2)}, u32[]{:S(2)}) collective-permute-start(bf16[2,512,256]{2,1,0:T(8,128)(2,1)S(1)} %collective-permute-done.6.refs_1_), channel_id=1, source_target_pairs={{0,16},{2,18},{4,20},{6,22},{8,0},{10,2},{12,4},{14,6},{16,24},{18... | collective-permute-start | bytes 1572872 | tf_op jit(solution)/shard_map/ppermute | solution.py:251
  64.9 17.1 %collective-permute-start.20 = (bf16[2,256,256]{2,1,0:T(8,128)(2,1)S(1)}, bf16[2,256,256]{2,1,0:T(8,128)(2,1)S(1)}, u32[]{:S(2)}, u32[]{:S(2)}) collective-permute-start(bf16[2,256,256]{2,1,0:T(8,128)(2,1)S(1)} %slice.27), channel_id=1, source_target_pairs={{0,16},{2,18},{4,20},{6,22},{8,0},{10,2},{12,4},{14,6},{16,24},{18... | collective-permute-start | bytes 786440 | tf_op jit(solution)/shard_map/ppermute | solution.py:251
  68.3 13.6 %collective-permute-start.19 = (bf16[2,256,256]{2,1,0:T(8,128)(2,1)S(1)}, bf16[2,256,256]{2,1,0:T(8,128)(2,1)S(1)}, u32[]{:S(2)}, u32[]{:S(2)}) collective-permute-start(bf16[2,256,256]{2,1,0:T(8,128)(2,1)S(1)} %slice.26), channel_id=1, source_target_pairs={{0,4},{2,6},{4,0},{6,2},{8,12},{10,14},{12,8},{14,10},{16,20},{18,... | collective-permute-start | bytes 786440 | tf_op jit(solution)/shard_map/ppermute | solution.py:252
  76.1 10.2 %collective-permute-start.18 = (bf16[2,256,256]{2,1,0:T(8,128)(2,1)S(1)}, bf16[2,256,256]{2,1,0:T(8,128)(2,1)S(1)}, u32[]{:S(2)}, u32[]{:S(2)}) collective-permute-start(bf16[2,256,256]{2,1,0:T(8,128)(2,1)S(1)} %slice.25), channel_id=1, source_target_pairs={{0,16},{2,18},{4,20},{6,22},{8,0},{10,2},{12,4},{14,6},{16,24},{18... | collective-permute-start | bytes 786440 | tf_op jit(solution)/shard_map/ppermute | solution.py:251
  79.7 6.6 %collective-permute-start.17 = (bf16[2,256,256]{2,1,0:T(8,128)(2,1)S(1)}, bf16[2,256,256]{2,1,0:T(8,128)(2,1)S(1)}, u32[]{:S(2)}, u32[]{:S(2)}) collective-permute-start(bf16[2,256,256]{2,1,0:T(8,128)(2,1)S(1)} %slice.24), channel_id=1, source_target_pairs={{0,4},{2,6},{4,0},{6,2},{8,12},{10,14},{12,8},{14,10},{16,20},{18,... | collective-permute-start | bytes 786440 | tf_op jit(solution)/shard_map/ppermute | solution.py:252
  88.3 2.2 %collective-permute-start.21 = (f32[256,512]{1,0:T(8,128)S(1)}, f32[256,512]{1,0:T(8,128)S(1)}, u32[]{:S(2)}, u32[]{:S(2)}) collective-permute-start(f32[256,512]{1,0:T(8,128)S(1)} %get-tuple-element.95), channel_id=1, source_target_pairs={{0,2},{2,0},{4,6},{6,4},{8,10},{10,8},{12,14},{14,12},{16,18},{18,... | collective-permute-start | bytes 1572872 | tf_op jit(solution)/shard_map/ppermute | solution.py:253
  89.9 2.2 %collective-permute-start.23 = (f32[8,512]{1,0:T(8,128)S(1)}, f32[8,512]{1,0:T(8,128)S(1)}, u32[]{:S(2)}, u32[]{:S(2)}) collective-permute-start(f32[8,512]{1,0:T(8,128)S(1)} %get-tuple-element.99), channel_id=1, source_target_pairs={{0,2},{2,0},{4,6},{6,4},{8,10},{10,8},{12,14},{14,12},{16,18},{18,... | collective-permute-start | bytes 49160 | tf_op jit(solution)/shard_map/ppermute | solution.py:253
  90.5 6.4 %collective-permute-start.22 = (bf16[128,512]{1,0:T(8,128)(2,1)S(1)}, bf16[128,512]{1,0:T(8,128)(2,1)S(1)}, u32[]{:S(2)}, u32[]{:S(2)}) collective-permute-start(bf16[128,512]{1,0:T(8,128)(2,1)S(1)} %fusion), channel_id=1, source_target_pairs={{0,1},{1,0},{2,3},{3,2},{4,5},{5,4},{6,7},{7,6},{8,9},{9,8},{10,11... | collective-permute-start | bytes 393224 | tf_op jit(solution)/shard_map/ppermute | solution.py:254
  92.1 4.2 %collective-permute-start.24 = (f32[8,512]{1,0:T(8,128)S(1)}, f32[8,512]{1,0:T(8,128)S(1)}, u32[]{:S(2)}, u32[]{:S(2)}) collective-permute-start(f32[8,512]{1,0:T(8,128)S(1)} %add.34), channel_id=1, source_target_pairs={{0,1},{1,0},{2,3},{3,2},{4,5},{5,4},{6,7},{7,6},{8,9},{9,8},{10,11... | collective-permute-start | bytes 49160 | tf_op jit(solution)/shard_map/ppermute | solution.py:254

commit v6 on v5

--- a/solution.py
+++ b/solution.py
@@ -294,12 +294,18 @@
                 )
             elif s == 2 and h == 0:
                 moved, swapped, spectra, w, v, columns = tie((moved, swapped, spectra, w, v, columns))
+            elif (s, h) == (layers - 2, 1):
+                spectra = add_spectra(n_mode, [swapped], [(s, 1, h)], both, spectra)
+                moved, swapped, spectra = tie((moved, swapped, spectra))
             else:
                 moved, swapped, spectra = tie((moved, swapped, spectra))
             z[h].append(moved)
             x[h].append(swapped)
-            wanted = [(s, 1, h), (s + 1, 0, h)]
-            spectra = add_spectra(n_mode, [swapped, moved], wanted, both, spectra)
+            if (s, h) == (layers - 2, 1):
+                spectra = add_spectra(n_mode, [moved], [(s + 1, 0, h)], both, spectra)
+            else:
+                wanted = [(s, 1, h), (s + 1, 0, h)]
+                spectra = add_spectra(n_mode, [swapped, moved], wanted, both, spectra)
     cut = lines // 2
     ends = [(across(z[h][-1][:, :cut]), ring(x[h][-1][:, cut:])) for h in range(2)]
     w, v, columns, table = [pinned(a) for a in (w, v, columns, table)]
@@ -317,10 +323,12 @@
     out = [((8, rows), F32)] * 2
     operands = [*ends[1], columns, pinned(spectra), pinned(weights)]
     keep_m, give_m = on_chip(moment_body, out, operands, "moments")
+    got, keep_m, give_m = tie((got, keep_m, give_m))
     send = (keep[elems:] + got[elems:]).astype(BF16)
     half = keep_m + mate(give_m)
     stress = (keep[:elems] + got[:elems]) + peer(send).astype(F32)
-    moments = half + peer(half)
+    stress, other_half = tie((stress, peer(half)))
+    moments = half + other_half
     start = lax.axis_index("node") * (rows // 2)
     return stress, lax.dynamic_slice(moments, (0, start), (4, rows // 2))
 

time: 97.9 us -> 97.3 us (level)
    ppermute x6, waiting for transfers between devices: 1.17 us -> 2.69 us  [paired_shards(): lax.ppermute(a, 'mode', [(i, i ^ 1) for i in range(n_mode)])]
    ppermute x3, waiting for transfers between devices: 5.65 us -> 4.61 us  [paired_shards(): peer = lambda a: lax.ppermute(a, 'node', [(0, 1), (1, 0)])]
    pallas_call x12 -> x13, Pallas kernels: 24.4 us -> 24.8 us  [on_chip(): pl.pallas_call(body, out_shape=outs, in_specs=[HBM] * len(both) + [VMEM]...]
  transfers between devices with their start and end apart: 25 -> 25, of which waited for: 14 -> 18; matrix products, arithmetic and copies ran while one was open for 1% -> 1% of each run, Pallas kernels for 23% -> 23%
where the time goes in v6:
time: 97.3 us; the launch traced here: 97.1 us
  starting transfers between devices  35.8 us (37%)
  waiting for transfers between devices  32.2 us (33%)
  Pallas kernels  24.8 us (25%)
  local copies, waits for them, and re-layouts  2.06 us (2%)
  other arithmetic  1.39 us (1%)
    pallas_call x13, Pallas kernels, on_chip(): pl.pallas_call(body, out_shape=outs, in_specs=[HBM] * len(both) + [VMEM]...  24.8 us
    ppermute x8, starting transfers between devices, paired_shards(): lax.ppermute(a, 'mode', [(i, after[i // 4] * 4 + i % 4) for i in range(n_...  24 us
    ppermute x8, waiting for transfers between devices, paired_shards(): lax.ppermute(a, 'mode', [(i, i ^ 2) for i in range(n_mode)])  13.7 us
    ppermute x8, waiting for transfers between devices, paired_shards(): lax.ppermute(a, 'mode', [(i, after[i // 4] * 4 + i % 4) for i in range(n_...  11.2 us
    ppermute x8, starting transfers between devices, paired_shards(): lax.ppermute(a, 'mode', [(i, i ^ 2) for i in range(n_mode)])  7.57 us
    ppermute x3, waiting for transfers between devices, paired_shards(): peer = lambda a: lax.ppermute(a, 'node', [(0, 1), (1, 0)])  4.61 us
    ppermute x3, starting transfers between devices, paired_shards(): peer = lambda a: lax.ppermute(a, 'node', [(0, 1), (1, 0)])  3.61 us
    ppermute x6, waiting for transfers between devices, paired_shards(): lax.ppermute(a, 'mode', [(i, i ^ 1) for i in range(n_mode)])  2.69 us
  transfers between devices with their start and end apart: 25, of which 18 were waited for; matrix products, arithmetic and copies ran while one was open for 1% of the time, Pallas kernels for 23%

profile of v6, /device:TPU:0, one launch (start us, length us, event | category | flops | bytes accessed | tf_op | source)
XLA Modules:
  0.0 97.1 jit_solution(15487503174988269031)
XLA Ops:
  1.9 3.0 %collective-permute-start.5 = (bf16[2,512,256]{2,1,0:T(8,128)(2,1)S(1)}, bf16[2,512,256]{2,1,0:T(8,128)(2,1)S(1)}, u32[]{:S(2)}, u32[]{:S(2)}) collective-permute-start(bf16[2,512,256]{2,1,0:T(8,128)(2,1)S(1)} %get-tuple-element.110.refs_0_), channel_id=1, source_target_pairs={{0,4},{2,6},{4,0},{6,2},{8,12},{10,14},{12,8},{14,10},{16,20},{18,... | collective-permute-start | bytes 1572872 | tf_op jit(solution)/shard_map/ppermute | solution.py:252
  4.9 2.6 %collective-permute-start.4 = (bf16[2,512,256]{2,1,0:T(8,128)(2,1)S(1)}, bf16[2,512,256]{2,1,0:T(8,128)(2,1)S(1)}, u32[]{:S(2)}, u32[]{:S(2)}) collective-permute-start(bf16[2,512,256]{2,1,0:T(8,128)(2,1)S(1)} %get-tuple-element.110.refs_0_), channel_id=1, source_target_pairs={{0,16},{2,18},{4,20},{6,22},{8,0},{10,2},{12,4},{14,6},{16,24},{18... | collective-permute-start | bytes 1572872 | tf_op jit(solution)/shard_map/ppermute | solution.py:251
  8.7 2.0 %table.1 = (bf16[1024,1024]{1,0:T(8,128)(2,1)S(1)}, f32[512,8]{1,0:T(8,128)S(1)}) custom-call(s32[1,1024]{1,0:T(1,128)S(1)} %bitcast.8), custom_call_target="tpu_custom_call" | custom-call | flops 99999997952 | bytes 1000 | tf_op jit(solution)/shard_map/table/pallas_call | solution.py:50
  11.4 1.6 %collective-permute-start.1 = (bf16[2,512,256]{2,1,0:T(8,128)(2,1)S(1)}, bf16[2,512,256]{2,1,0:T(8,128)(2,1)S(1)}, u32[]{:S(2)}, u32[]{:S(2)}) collective-permute-start(bf16[2,512,256]{2,1,0:T(8,128)(2,1)S(1)} %collective-permute-done.refs_1_), channel_id=1, source_target_pairs={{0,16},{2,18},{4,20},{6,22},{8,0},{10,2},{12,4},{14,6},{16,24},{18... | collective-permute-start | bytes 1572872 | tf_op jit(solution)/shard_map/ppermute | solution.py:251
  12.9 4.8 %collective-permute-done.5.refs_0_ = bf16[2,512,256]{2,1,0:T(8,128)(2,1)S(1)} collective-permute-done((bf16[2,512,256]{2,1,0:T(8,128)(2,1)S(1)}, bf16[2,512,256]{2,1,0:T(8,128)(2,1)S(1)}, u32[]{:S(2)}, u32[]{:S(2)}) %collective-permute-start.5) | collective-permute-done | bytes 524320 | tf_op jit(solution)/shard_map/ppermute | solution.py:252
  17.7 2.2 %collective-permute-done.4.refs_1_ = bf16[2,512,256]{2,1,0:T(8,128)(2,1)S(1)} collective-permute-done((bf16[2,512,256]{2,1,0:T(8,128)(2,1)S(1)}, bf16[2,512,256]{2,1,0:T(8,128)(2,1)S(1)}, u32[]{:S(2)}, u32[]{:S(2)}) %collective-permute-start.4) | collective-permute-done | bytes 524320 | tf_op jit(solution)/shard_map/ppermute | solution.py:251
  20.4 3.4 %collective-permute-start.8 = (bf16[2,512,256]{2,1,0:T(8,128)(2,1)S(1)}, bf16[2,512,256]{2,1,0:T(8,128)(2,1)S(1)}, u32[]{:S(2)}, u32[]{:S(2)}) collective-permute-start(bf16[2,512,256]{2,1,0:T(8,128)(2,1)S(1)} %collective-permute-done.4.refs_1_), channel_id=1, source_target_pairs={{0,16},{2,18},{4,20},{6,22},{8,0},{10,2},{12,4},{14,6},{16,24},{18... | collective-permute-start | bytes 1572872 | tf_op jit(solution)/shard_map/ppermute | solution.py:251
  23.8 1.7 %add_spectra.8.refs_2_ = f32[2,512,1024]{2,1,0:T(8,128)S(1)} custom-call(bf16[512,4096]{1,0:T(8,128)(2,1)S(1)} %copy-done, bf16[512,4096]{1,0:T(8,128)(2,1)S(1)} %collective-permute-done.3.other, bf16[2,512,256]{2,1,0:T(8,128)(2,1)S(1)} %get-tuple-element.110.refs_0_, bf16[2,512,256]{2,1,0:T(8,128)(2,1)S(1)} %collective-permute-done.refs_1_), custom_call_target="tpu_custom_call" | custom-call | flops 1000 | bytes 1000 | tf_op jit(solution)/shard_map/add_spectra/pallas_call | solution.py:50
  25.5 1.7 %add_spectra.9.refs_2_ = f32[2,512,1024]{2,1,0:T(8,128)S(1)} custom-call(bf16[512,4096]{1,0:T(8,128)(2,1)S(1)} %copy-done, bf16[512,4096]{1,0:T(8,128)(2,1)S(1)} %collective-permute-done.3.other, bf16[2,512,256]{2,1,0:T(8,128)(2,1)S(1)} %collective-permute-done.5.refs_0_, ...), custom_call_target="tpu_custom_call", output_to_operand_aliasing={{}: (4, {})} | custom-call | flops 1000 | bytes 1000 | tf_op jit(solution)/shard_map/add_spectra/pallas_call | solution.py:50
  27.2 1.7 %collective-permute-done.2.refs_0_ = bf16[2,512,256]{2,1,0:T(8,128)(2,1)S(1)} collective-permute-done((bf16[2,512,256]{2,1,0:T(8,128)(2,1)S(1)}, bf16[2,512,256]{2,1,0:T(8,128)(2,1)S(1)}, u32[]{:S(2)}, u32[]{:S(2)}) %collective-permute-start.2) | collective-permute-done | bytes 524320 | tf_op jit(solution)/shard_map/ppermute | solution.py:252
  28.9 2.2 %collective-permute-done.1.refs_1_ = bf16[2,512,256]{2,1,0:T(8,128)(2,1)S(1)} collective-permute-done((bf16[2,512,256]{2,1,0:T(8,128)(2,1)S(1)}, bf16[2,512,256]{2,1,0:T(8,128)(2,1)S(1)}, u32[]{:S(2)}, u32[]{:S(2)}) %collective-permute-start.1) | collective-permute-done | bytes 524320 | tf_op jit(solution)/shard_map/ppermute | solution.py:251
  31.7 3.4 %collective-permute-start.6 = (bf16[2,512,256]{2,1,0:T(8,128)(2,1)S(1)}, bf16[2,512,256]{2,1,0:T(8,128)(2,1)S(1)}, u32[]{:S(2)}, u32[]{:S(2)}) collective-permute-start(bf16[2,512,256]{2,1,0:T(8,128)(2,1)S(1)} %collective-permute-done.1.refs_1_), channel_id=1, source_target_pairs={{0,16},{2,18},{4,20},{6,22},{8,0},{10,2},{12,4},{14,6},{16,24},{18... | collective-permute-start | bytes 1572872 | tf_op jit(solution)/shard_map/ppermute | solution.py:251
  35.0 1.7 %add_spectra.10.refs_2_ = f32[2,512,1024]{2,1,0:T(8,128)S(1)} custom-call(bf16[512,4096]{1,0:T(8,128)(2,1)S(1)} %copy-done, bf16[512,4096]{1,0:T(8,128)(2,1)S(1)} %collective-permute-done.3.other, bf16[2,512,256]{2,1,0:T(8,128)(2,1)S(1)} %collective-permute-done.2.refs_0_, ...), custom_call_target="tpu_custom_call", output_to_operand_aliasing={{}: (4, {})} | custom-call | flops 1000 | bytes 1000 | tf_op jit(solution)/shard_map/add_spectra/pallas_call | solution.py:50
  36.7 3.4 %collective-permute-done.9.refs_0_ = bf16[2,512,256]{2,1,0:T(8,128)(2,1)S(1)} collective-permute-done((bf16[2,512,256]{2,1,0:T(8,128)(2,1)S(1)}, bf16[2,512,256]{2,1,0:T(8,128)(2,1)S(1)}, u32[]{:S(2)}, u32[]{:S(2)}) %collective-permute-start.9) | collective-permute-done | bytes 524320 | tf_op jit(solution)/shard_map/ppermute | solution.py:252
  40.2 2.2 %collective-permute-done.8.refs_1_ = bf16[2,512,256]{2,1,0:T(8,128)(2,1)S(1)} collective-permute-done((bf16[2,512,256]{2,1,0:T(8,128)(2,1)S(1)}, bf16[2,512,256]{2,1,0:T(8,128)(2,1)S(1)}, u32[]{:S(2)}, u32[]{:S(2)}) %collective-permute-start.8) | collective-permute-done | bytes 524320 | tf_op jit(solution)/shard_map/ppermute | solution.py:251
  42.9 3.4 %collective-permute-start.15 = (bf16[2,512,256]{2,1,0:T(8,128)(2,1)S(1)}, bf16[2,512,256]{2,1,0:T(8,128)(2,1)S(1)}, u32[]{:S(2)}, u32[]{:S(2)}) collective-permute-start(bf16[2,512,256]{2,1,0:T(8,128)(2,1)S(1)} %collective-permute-done.8.refs_1_), channel_id=1, source_target_pairs={{0,16},{2,18},{4,20},{6,22},{8,0},{10,2},{12,4},{14,6},{16,24},{18... | collective-permute-start | bytes 1572872 | tf_op jit(solution)/shard_map/ppermute | solution.py:251
  47.5 1.5 %collective-permute-start.10 = (f32[2,8,128]{2,1,0:T(8,128)S(1)}, f32[2,8,128]{2,1,0:T(8,128)S(1)}, u32[]{:S(2)}, u32[]{:S(2)}) collective-permute-start(f32[2,8,128]{2,1,0:T(8,128)S(1)} %pad_maximum_fusion.refs_0_), channel_id=1, source_target_pairs={{0,1},{1,0},{2,3},{3,2},{4,5},{5,4},{6,7},{7,6},{8,9},{9,8},{10,11... | collective-permute-start | bytes 24584 | tf_op jit(solution)/shard_map/ppermute | solution.py:254
  49.1 2.1 %collective-permute-done.10.refs_1_ = f32[2,8,128]{2,1,0:T(8,128)S(1)} collective-permute-done((f32[2,8,128]{2,1,0:T(8,128)S(1)}, f32[2,8,128]{2,1,0:T(8,128)S(1)}, u32[]{:S(2)}, u32[]{:S(2)}) %collective-permute-start.10) | collective-permute-done | bytes 8224 | tf_op jit(solution)/shard_map/ppermute | solution.py:254
  51.2 1.7 %add_spectra.11.refs_2_ = f32[2,512,1024]{2,1,0:T(8,128)S(1)} custom-call(bf16[512,4096]{1,0:T(8,128)(2,1)S(1)} %copy-done, bf16[512,4096]{1,0:T(8,128)(2,1)S(1)} %collective-permute-done.3.other, bf16[2,512,256]{2,1,0:T(8,128)(2,1)S(1)} %collective-permute-done.9.refs_0_, ...), custom_call_target="tpu_custom_call", output_to_operand_aliasing={{}: (4, {})} | custom-call | flops 1000 | bytes 1000 | tf_op jit(solution)/shard_map/add_spectra/pallas_call | solution.py:50
  54.5 3.1 %collective-permute-start.13 = (bf16[2,512,256]{2,1,0:T(8,128)(2,1)S(1)}, bf16[2,512,256]{2,1,0:T(8,128)(2,1)S(1)}, u32[]{:S(2)}, u32[]{:S(2)}) collective-permute-start(bf16[2,512,256]{2,1,0:T(8,128)(2,1)S(1)} %collective-permute-done.6.refs_1_), channel_id=1, source_target_pairs={{0,16},{2,18},{4,20},{6,22},{8,0},{10,2},{12,4},{14,6},{16,24},{18... | collective-permute-start | bytes 1572872 | tf_op jit(solution)/shard_map/ppermute | solution.py:251
  57.5 1.7 %add_spectra.12.refs_2_ = f32[2,512,1024]{2,1,0:T(8,128)S(1)} custom-call(bf16[512,4096]{1,0:T(8,128)(2,1)S(1)} %copy-done, bf16[512,4096]{1,0:T(8,128)(2,1)S(1)} %collective-permute-done.3.other, bf16[2,512,256]{2,1,0:T(8,128)(2,1)S(1)} %collective-permute-done.7.refs_0_, ...), custom_call_target="tpu_custom_call", output_to_operand_aliasing={{}: (4, {})} | custom-call | flops 1000 | bytes 1000 | tf_op jit(solution)/shard_map/add_spectra/pallas_call | solution.py:50
  59.2 2.8 %weights.1 = (bf16[1024,512]{1,0:T(8,128)(2,1)S(1)}, bf16[1024,256]{1,0:T(8,128)(2,1)S(1)}, bf16[2,2,512,256]{3,2,1,0:T(8,128)(2,1)S(1)}) custom-call(bf16[512,4096]{1,0:T(8,128)(2,1)S(1)} %copy-done, bf16[512,4096]{1,0:T(8,128)(2,1)S(1)} %collective-permute-done.3.other, f32[2,8,128]{2,1,0:T(8,128)S(1)} %pad_maximum_fusion.refs_0_, ...), custom_call_target="tpu_custom_call" | custom-call | flops 1000 | bytes 1000 | tf_op jit(solution)/shard_map/weights/pallas_call | solution.py:50
  62.6 2.2 %collective-permute-done.15.refs_1_ = bf16[2,512,256]{2,1,0:T(8,128)(2,1)S(1)} collective-permute-done((bf16[2,512,256]{2,1,0:T(8,128)(2,1)S(1)}, bf16[2,512,256]{2,1,0:T(8,128)(2,1)S(1)}, u32[]{:S(2)}, u32[]{:S(2)}) %collective-permute-start.15) | collective-permute-done | bytes 524320 | tf_op jit(solution)/shard_map/ppermute | solution.py:251
  64.9 3.6 %collective-permute-start.20 = (bf16[2,256,256]{2,1,0:T(8,128)(2,1)S(1)}, bf16[2,256,256]{2,1,0:T(8,128)(2,1)S(1)}, u32[]{:S(2)}, u32[]{:S(2)}) collective-permute-start(bf16[2,256,256]{2,1,0:T(8,128)(2,1)S(1)} %slice.27), channel_id=1, source_target_pairs={{0,16},{2,18},{4,20},{6,22},{8,0},{10,2},{12,4},{14,6},{16,24},{18... | collective-permute-start | bytes 786440 | tf_op jit(solution)/shard_map/ppermute | solution.py:251
  69.0 1.7 %add_spectra.13.refs_1_ = f32[2,512,1024]{2,1,0:T(8,128)S(1)} custom-call(bf16[512,4096]{1,0:T(8,128)(2,1)S(1)} %copy-done, bf16[512,4096]{1,0:T(8,128)(2,1)S(1)} %collective-permute-done.3.other, bf16[2,512,256]{2,1,0:T(8,128)(2,1)S(1)} %collective-permute-done.16.refs_0_, ...), custom_call_target="tpu_custom_call", output_to_operand_aliasing={{}: (4, {})} | custom-call | flops 1000 | bytes 1000 | tf_op jit(solution)/shard_map/add_spectra/pallas_call | solution.py:50
  70.7 3.2 %collective-permute-done.14.refs_0_ = bf16[2,512,256]{2,1,0:T(8,128)(2,1)S(1)} collective-permute-done((bf16[2,512,256]{2,1,0:T(8,128)(2,1)S(1)}, bf16[2,512,256]{2,1,0:T(8,128)(2,1)S(1)}, u32[]{:S(2)}, u32[]{:S(2)}) %collective-permute-start.14) | collective-permute-done | bytes 524320 | tf_op jit(solution)/shard_map/ppermute | solution.py:252
  77.1 3.0 %collective-permute-start.18 = (bf16[2,256,256]{2,1,0:T(8,128)(2,1)S(1)}, bf16[2,256,256]{2,1,0:T(8,128)(2,1)S(1)}, u32[]{:S(2)}, u32[]{:S(2)}) collective-permute-start(bf16[2,256,256]{2,1,0:T(8,128)(2,1)S(1)} %slice.25), channel_id=1, source_target_pairs={{0,16},{2,18},{4,20},{6,22},{8,0},{10,2},{12,4},{14,6},{16,24},{18... | collective-permute-start | bytes 786440 | tf_op jit(solution)/shard_map/ppermute | solution.py:251
  81.7 4.3 %first_stress.1 = (f32[2,512,1024]{2,1,0:T(8,128)S(1)}, f32[512,512]{1,0:T(8,128)S(1)}) custom-call(bf16[2,256,256]{2,1,0:T(8,128)(2,1)S(1)} %collective-permute-done.19.near, bf16[2,256,256]{2,1,0:T(8,128)(2,1)S(1)} %collective-permute-done.20.far, bf16[2,2,512,256]{3,2,1,0:T(8,128)(2,1)S(1)} %get-tuple-element.87.columns, ...), custom_call_target="tpu_custom_call", output_to_operand_aliasing={{0}: (3, {})} | custom-call | flops 5000000000 | bytes 1000 | tf_op jit(solution)/shard_map/first_stress/pallas_call | solution.py:50
  86.0 2.0 %last_stress.1 = (f32[256,512]{1,0:T(8,128)S(1)}, f32[256,512]{1,0:T(8,128)S(1)}) custom-call(bf16[2,256,256]{2,1,0:T(8,128)(2,1)S(1)} %collective-permute-done.17.near, bf16[2,256,256]{2,1,0:T(8,128)(2,1)S(1)} %collective-permute-done.18.far, bf16[1024,256]{1,0:T(8,128)(2,1)S(1)} %get-tuple-element.95.v, bf16[1024,1024]{1,0:T(8,128)(2,1)S(1)} %get-tuple-element.90.table, ...), custom_call_target="tpu_custom_call" | custom-call | flops 1000 | bytes 1000 | tf_op jit(solution)/shard_map/last_stress/pallas_call | solution.py:50
  88.1 1.5 %moments.1 = (f32[8,512]{1,0:T(8,128)S(1)}, f32[8,512]{1,0:T(8,128)S(1)}) custom-call(bf16[2,256,256]{2,1,0:T(8,128)(2,1)S(1)} %collective-permute-done.17.near, bf16[2,256,256]{2,1,0:T(8,128)(2,1)S(1)} %collective-permute-done.18.far, bf16[2,2,512,256]{3,2,1,0:T(8,128)(2,1)S(1)} %get-tuple-element.87.columns, ...), custom_call_target="tpu_custom_call" | custom-call | flops 1000 | bytes 1000 | tf_op jit(solution)/shard_map/moments/pallas_call | solution.py:50
  90.0 1.6 %collective-permute-start.22 = (bf16[128,512]{1,0:T(8,128)(2,1)S(1)}, bf16[128,512]{1,0:T(8,128)(2,1)S(1)}, u32[]{:S(2)}, u32[]{:S(2)}) collective-permute-start(bf16[128,512]{1,0:T(8,128)(2,1)S(1)} %add_convert_fusion), channel_id=1, source_target_pairs={{0,1},{1,0},{2,3},{3,2},{4,5},{5,4},{6,7},{7,6},{8,9},{9,8},{10,11... | collective-permute-start | bytes 393224 | tf_op jit(solution)/shard_map/ppermute | solution.py:254
  93.3 2.4 %collective-permute-done.22 = bf16[128,512]{1,0:T(8,128)(2,1)S(1)} collective-permute-done((bf16[128,512]{1,0:T(8,128)(2,1)S(1)}, bf16[128,512]{1,0:T(8,128)(2,1)S(1)}, u32[]{:S(2)}, u32[]{:S(2)}) %collective-permute-start.22) | collective-permute-done | bytes 131104 | tf_op jit(solution)/shard_map/ppermute | solution.py:254
  (50 shorter events, 17.1 us)
Async XLA Ops:
  1.9 15.8 %collective-permute-start.5 = (bf16[2,512,256]{2,1,0:T(8,128)(2,1)S(1)}, bf16[2,512,256]{2,1,0:T(8,128)(2,1)S(1)}, u32[]{:S(2)}, u32[]{:S(2)}) collective-permute-start(bf16[2,512,256]{2,1,0:T(8,128)(2,1)S(1)} %get-tuple-element.110.refs_0_), channel_id=1, source_target_pairs={{0,4},{2,6},{4,0},{6,2},{8,12},{10,14},{12,8},{14,10},{16,20},{18,... | collective-permute-start | bytes 1572872 | tf_op jit(solution)/shard_map/ppermute | solution.py:252
  4.9 15.0 %collective-permute-start.4 = (bf16[2,512,256]{2,1,0:T(8,128)(2,1)S(1)}, bf16[2,512,256]{2,1,0:T(8,128)(2,1)S(1)}, u32[]{:S(2)}, u32[]{:S(2)}) collective-permute-start(bf16[2,512,256]{2,1,0:T(8,128)(2,1)S(1)} %get-tuple-element.110.refs_0_), channel_id=1, source_target_pairs={{0,16},{2,18},{4,20},{6,22},{8,0},{10,2},{12,4},{14,6},{16,24},{18... | collective-permute-start | bytes 1572872 | tf_op jit(solution)/shard_map/ppermute | solution.py:251
  7.5 3.2 %collective-permute-start = (bf16[2,512,256]{2,1,0:T(8,128)(2,1)S(1)}, bf16[2,512,256]{2,1,0:T(8,128)(2,1)S(1)}, u32[]{:S(2)}, u32[]{:S(2)}) collective-permute-start(bf16[2,512,256]{2,1,0:T(8,128)(2,1)S(1)} %get-tuple-element.111), channel_id=1, source_target_pairs={{0,2},{2,0},{4,6},{6,4},{8,10},{10,8},{12,14},{14,12},{16,18},{18,... | collective-permute-start | bytes 1572872 | tf_op jit(solution)/shard_map/ppermute | solution.py:253
  7.5 16.3 %collective-permute-start.3 = (bf16[512,4096]{1,0:T(8,128)(2,1)}, bf16[512,4096]{1,0:T(8,128)(2,1)S(1)}, u32[]{:S(2)}, u32[]{:S(2)}) collective-permute-start(bf16[512,4096]{1,0:T(8,128)(2,1)} %own.17), channel_id=1, source_target_pairs={{0,2},{2,0},{4,6},{6,4},{8,10},{10,8},{12,14},{14,12},{16,18},{18,... | collective-permute-start | bytes 12582920 | tf_op jit(solution)/shard_map/ppermute | solution.py:253
  8.0 0.7 copy-start.1
  8.7 15.1 %copy-start = (bf16[512,4096]{1,0:T(8,128)(2,1)S(1)}, bf16[512,4096]{1,0:T(8,128)(2,1)}, u32[]{:S(2)}) copy-start(bf16[512,4096]{1,0:T(8,128)(2,1)} %own.17) | copy-start | bytes 12582916
  10.8 18.2 %collective-permute-start.2 = (bf16[2,512,256]{2,1,0:T(8,128)(2,1)S(1)}, bf16[2,512,256]{2,1,0:T(8,128)(2,1)S(1)}, u32[]{:S(2)}, u32[]{:S(2)}) collective-permute-start(bf16[2,512,256]{2,1,0:T(8,128)(2,1)S(1)} %collective-permute-done.refs_1_), channel_id=1, source_target_pairs={{0,4},{2,6},{4,0},{6,2},{8,12},{10,14},{12,8},{14,10},{16,20},{18,... | collective-permute-start | bytes 1572872 | tf_op jit(solution)/shard_map/ppermute | solution.py:252
  11.4 19.8 %collective-permute-start.1 = (bf16[2,512,256]{2,1,0:T(8,128)(2,1)S(1)}, bf16[2,512,256]{2,1,0:T(8,128)(2,1)S(1)}, u32[]{:S(2)}, u32[]{:S(2)}) collective-permute-start(bf16[2,512,256]{2,1,0:T(8,128)(2,1)S(1)} %collective-permute-done.refs_1_), channel_id=1, source_target_pairs={{0,16},{2,18},{4,20},{6,22},{8,0},{10,2},{12,4},{14,6},{16,24},{18... | collective-permute-start | bytes 1572872 | tf_op jit(solution)/shard_map/ppermute | solution.py:251
  19.9 20.3 %collective-permute-start.9 = (bf16[2,512,256]{2,1,0:T(8,128)(2,1)S(1)}, bf16[2,512,256]{2,1,0:T(8,128)(2,1)S(1)}, u32[]{:S(2)}, u32[]{:S(2)}) collective-permute-start(bf16[2,512,256]{2,1,0:T(8,128)(2,1)S(1)} %collective-permute-done.4.refs_1_), channel_id=1, source_target_pairs={{0,4},{2,6},{4,0},{6,2},{8,12},{10,14},{12,8},{14,10},{16,20},{18,... | collective-permute-start | bytes 1572872 | tf_op jit(solution)/shard_map/ppermute | solution.py:252
  20.4 21.9 %collective-permute-start.8 = (bf16[2,512,256]{2,1,0:T(8,128)(2,1)S(1)}, bf16[2,512,256]{2,1,0:T(8,128)(2,1)S(1)}, u32[]{:S(2)}, u32[]{:S(2)}) collective-permute-start(bf16[2,512,256]{2,1,0:T(8,128)(2,1)S(1)} %collective-permute-done.4.refs_1_), channel_id=1, source_target_pairs={{0,16},{2,18},{4,20},{6,22},{8,0},{10,2},{12,4},{14,6},{16,24},{18... | collective-permute-start | bytes 1572872 | tf_op jit(solution)/shard_map/ppermute | solution.py:251
  27.2 19.1 %copy-start.2 = (s32[128,8]{0,1:T(8,128)S(1)}, s32[128,8]{0,1:T(8,128)}, u32[]{:S(2)}) copy-start(s32[128,8]{0,1:T(8,128)} %param.8) | copy-start | bytes 12292
  27.2 19.1 %copy-start.3 = (f32[128,8]{0,1:T(8,128)S(1)}, f32[128,8]{0,1:T(8,128)}, u32[]{:S(2)}) copy-start(f32[128,8]{0,1:T(8,128)} %param.9) | copy-start | bytes 12292
  31.1 21.8 %collective-permute-start.7 = (bf16[2,512,256]{2,1,0:T(8,128)(2,1)S(1)}, bf16[2,512,256]{2,1,0:T(8,128)(2,1)S(1)}, u32[]{:S(2)}, u32[]{:S(2)}) collective-permute-start(bf16[2,512,256]{2,1,0:T(8,128)(2,1)S(1)} %collective-permute-done.1.refs_1_), channel_id=1, source_target_pairs={{0,4},{2,6},{4,0},{6,2},{8,12},{10,14},{12,8},{14,10},{16,20},{18,... | collective-permute-start | bytes 1572872 | tf_op jit(solution)/shard_map/ppermute | solution.py:252
  31.7 21.9 %collective-permute-start.6 = (bf16[2,512,256]{2,1,0:T(8,128)(2,1)S(1)}, bf16[2,512,256]{2,1,0:T(8,128)(2,1)S(1)}, u32[]{:S(2)}, u32[]{:S(2)}) collective-permute-start(bf16[2,512,256]{2,1,0:T(8,128)(2,1)S(1)} %collective-permute-done.1.refs_1_), channel_id=1, source_target_pairs={{0,16},{2,18},{4,20},{6,22},{8,0},{10,2},{12,4},{14,6},{16,24},{18... | collective-permute-start | bytes 1572872 | tf_op jit(solution)/shard_map/ppermute | solution.py:251
  42.4 20.3 %collective-permute-start.16 = (bf16[2,512,256]{2,1,0:T(8,128)(2,1)S(1)}, bf16[2,512,256]{2,1,0:T(8,128)(2,1)S(1)}, u32[]{:S(2)}, u32[]{:S(2)}) collective-permute-start(bf16[2,512,256]{2,1,0:T(8,128)(2,1)S(1)} %collective-permute-done.8.refs_1_), channel_id=1, source_target_pairs={{0,4},{2,6},{4,0},{6,2},{8,12},{10,14},{12,8},{14,10},{16,20},{18,... | collective-permute-start | bytes 1572872 | tf_op jit(solution)/shard_map/ppermute | solution.py:252
  42.9 21.9 %collective-permute-start.15 = (bf16[2,512,256]{2,1,0:T(8,128)(2,1)S(1)}, bf16[2,512,256]{2,1,0:T(8,128)(2,1)S(1)}, u32[]{:S(2)}, u32[]{:S(2)}) collective-permute-start(bf16[2,512,256]{2,1,0:T(8,128)(2,1)S(1)} %collective-permute-done.8.refs_1_), channel_id=1, source_target_pairs={{0,16},{2,18},{4,20},{6,22},{8,0},{10,2},{12,4},{14,6},{16,24},{18... | collective-permute-start | bytes 1572872 | tf_op jit(solution)/shard_map/ppermute | solution.py:251
  46.3 1.2 %collective-permute-start.11 = (f32[2,8,128]{2,1,0:T(8,128)S(1)}, f32[2,8,128]{2,1,0:T(8,128)S(1)}, u32[]{:S(2)}, u32[]{:S(2)}) collective-permute-start(f32[2,8,128]{2,1,0:T(8,128)S(1)} %pad_maximum_fusion.refs_0_), channel_id=1, source_target_pairs={{0,2},{2,0},{4,6},{6,4},{8,10},{10,8},{12,14},{14,12},{16,18},{18,... | collective-permute-start | bytes 24584 | tf_op jit(solution)/shard_map/ppermute | solution.py:253
  47.5 3.7 %collective-permute-start.10 = (f32[2,8,128]{2,1,0:T(8,128)S(1)}, f32[2,8,128]{2,1,0:T(8,128)S(1)}, u32[]{:S(2)}, u32[]{:S(2)}) collective-permute-start(f32[2,8,128]{2,1,0:T(8,128)S(1)} %pad_maximum_fusion.refs_0_), channel_id=1, source_target_pairs={{0,1},{1,0},{2,3},{3,2},{4,5},{5,4},{6,7},{7,6},{8,9},{9,8},{10,11... | collective-permute-start | bytes 24584 | tf_op jit(solution)/shard_map/ppermute | solution.py:254
  51.2 1.7 %collective-permute-start.12 = (f32[2,8,128]{2,1,0:T(8,128)S(1)}, f32[2,8,128]{2,1,0:T(8,128)S(1)}, u32[]{:S(2)}, u32[]{:S(2)}) collective-permute-start(f32[2,8,128]{2,1,0:T(8,128)S(1)} %collective-permute-done.10.refs_1_), channel_id=1, source_target_pairs={{0,2},{2,0},{4,6},{6,4},{8,10},{10,8},{12,14},{14,12},{16,18},{18,... | collective-permute-start | bytes 24584 | tf_op jit(solution)/shard_map/ppermute | solution.py:253
  53.6 20.3 %collective-permute-start.14 = (bf16[2,512,256]{2,1,0:T(8,128)(2,1)S(1)}, bf16[2,512,256]{2,1,0:T(8,128)(2,1)S(1)}, u32[]{:S(2)}, u32[]{:S(2)}) collective-permute-start(bf16[2,512,256]{2,1,0:T(8,128)(2,1)S(1)} %collective-permute-done.6.refs_1_), channel_id=1, source_target_pairs={{0,4},{2,6},{4,0},{6,2},{8,12},{10,14},{12,8},{14,10},{16,20},{18,... | collective-permute-start | bytes 1572872 | tf_op jit(solution)/shard_map/ppermute | solution.py:252
  54.5 21.6 %collective-permute-start.13 = (bf16[2,512,256]{2,1,0:T(8,128)(2,1)S(1)}, bf16[2,512,256]{2,1,0:T(8,128)(2,1)S(1)}, u32[]{:S(2)}, u32[]{:S(2)}) collective-permute-start(bf16[2,512,256]{2,1,0:T(8,128)(2,1)S(1)} %collective-permute-done.6.refs_1_), channel_id=1, source_target_pairs={{0,16},{2,18},{4,20},{6,22},{8,0},{10,2},{12,4},{14,6},{16,24},{18... | collective-permute-start | bytes 1572872 | tf_op jit(solution)/shard_map/ppermute | solution.py:251
  64.9 16.8 %collective-permute-start.20 = (bf16[2,256,256]{2,1,0:T(8,128)(2,1)S(1)}, bf16[2,256,256]{2,1,0:T(8,128)(2,1)S(1)}, u32[]{:S(2)}, u32[]{:S(2)}) collective-permute-start(bf16[2,256,256]{2,1,0:T(8,128)(2,1)S(1)} %slice.27), channel_id=1, source_target_pairs={{0,16},{2,18},{4,20},{6,22},{8,0},{10,2},{12,4},{14,6},{16,24},{18... | collective-permute-start | bytes 786440 | tf_op jit(solution)/shard_map/ppermute | solution.py:251
  68.5 13.2 %collective-permute-start.19 = (bf16[2,256,256]{2,1,0:T(8,128)(2,1)S(1)}, bf16[2,256,256]{2,1,0:T(8,128)(2,1)S(1)}, u32[]{:S(2)}, u32[]{:S(2)}) collective-permute-start(bf16[2,256,256]{2,1,0:T(8,128)(2,1)S(1)} %slice.26), channel_id=1, source_target_pairs={{0,4},{2,6},{4,0},{6,2},{8,12},{10,14},{12,8},{14,10},{16,20},{18,... | collective-permute-start | bytes 786440 | tf_op jit(solution)/shard_map/ppermute | solution.py:252
  76.1 9.9 %collective-permute-start.17 = (bf16[2,256,256]{2,1,0:T(8,128)(2,1)S(1)}, bf16[2,256,256]{2,1,0:T(8,128)(2,1)S(1)}, u32[]{:S(2)}, u32[]{:S(2)}) collective-permute-start(bf16[2,256,256]{2,1,0:T(8,128)(2,1)S(1)} %slice.24), channel_id=1, source_target_pairs={{0,4},{2,6},{4,0},{6,2},{8,12},{10,14},{12,8},{14,10},{16,20},{18,... | collective-permute-start | bytes 786440 | tf_op jit(solution)/shard_map/ppermute | solution.py:252
  77.1 8.9 %collective-permute-start.18 = (bf16[2,256,256]{2,1,0:T(8,128)(2,1)S(1)}, bf16[2,256,256]{2,1,0:T(8,128)(2,1)S(1)}, u32[]{:S(2)}, u32[]{:S(2)}) collective-permute-start(bf16[2,256,256]{2,1,0:T(8,128)(2,1)S(1)} %slice.25), channel_id=1, source_target_pairs={{0,16},{2,18},{4,20},{6,22},{8,0},{10,2},{12,4},{14,6},{16,24},{18... | collective-permute-start | bytes 786440 | tf_op jit(solution)/shard_map/ppermute | solution.py:251
  88.0 2.0 %collective-permute-start.21 = (f32[256,512]{1,0:T(8,128)S(1)}, f32[256,512]{1,0:T(8,128)S(1)}, u32[]{:S(2)}, u32[]{:S(2)}) collective-permute-start(f32[256,512]{1,0:T(8,128)S(1)} %get-tuple-element.100), channel_id=1, source_target_pairs={{0,2},{2,0},{4,6},{6,4},{8,10},{10,8},{12,14},{14,12},{16,18},{18,... | collective-permute-start | bytes 1572872 | tf_op jit(solution)/shard_map/ppermute | solution.py:253
  90.0 5.7 %collective-permute-start.22 = (bf16[128,512]{1,0:T(8,128)(2,1)S(1)}, bf16[128,512]{1,0:T(8,128)(2,1)S(1)}, u32[]{:S(2)}, u32[]{:S(2)}) collective-permute-start(bf16[128,512]{1,0:T(8,128)(2,1)S(1)} %add_convert_fusion), channel_id=1, source_target_pairs={{0,1},{1,0},{2,3},{3,2},{4,5},{5,4},{6,7},{7,6},{8,9},{9,8},{10,11... | collective-permute-start | bytes 393224 | tf_op jit(solution)/shard_map/ppermute | solution.py:254
  91.6 1.2 %collective-permute-start.23 = (f32[8,512]{1,0:T(8,128)S(1)}, f32[8,512]{1,0:T(8,128)S(1)}, u32[]{:S(2)}, u32[]{:S(2)}) collective-permute-start(f32[8,512]{1,0:T(8,128)S(1)} %get-tuple-element.107), channel_id=1, source_target_pairs={{0,2},{2,0},{4,6},{6,4},{8,10},{10,8},{12,14},{14,12},{16,18},{18,... | collective-permute-start | bytes 49160 | tf_op jit(solution)/shard_map/ppermute | solution.py:253
  92.8 3.7 %collective-permute-start.24 = (f32[8,512]{1,0:T(8,128)S(1)}, f32[8,512]{1,0:T(8,128)S(1)}, u32[]{:S(2)}, u32[]{:S(2)}) collective-permute-start(f32[8,512]{1,0:T(8,128)S(1)} %add.34), channel_id=1, source_target_pairs={{0,1},{1,0},{2,3},{3,2},{4,5},{5,4},{6,7},{7,6},{8,9},{9,8},{10,11... | collective-permute-start | bytes 49160 | tf_op jit(solution)/shard_map/ppermute | solution.py:254
